TPU v7x, 32 devices: a whole 2x2x4 slice. The times are simulated.
32 devices in a mesh: gx: 4 (over z), gy: 8 (over y, x, core).
Axes of the slice: x: 2, y: 2, z: 4, core: 2. Of those that a mesh axis runs over, the one named last changes fastest.
Arguments:
- bin_population: int32 [64, 512], P('gy', 'gx'), may hold values from 1 to 16
- local_coordinates: float32 [3, 16, 64, 512], P(None, None, 'gy', 'gx'), may hold values from 0 to 1
- field_tilt: float32 [2, 16, 64, 512], P(None, None, 'gy', 'gx'), may hold values from -3.140625 to 3.140625
- body_weights: float32 [16, 64, 512], P(None, 'gy', 'gx'), may hold values from 0.5 to 2
- thermal_conductance: float32 [16, 64, 512], P(None, 'gy', 'gx'), may hold values from 1 to 6
- heat_storage: float32 [16, 64, 512], P(None, 'gy', 'gx'), may hold values from 0.6 to 1.2
- thermal_level: float32 [16, 64, 512], P(None, 'gy', 'gx'), may hold values from 0.5 to 4
- motion_vectors: float32 [3, 16, 64, 512], P(None, None, 'gy', 'gx'), may hold values from -0.2 to 0.2
Outputs:
- heated: float32 [16, 64, 512], P(None, 'gy', 'gx')
- moved: float32 [3, 16, 64, 512], P(None, None, 'gy', 'gx')
Inputs may be any that keep to these rules, and one draw needn't show every extreme that they name: Slots 0 to bin_population - 1 of a cell hold particles, the others are empty.
All inputs are finite; a program needn't handle non-finite values.
Results may differ from a plain program's by a relative error of at most 0.0001.
Values sent between devices are 32-bit elements; how exact they have to be, the bound alone decides.
No kernel may reach another device: no remote copies, remote signals or barrier semaphores. Data moves between devices by JAX's collectives and lax.ppermute only.
A program may use at most 64 MiB of HBM per device.

v0:
```python
import functools
import math

import jax
import jax.numpy as jnp
from jax import lax
from jax.experimental import pallas as pl
from jax.experimental.pallas import tpu as pltpu
from jax.sharding import PartitionSpec as P

SECTIONS = 4
ISO_PART = 0.1
HEAT_RATIO = 5.0 / 3.0
COURANT = 0.3
VISCOSITY = 0.5

F32 = jnp.float32
FAR = 1.0e4
SUB = 8
HALO = 2
STRIDE = 8
NGEO = 7

ROW_SAME = ((0, 0, 0, False), (1, 1, 0, True))
ROW_NEXT = ((-1, -1, 1, True), (0, 0, 1, True), (1, 1, 1, True))
STRIP_SAME = ((0, 0, 0, False), (1, 1, 0, True))
STRIP_NEXT = ((STRIDE - 1, -1, 1, True), (STRIDE, 0, 1, True), (STRIDE + 1, 1, 1, True))


def conduction_polynomial(total):
    weight = 4.0 / (total * total + total - 2)
    c = [1.0 / 3.0] * 3 + [(j * j + j - 2) / (2.0 * j * (j + 1)) for j in range(3, total + 1)]
    older = [1.0] + [0.0] * total
    newer = [1.0, c[1] * weight] + [0.0] * (total - 1)
    for j in range(2, total + 1):
        m = (2 * j - 1) / j * c[j] / c[j - 1]
        n = -(j - 1) / j * c[j] / c[j - 2]
        fresh = [m * a + n * b for a, b in zip(newer, older)]
        fresh[0] += 1.0 - m - n
        for k in range(total):
            fresh[k + 1] += m * weight * newer[k]
        fresh[1] -= (1.0 - c[j - 1]) * m * weight
        older, newer = newer, fresh
    return newer


def roll(x, shift):
    lanes = x.shape[-1]
    return x if shift % lanes == 0 else pltpu.roll(x, shift % lanes, x.ndim - 1)


def lane_iota(shape):
    return lax.broadcasted_iota(jnp.int32, shape, len(shape) - 1)


def spread(ref, p, lanes):
    return jnp.broadcast_to(ref[p : p + 1, :], (SUB, lanes))


def sincos(x):
    k = jnp.floor(x * (2.0 / math.pi) + 0.5)
    r = ((x - k * 1.5703125) - k * 4.837512969970703125e-4) - k * 7.54978995489188216e-8
    z = r * r
    s = r + r * z * (-1.6666654611e-1 + z * (8.3321608736e-3 + z * -1.9515295891e-4))
    c = (
        1.0
        - 0.5 * z
        + z * z * (4.166664568298827e-2 + z * (-1.388731625493765e-3 + z * 2.443315711809948e-5))
    )
    kk = k * k
    odd = kk == 1.0
    turned = kk == 4.0
    s_neg = jnp.logical_or(turned, k == -1.0)
    c_neg = jnp.logical_or(turned, k == 1.0)
    sv = jnp.where(odd, c, s)
    cv = jnp.where(odd, s, c)
    return jnp.where(s_neg, -sv, sv), jnp.where(c_neg, -cv, cv)


def prep_kernel(pop, coord, tilt, mass, kappa, cap, temp, vel, geo, aux, su, sd, mx):
    rows, slots, lanes = geo.shape[1:]
    slot = lax.broadcasted_iota(jnp.int32, (slots, lanes), 0)
    best = None
    for r in range(rows):
        pick = (pl.ds(r, slots, stride=rows), slice(None))
        live = slot < pop[r : r + 1, :]
        st, ct = sincos(tilt[(0,) + pick])
        sp, cp = sincos(tilt[(1,) + pick])
        half = math.sqrt(0.5)
        st = st * half
        t = temp[pick]
        v = [vel[(k,) + pick] for k in range(3)]
        tiles = [
            jnp.where(live, coord[(0,) + pick], FAR),
            coord[(1,) + pick],
            coord[(2,) + pick],
            0.5 * kappa[pick],
            st * cp,
            st * sp,
            ct * half,
        ]
        for k, tile in enumerate(tiles):
            geo[k, r] = tile
        inv_cap = jnp.where(live, 1.0 / cap[pick], 0.0)
        m = mass[pick]
        side = [t, inv_cap, m] + v
        for k, tile in enumerate(side):
            aux[k, r] = tile
        for ref, first, edge in ((su, 0, 0), (sd, rows - HALO, rows - 1)):
            if first <= r < first + HALO:
                for k, tile in enumerate(tiles + [t]):
                    ref[k * HALO + r - first] = tile
            if r == edge:
                for k, tile in enumerate(side[1:]):
                    ref[(NGEO + 1) * HALO + k] = tile
        bound = jnp.sqrt(HEAT_RATIO * (HEAT_RATIO - 1.0) * t) + jnp.sqrt(
            v[0] * v[0] + v[1] * v[1] + v[2] * v[2]
        )
        bound = jnp.where(live, bound, 0.0)
        best = bound if best is None else jnp.maximum(best, bound)
    mx[...] = best
    su[(NGEO + 1) * HALO + 5] = best
    sd[(NGEO + 1) * HALO + 5] = best


def weights(entries, own, far, kills, w_ref, s_ref, idx, first):
    slots, lanes = own(0).shape
    groups = slots // SUB
    for e, (shift, dx, dy, _) in enumerate(entries):
        for g in range(groups):
            j = [roll(far(k)[g * SUB : (g + 1) * SUB, :], -shift) for k in range(NGEO)]
            if dx:
                j[0] = j[0] + float(dx)
            if dy:
                j[1] = j[1] + float(dy)
            if kills[e] is not None:
                j[0] = jnp.where(kills[e], -FAR, j[0])
            for p in range(slots):
                i = [spread(own(k), p, lanes) for k in range(NGEO)]
                dxx, dyy, dzz = (i[k] - j[k] for k in range(3))
                s = jnp.maximum(1.0 - (dxx * dxx + dyy * dyy + dzz * dzz), 0.0)
                a = i[4] * dxx + i[5] * dyy + i[6] * dzz
                b = j[4] * dxx + j[5] * dyy + j[6] * dzz
                w = (s * s * s) * (ISO_PART + (a * a + b * b)) * (i[3] + j[3])
                slot = (first + e) * groups + g
                w_ref[idx, p, slot] = w
                s_ref[idx, p, slot] = s


def row_kills(entries, lanes):
    lane = lane_iota((SUB, lanes))
    return [
        None if e[0] == 0 else lane == (lanes - 1 if e[0] > 0 else 0) for e in entries
    ]


def near_kernel(geo, wh, wx, sh, sx):
    rows, lanes = geo.shape[1], geo.shape[3]
    same, nxt = row_kills(ROW_SAME, lanes), row_kills(ROW_NEXT, lanes)

    @pl.loop(0, rows)
    def _(r):
        weights(ROW_SAME, lambda k: geo.at[k, r], lambda k: geo.at[k, r], same, wh, sh, r, 0)

    @pl.loop(0, rows - 1)
    def _(r):
        weights(ROW_NEXT, lambda k: geo.at[k, r], lambda k: geo.at[k, r + 1], nxt, wx, sx, r, 0)


def rim_kernel(hi, hj, wh, wx, sh, sx):
    lanes = hi.shape[3]
    same, nxt = row_kills(ROW_SAME, lanes), row_kills(ROW_NEXT, lanes)

    @pl.loop(0, 4)
    def _(r):
        weights(ROW_NEXT, lambda k: hi.at[k, r], lambda k: hj.at[k, r], nxt, wx, sx, r, 0)

    @pl.loop(0, 2)
    def _(r):
        weights(
            ROW_SAME, lambda k: hi.at[k, 1 + 2 * r], lambda k: hi.at[k, 1 + 2 * r], same, wh, sh, r, 0
        )


def pack_kernel(geo, aux, ru, rd, mx, *rest):
    spare, (hi, hj, th, ich, mvh, cl, cr, ma) = rest[:-8], rest[-8:]
    rows, slots, lanes = geo.shape[1:]
    full = rows + 2 * HALO
    at_top = lax.axis_index("gy") == 0
    at_end = lax.axis_index("gy") == lax.axis_size("gy") - 1
    base = (NGEO + 1) * HALO

    def feature(k, row):
        if row < HALO:
            tile = ru[k * HALO + row]
            return jnp.where(at_top, FAR, tile) if k == 0 else tile
        if row >= rows + HALO:
            tile = rd[k * HALO + row - rows - HALO]
            return jnp.where(at_end, FAR, tile) if k == 0 else tile
        return geo[k, row - HALO] if k < NGEO else aux[0, row - HALO]

    def side(k, row):
        if row == HALO - 1:
            tile = ru[base + k]
            return jnp.where(at_top, 0.0, tile) if k == 0 else tile
        if row == rows + HALO:
            tile = rd[base + k]
            return jnp.where(at_end, 0.0, tile) if k == 0 else tile
        if HALO <= row < rows + HALO:
            return aux[1 + k, row - HALO]
        return None

    for k in range(NGEO):
        for n, row in enumerate((0, 1, rows + 1, rows + 2)):
            hi[k, n] = feature(k, row)
            hj[k, n] = feature(k, row + 1)
    for n, row in enumerate((0, 1, rows + 2, rows + 3)):
        th[n] = feature(NGEO, row)
    for n, row in enumerate((1, rows + 2)):
        ich[n] = side(0, row)
        for k in range(4):
            mvh[k, n] = side(1 + k, row)
    lane = lane_iota((slots, lanes))
    key = lane % STRIDE
    line = lane // STRIDE
    for k in range(NGEO + 2):
        left = jnp.full((slots, lanes), FAR if k == 0 else 0.0, F32)
        right = left
        for row in range(full):
            tile = feature(k, row) if k <= NGEO else side(0, row)
            if tile is None:
                continue
            here = line == row
            left = jnp.where(here, roll(tile, STRIDE * row + 1), left)
            right = jnp.where(here, roll(tile, STRIDE * row + 5 - lanes), right)
        blank = FAR if k == 0 else 0.0
        cl[k] = jnp.where(jnp.logical_and(key >= 1, key <= 5), left, blank)
        cr[k] = jnp.where(key <= 4, right, blank)
    left = jnp.zeros((slots, lanes), F32)
    right = left
    for row in range(HALO - 1, rows + HALO + 1):
        m, vx, vy, vz = (side(1 + k, row) for k in range(4))
        at = STRIDE * row
        here = line == row

        def put(into, tile, shift, where):
            return jnp.where(jnp.logical_and(here, where), roll(tile, shift), into)

        left = put(left, m, at + 1, jnp.logical_or(key == 1, key == 2))
        right = put(right, m, at + 5 - lanes, jnp.logical_or(key == 3, key == 4))
        for k, tile in enumerate((vx, vy, vz)):
            left = put(left, tile, at + 3 + k, key == 3 + k)
            right = put(right, tile, at + 3 - k - lanes, key == 2 - k)
    cl[NGEO + 2] = left
    cr[NGEO + 2] = right
    best = jnp.maximum(jnp.maximum(ru[base + 5], rd[base + 5]), mx[...])
    for ref in spare:
        best = jnp.maximum(best, ref[...])
    ma[...] = best
    cl[NGEO + 3] = best
    cr[NGEO + 3] = best


def gathered(acc):
    slots = acc.shape[0] // SUB
    total = acc[pl.ds(0, slots, stride=SUB), :]
    for k in range(1, SUB):
        total = total + acc[pl.ds(k, slots, stride=SUB), :]
    return total


def apply_block(entries, own, far_tile, w_ref, idx, first, acc, acc_d, cube):
    slots, lanes = own.shape
    groups = slots // SUB
    far = {}
    back = {}
    bare = {}
    for e, entry in enumerate(entries):
        for g in range(groups):
            far[e, g] = roll(far_tile[g * SUB : (g + 1) * SUB, :], -entry[0])
    for p in range(slots):
        mine = spread(own, p, lanes)
        total = None
        total_d = None
        for e, entry in enumerate(entries):
            for g in range(groups):
                w = w_ref[idx, p, (first + e) * groups + g]
                if cube:
                    w = w * w * w
                term = w * far[e, g]
                total = term if total is None else total + term
                if acc_d is not None:
                    total_d = w if total_d is None else total_d + w
                if entry[3]:
                    term = w * mine
                    back[e, g] = back[e, g] + term if p else term
                    if acc_d is not None:
                        bare[e, g] = bare[e, g] + w if p else w
        acc[p * SUB : (p + 1) * SUB, :] = total
        if acc_d is not None:
            acc_d[p * SUB : (p + 1) * SUB, :] = total_d

    def joined(parts):
        return {
            e: roll(jnp.concatenate([parts[e, g] for g in range(groups)], 0), entry[0])
            for e, entry in enumerate(entries)
            if entry[3]
        }

    sums = gathered(acc)
    if acc_d is None:
        return sums, joined(back), None, None
    return sums, joined(back), gathered(acc_d), joined(bare)


def partner_sums(wset, val, val_t, out, out_t, acc, bare=None, cube=False):
    wh, wx, wh2, wx2, wt = wset
    rows = wh.shape[0]
    slots, lanes = val.shape[1:]
    acc_d, out_d, out_dt = bare if bare is not None else (None, None, None)
    out[...] = jnp.zeros(out.shape, F32)
    if bare is not None:
        out_d[...] = jnp.zeros(out.shape, F32)

    def same(w_ref, idx, row):
        own = val.at[row]
        sums, back, sums_d, bare_d = apply_block(
            ROW_SAME, own, own[...], w_ref, idx, 0, acc, acc_d, cube
        )
        out[row] += sums + back[1]
        if bare is not None:
            out_d[row] += sums_d + bare_d[1]

    def following(w_ref, idx, row):
        sums, back, sums_d, bare_d = apply_block(
            ROW_NEXT, val.at[row], val[row + 1], w_ref, idx, 0, acc, acc_d, cube
        )
        out[row] += sums
        out[row + 1] += back[0] + back[1] + back[2]
        if bare is not None:
            out_d[row] += sums_d
            out_d[row + 1] += bare_d[0] + bare_d[1] + bare_d[2]

    @pl.loop(0, rows)
    def _(r):
        same(wh, r, r + HALO)

    @pl.loop(0, rows - 1)
    def _(r):
        following(wx, r, r + HALO)

    @pl.loop(0, 4)
    def _(r):
        following(wx2, r, jnp.where(r < 2, r, r + rows - 1))

    @pl.loop(0, 2)
    def _(r):
        same(wh2, r, 1 + r * (rows + 1))

    @pl.loop(0, 2)
    def _(side):
        own = val_t.at[side]
        tile = own[...]
        s1, b1, d1, e1 = apply_block(STRIP_SAME, own, tile, wt, side, 0, acc, acc_d, cube)
        s2, b2, d2, e2 = apply_block(
            STRIP_NEXT, own, tile, wt, side, len(STRIP_SAME), acc, acc_d, cube
        )
        out_t[side] = s1 + b1[1] + s2 + b2[0] + b2[1] + b2[2]
        if bare is not None:
            out_dt[side] = d1 + e1[1] + d2 + e2[0] + e2[1] + e2[2]

    def ends(strip, ref):
        lane = lane_iota((slots, lanes))
        low, high = strip[0], strip[1]
        for row in range(ref.shape[0]):
            at = STRIDE * row
            edge = jnp.where(
                lane == 0,
                roll(low, -(at + 5)),
                jnp.where(lane == lanes - 1, roll(high, lanes - 1 - at), 0.0),
            )
            ref[row] += edge

    ends(out_t, out)
    if bare is not None:
        ends(out_dt, out_d)


def fill_strips(val, val_t):
    slots, lanes = val.shape[1:]
    lane = lane_iota((slots, lanes))
    low, high = val_t[0], val_t[1]
    for row in range(val.shape[0]):
        at = STRIDE * row
        low = jnp.where(lane == at + 5, roll(val[row], at + 5), low)
        high = jnp.where(lane == at, roll(val[row], at + 1 - lanes), high)
    val_t[0] = low
    val_t[1] = high


def advance(val, val_t, out, out_t, diag, diag_t, ic, ict):
    for row in range(val.shape[0]):
        val[row] = ic[row] * (out[row] - val[row] * diag[row])
    for side in range(2):
        val_t[side] = ict[side] * (out_t[side] - val_t[side] * diag_t[side])
    fill_strips(val, val_t)


def first_half_kernel(
    aux, th, ich, rl, rr, cl, cr, wh, wx, wh2, wx2, *rest
):
    spare = rest[: -(14 + 6)]
    (st, v1, v1t, val, val_t, diag, diag_t, ic, ict, tside, tt, su, sd, ma2) = rest[-20:-6]
    wt, tgeo, out, out_t, acc, acc_d = rest[-6:]
    rows = wh.shape[0]
    slots, lanes = val.shape[1:]
    full = rows + 2 * HALO
    at_left = lax.axis_index("gx") == 0
    at_right = lax.axis_index("gx") == lax.axis_size("gx") - 1
    lane = lane_iota((slots, lanes))
    key = lane % STRIDE
    from_left = key <= 4
    from_right = jnp.logical_and(key >= 1, key <= 5)
    own_left = key == 5
    own_right = key == 0
    for k in range(NGEO + 1):
        left, right = rl[k], rr[k]
        blank = 0.0
        if k == 0:
            left = jnp.where(at_left, FAR, left)
            right = jnp.where(at_right, FAR, right)
            blank = FAR
        left = jnp.where(from_left, left, jnp.where(own_left, roll(cl[k], 4), blank))
        right = jnp.where(from_right, right, jnp.where(own_right, roll(cr[k], -4), blank))
        if k < NGEO:
            tgeo[k, 0] = left
            tgeo[k, 1] = right
        else:
            tt[0] = left
            tt[1] = right
            val_t[0] = left
            val_t[1] = right
    ict[0] = jnp.where(jnp.logical_and(from_left, jnp.logical_not(at_left)), rl[NGEO + 1], 0.0)
    ict[1] = jnp.where(jnp.logical_and(from_right, jnp.logical_not(at_right)), rr[NGEO + 1], 0.0)
    pl_, pr, ol, orr = rl[NGEO + 2], rr[NGEO + 2], cl[NGEO + 2], cr[NGEO + 2]
    for k in range(3):
        tside[k, 0] = tgeo[k, 0]
        tside[k, 1] = tgeo[k, 1]
    tside[3, 0] = jnp.where(
        jnp.logical_or(key == 3, key == 4), pl_, jnp.where(own_left, roll(ol, 4), 0.0)
    )
    tside[3, 1] = jnp.where(
        jnp.logical_or(key == 1, key == 2), pr, jnp.where(own_right, roll(orr, -4), 0.0)
    )
    for k in range(3):
        tside[4 + k, 0] = jnp.where(
            key == 4, roll(pl_, 2 + k), jnp.where(own_left, roll(ol, 2 - k), 0.0)
        )
        tside[4 + k, 1] = jnp.where(
            key == 1, roll(pr, -2 - k), jnp.where(own_right, roll(orr, k - 2), 0.0)
        )
    small = lane_iota((SUB, lanes)) % STRIDE

    @pl.loop(0, 2)
    def _(side):
        mine = small == 5 - 5 * side
        own = lambda k: tgeo.at[k, side]
        weights(STRIP_SAME, own, own, [mine, None], wt, st, side, 0)
        weights(STRIP_NEXT, own, own, [None, mine, None], wt, st, side, len(STRIP_SAME))

    for row in range(full):
        if row < HALO:
            val[row] = th[row]
        elif row < rows + HALO:
            val[row] = aux[0, row - HALO]
        else:
            val[row] = th[row - rows]
        if row == HALO - 1:
            ic[row] = ich[0]
        elif row == rows + HALO:
            ic[row] = ich[1]
        elif HALO <= row < rows + HALO:
            ic[row] = aux[1, row - HALO]
        else:
            ic[row] = jnp.zeros((slots, lanes), F32)
    wset = (wh, wx, wh2, wx2, wt)
    partner_sums(wset, val, val_t, out, out_t, acc, (acc_d, diag, diag_t))
    advance(val, val_t, out, out_t, diag, diag_t, ic, ict)
    for row in range(rows):
        v1[row] = val[row + HALO]
    v1t[...] = val_t[...]
    partner_sums(wset, val, val_t, out, out_t, acc)
    advance(val, val_t, out, out_t, diag, diag_t, ic, ict)
    best = jnp.maximum(rl[NGEO + 3], rr[NGEO + 3])
    for ref in spare:
        best = jnp.maximum(best, ref[...])
    ma2[...] = best
    for n in range(HALO):
        su[n] = val[HALO + n]
        sd[n] = val[rows + n]
    for side in range(2):
        su[HALO + side] = val_t[side]
        sd[HALO + side] = val_t[side]
    su[HALO + 2] = best
    sd[HALO + 2] = best


def density_kernel(aux, mvh, ict, tside, sh, sx, sh2, sx2, st, mu, mut, inv, invt, val, out, out_t, acc):
    rows = sh.shape[0]
    slots, lanes = val.shape[1:]
    for row in range(rows + 2 * HALO):
        if row == HALO - 1:
            val[row] = mvh[0, 0]
        elif row == rows + HALO:
            val[row] = mvh[0, 1]
        elif HALO <= row < rows + HALO:
            val[row] = aux[2, row - HALO]
        else:
            val[row] = jnp.zeros((slots, lanes), F32)
    mass_t = tside.at[3]
    partner_sums((sh, sx, sh2, sx2, st), val, mass_t, out, out_t, acc, cube=True)
    scale = math.sqrt(VISCOSITY)
    for row in range(rows):
        live = aux[1, row] > 0.0
        density = jnp.where(live, out[row + HALO], 1.0)
        inverse = 1.0 / density
        inv[row] = inverse
        mu[row] = scale * aux[2, row] * inverse
    for side in range(2):
        live = ict[side] > 0.0
        inverse = 1.0 / jnp.where(live, out_t[side], 1.0)
        invt[side] = inverse
        mut[side] = scale * mass_t[side] * inverse
    fill_strips_rows(mu, mut)


def fill_strips_rows(val, val_t):
    slots, lanes = val.shape[1:]
    lane = lane_iota((slots, lanes))
    low, high = val_t[0], val_t[1]
    for row in range(val.shape[0]):
        at = STRIDE * (row + HALO)
        low = jnp.where(lane == at + 5, roll(val[row], at + 5), low)
        high = jnp.where(lane == at, roll(val[row], at + 1 - lanes), high)
    val_t[0] = low
    val_t[1] = high


def second_half_kernel(
    aux, v1, v1t, v2, v2t, tt, ma2, ru, rd, diag, diag_t, ic, ict, wh, wx, wh2, wx2, st_geo,
    mu, mut, inv, invt,
    heated, press, press_t, su, sd, dt,
    val, val_t, wt, out, out_t, acc, heat, heat_t,
):
    rows = wh.shape[0]
    slots, lanes = val.shape[1:]
    full = rows + 2 * HALO
    coef = conduction_polynomial(SECTIONS)
    best = jnp.maximum(jnp.maximum(ru[HALO + 2], rd[HALO + 2]), ma2[...])
    best = jnp.max(jnp.max(best, axis=1, keepdims=True), axis=0, keepdims=True)
    step = COURANT / jnp.broadcast_to(best, (SUB, lanes))
    dt[...] = step
    step = jnp.concatenate([step] * (slots // SUB), 0)
    for row in range(full):
        if row < HALO:
            val[row] = ru[row]
        elif row < rows + HALO:
            val[row] = v2[row]
        else:
            val[row] = rd[row - rows - HALO]
    lane = lane_iota((slots, lanes))
    turn = STRIDE * rows
    for side in range(2):
        val_t[side] = jnp.where(
            lane < STRIDE * HALO,
            roll(ru[HALO + side], -turn),
            jnp.where(lane >= STRIDE * (rows + HALO), roll(rd[HALO + side], turn), v2t[side]),
        )
    step2 = step * step
    for row in range(rows):
        heat[row] = (
            aux[0, row]
            + (coef[1] * step) * v1[row]
            + (coef[2] * step2) * val[row + HALO]
        )
    for side in range(2):
        heat_t[side] = tt[side] + (coef[1] * step) * v1t[side] + (coef[2] * step2) * val_t[side]
    wset = (wh, wx, wh2, wx2, st_geo)
    power = step2
    for section in (3, 4):
        partner_sums(wset, val, val_t, out, out_t, acc)
        advance(val, val_t, out, out_t, diag, diag_t, ic, ict)
        power = power * step
        for row in range(rows):
            heat[row] += (coef[section] * power) * val[row + HALO]
        for side in range(2):
            heat_t[side] += (coef[section] * power) * val_t[side]
    for row in range(rows):
        heated[pl.ds(row, slots, stride=rows), :] = heat[row]
        press[row] = (6.0 * (HEAT_RATIO - 1.0)) * heat[row] * inv[row]
    for side in range(2):
        press_t[side] = (6.0 * (HEAT_RATIO - 1.0)) * heat_t[side] * invt[side]
    fill_strips_rows(press, press_t)
    for ref, row in ((su, 0), (sd, rows - 1)):
        ref[0] = press[row]
        ref[1] = mu[row]
        for side in range(2):
            ref[2 + side] = press_t[side]
            ref[4 + side] = mut[side]


def kick_block(entries, own, far, s_ref, idx, first, acc, fresh, back):
    slots, lanes = own(0).shape
    groups = slots // SUB
    for e, (shift, dx, dy, both) in enumerate(entries):
        j = []
        for g in range(groups):
            t = [roll(far(k)[g * SUB : (g + 1) * SUB, :], -shift) for k in range(9)]
            if dx:
                t[0] = t[0] + float(dx)
            if dy:
                t[1] = t[1] + float(dy)
            j.append(t)
        sums = [[None] * 3 for _ in range(groups)]
        for p in range(slots):
            i = [spread(own(k), p, lanes) for k in range(9)]
            mine = [None] * 3
            for g in range(groups):
                s = s_ref[idx, p, (first + e) * groups + g]
                s2 = s * s
                drag = (s2 * s) * (i[4] * j[g][4])
                push = (i[3] + j[g][3]) * (s2 * (i[5] * j[g][5]))
                for k in range(3):
                    term = push * (i[k] - j[g][k]) + drag * (j[g][6 + k] - i[6 + k])
                    mine[k] = term if mine[k] is None else mine[k] + term
                    if both:
                        sums[g][k] = term if sums[g][k] is None else sums[g][k] + term
            for k in range(3):
                place = (k, slice(p * SUB, (p + 1) * SUB), slice(None))
                acc[place] = mine[k] if fresh and e == 0 else acc[place] + mine[k]
        if both:
            for k in range(3):
                back(e, k, roll(jnp.concatenate([sums[g][k] for g in range(groups)], 0), shift))


def kick_near_kernel(geo, aux, mu, press, sh, sx, out, acc):
    rows = geo.shape[1]
    out[...] = jnp.zeros(out.shape, F32)

    def feature(k, row):
        if k < 3:
            return geo.at[k, row]
        if k == 3:
            return press.at[row]
        if k == 4:
            return mu.at[row]
        return aux.at[k - 3, row]

    def back_to(row):
        def back(e, k, tile):
            out[k, row] -= tile

        return back

    def settle(row):
        for k in range(3):
            out[k, row] += gathered(acc.at[k])

    @pl.loop(0, rows)
    def _(r):
        here = lambda k: feature(k, r)
        kick_block(ROW_SAME, here, here, sh, r, 0, acc, True, back_to(r))
        settle(r)

    @pl.loop(0, rows - 1)
    def _(r):
        kick_block(
            ROW_NEXT, lambda k: feature(k, r), lambda k: feature(k, r + 1), sx, r, 0, acc, True,
            back_to(r + 1),
        )
        settle(r)


def kick_rim_kernel(
    geo, aux, mu, press, hi, hj, mvh, tside, mut, press_t, ru, rd, sx2, st, near, dt,
    moved, rim, strip, out, out_t, acc,
):
    rows, slots, lanes = geo.shape[1:]
    for n in range(4):
        halo = n in (0, 3)
        side = 0 if n == 0 else 1
        row = 0 if n == 1 else rows - 1
        recv = ru if n == 0 else rd
        for k in range(9):
            if k < 3:
                tile = (hi[k, 1], geo[k, 0], geo[k, rows - 1], hj[k, 2])[n]
            elif k < 5:
                tile = recv[k - 3] if halo else (press, mu)[k - 3][row]
            else:
                tile = mvh[k - 5, side] if halo else aux[k - 3, row]
            rim[k, n] = tile
    lane = lane_iota((slots, lanes))
    turn = STRIDE * rows
    for side in range(2):
        for k in range(9):
            if k < 3:
                tile = tside[k, side]
            elif k < 5:
                at = 2 + 2 * (k - 3) + side
                tile = jnp.where(
                    lane < STRIDE * HALO,
                    roll(ru[at], -turn),
                    jnp.where(
                        lane >= STRIDE * (rows + HALO),
                        roll(rd[at], turn),
                        (press_t, mut)[k - 3][side],
                    ),
                )
            else:
                tile = tside[k - 2, side]
            strip[k, side] = tile
    out[...] = jnp.zeros(out.shape, F32)

    @pl.loop(0, 2)
    def _(n):
        def back(e, k, tile):
            out[k, 2 * n + 1] -= tile

        kick_block(
            ROW_NEXT, lambda k: rim.at[k, 2 * n], lambda k: rim.at[k, 2 * n + 1], sx2, 1 + n, 0, acc,
            True, back,
        )
        for k in range(3):
            out[k, 2 * n] += gathered(acc.at[k])

    @pl.loop(0, 2)
    def _(side):
        for k in range(3):
            out_t[k, side] = jnp.zeros((slots, lanes), F32)

        def back(e, k, tile):
            out_t[k, side] -= tile

        here = lambda k: strip.at[k, side]
        kick_block(STRIP_SAME, here, here, st, side, 0, acc, True, back)
        kick_block(STRIP_NEXT, here, here, st, side, len(STRIP_SAME), acc, False, back)
        for k in range(3):
            out_t[k, side] += gathered(acc.at[k])

    step = jnp.concatenate([dt[...]] * (slots // SUB), 0)
    for row in range(rows):
        live = aux[1, row] > 0.0
        factor = step / aux[2, row]
        at = STRIDE * (row + HALO)
        for k in range(3):
            total = near[k, row]
            if row == 0:
                total = total + out[k, 1]
            if row == rows - 1:
                total = total + out[k, 2]
            total = total + jnp.where(
                lane == 0,
                roll(out_t[k, 0], -(at + 5)),
                jnp.where(lane == lanes - 1, roll(out_t[k, 1], lanes - 1 - at), 0.0),
            )
            moved[k, pl.ds(row, slots, stride=rows), :] = aux[3 + k, row] + jnp.where(
                live, factor * total, 0.0
            )


VMEM_SPEC = pl.BlockSpec(memory_space=pltpu.VMEM)


def call(kernel, args, outs, scratch=(), name=None, limit=24):
    shapes = [jax.ShapeDtypeStruct(o, F32) for o in outs]
    return pl.pallas_call(
        kernel,
        in_specs=[VMEM_SPEC] * len(args),
        out_specs=[VMEM_SPEC] * len(outs),
        out_shape=shapes,
        scratch_shapes=[pltpu.VMEM(s, F32) for s in scratch],
        compiler_params=pltpu.CompilerParams(vmem_limit_bytes=limit * 1024 * 1024),
        name=name,
    )(*args)


def ring(axis, shift):
    n = lax.axis_size(axis)
    return [(i, (i + shift) % n) for i in range(n)]


def swap(to_lower, to_upper, axis):
    from_lower = lax.ppermute(to_upper, axis, ring(axis, 1))
    from_upper = lax.ppermute(to_lower, axis, ring(axis, -1))
    return from_lower, from_upper


def body(pop, coord, tilt, mass, kappa, cap, temp, vel):
    slots, rows, lanes = temp.shape
    flat = lambda x: x.reshape(x.shape[:-3] + (slots * rows, lanes))
    tile = (slots, lanes)
    full = rows + 2 * HALO
    groups = slots // SUB
    nsend = (NGEO + 1) * HALO + 6
    geo, aux, su, sd, mx = call(
        prep_kernel,
        (pop, flat(coord), flat(tilt), flat(mass), flat(kappa), flat(cap), flat(temp), flat(vel)),
        [(NGEO, rows) + tile, (6, rows) + tile, (nsend,) + tile, (nsend,) + tile, tile],
        name="prep",
    )
    ru, rd = swap(su, sd, "gy")
    spare = [lax.ppermute(mx, "gy", ring("gy", k)) for k in range(4, lax.axis_size("gy") - 2, 3)]
    same = lambda n: (n, slots, len(ROW_SAME) * groups, SUB, lanes)
    nxt = lambda n: (n, slots, len(ROW_NEXT) * groups, SUB, lanes)
    both = (2, slots, (len(ROW_SAME) + len(ROW_NEXT)) * groups, SUB, lanes)
    wh, wx, sh, sx = call(
        near_kernel, (geo,), [same(rows), nxt(rows - 1)] * 2, name="near"
    )
    hi, hj, th, ich, mvh, cl, cr, ma = call(
        pack_kernel,
        (geo, aux, ru, rd, mx, *spare),
        [(NGEO, 4) + tile] * 2
        + [(4,) + tile, (2,) + tile, (4, 2) + tile]
        + [(NGEO + 4,) + tile] * 2
        + [tile],
        name="pack",
    )
    rl, rr = swap(cl, cr, "gx")
    spare = [lax.ppermute(ma, "gx", ring("gx", k)) for k in range(2, lax.axis_size("gx") - 1)]
    wh2, wx2, sh2, sx2 = call(rim_kernel, (hi, hj), [same(2), nxt(4)] * 2, name="rim")
    ext = (full,) + tile
    two = (2,) + tile
    sumtile = (slots * SUB, lanes)
    st, v1, v1t, v2, v2t, diag, diag_t, ic, ict, tside, tt, su, sd, ma2, wt = call(
        first_half_outer,
        (aux, th, ich, rl, rr, cl, cr, wh, wx, wh2, wx2, ma, *spare),
        [both, (rows,) + tile, two, ext, two, ext, two, ext, two, (7,) + two, two]
        + [(HALO + 3,) + tile] * 2
        + [tile, both],
        [(NGEO,) + two, ext, two, sumtile, sumtile],
        name="first_half",
    )
    ru, rd = swap(su, sd, "gy")
    mu, mut, inv, invt = call(
        density_kernel,
        (aux, mvh, ict, tside, sh, sx, sh2, sx2, st),
        [(rows,) + tile, two] * 2,
        [ext, ext, two, sumtile],
        name="density",
    )
    heated, press, press_t, su, sd, dt = call(
        second_half_kernel,
        (aux, v1, v1t, v2, v2t, tt, ma2, ru, rd, diag, diag_t, ic, ict, wh, wx, wh2, wx2, wt)
        + (mu, mut, inv, invt),
        [(slots * rows, lanes), (rows,) + tile, two, (6,) + tile, (6,) + tile, (SUB, lanes)],
        [ext, two, (SUB, lanes), ext, two, sumtile, (rows,) + tile, two],
        name="second_half",
    )
    ru, rd = swap(su, sd, "gy")
    near = call(
        kick_near_kernel,
        (geo, aux, mu, press, sh, sx),
        [(3, rows) + tile],
        [(3,) + sumtile],
        name="kick_near",
    )[0]
    moved = call(
        kick_rim_kernel,
        (geo, aux, mu, press, hi, hj, mvh, tside, mut, press_t, ru, rd, sx2, st, near, dt),
        [(3, slots * rows, lanes)],
        [(9, 4) + tile, (9, 2) + tile, (3, 4) + tile, (3, 2) + tile, (3,) + sumtile],
        name="kick_rim",
    )[0]
    return heated.reshape(temp.shape), moved.reshape(vel.shape)


def first_half_outer(aux, th, ich, rl, rr, cl, cr, wh, wx, wh2, wx2, *rest):
    spare, outs, scratch = rest[:-20], rest[-20:-5], rest[-5:]
    first_half_kernel(
        aux, th, ich, rl, rr, cl, cr, wh, wx, wh2, wx2, *spare, *outs[:-1], outs[-1], *scratch
    )


def solution(mesh):
    in_specs = (
        P("gy", "gx"),
        P(None, None, "gy", "gx"),
        P(None, None, "gy", "gx"),
        P(None, "gy", "gx"),
        P(None, "gy", "gx"),
        P(None, "gy", "gx"),
        P(None, "gy", "gx"),
        P(None, None, "gy", "gx"),
    )
    out_specs = (P(None, "gy", "gx"), P(None, None, "gy", "gx"))
    return jax.shard_map(body, mesh=mesh, in_specs=in_specs, out_specs=out_specs, check_vma=False)
```

profile of v0, /device:TPU:0, one launch (start us, length us, event | category | flops | bytes accessed | tf_op | source)
XLA Modules:
  0.0 60.3 jit_solution(7943882310314829033)
XLA Ops:
  0.6 0.0 copy-start
  0.6 0.9 %copy-done = f32[3,16,8,128]{3,2,1,0:T(8,128)S(1)} copy-done((f32[3,16,8,128]{3,2,1,0:T(8,128)S(1)}, f32[3,16,8,128]{3,2,1,0:T(8,128)}, u32[]{:S(2)}) %copy-start) | copy-done | bytes 196632
  1.6 0.0 copy-start.1
  1.6 0.9 %copy-done.1 = f32[3,16,8,128]{3,2,1,0:T(8,128)S(1)} copy-done((f32[3,16,8,128]{3,2,1,0:T(8,128)S(1)}, f32[3,16,8,128]{3,2,1,0:T(8,128)}, u32[]{:S(2)}) %copy-start.1) | copy-done | bytes 196632
  2.5 0.0 copy-start.2
  2.5 0.9 %copy-done.2 = f32[2,16,8,128]{3,2,1,0:T(8,128)S(1)} copy-done((f32[2,16,8,128]{3,2,1,0:T(8,128)S(1)}, f32[2,16,8,128]{3,2,1,0:T(8,128)}, u32[]{:S(2)}) %copy-start.2) | copy-done | bytes 131096
  3.4 0.0 copy-start.3
  3.4 0.8 %copy-done.3 = f32[16,8,128]{2,1,0:T(8,128)S(1)} copy-done((f32[16,8,128]{2,1,0:T(8,128)S(1)}, f32[16,8,128]{2,1,0:T(8,128)}, u32[]{:S(2)}) %copy-start.3) | copy-done | bytes 65560
  4.2 0.0 copy-start.4
  4.2 0.8 %copy-done.4 = f32[16,8,128]{2,1,0:T(8,128)S(1)} copy-done((f32[16,8,128]{2,1,0:T(8,128)S(1)}, f32[16,8,128]{2,1,0:T(8,128)}, u32[]{:S(2)}) %copy-start.4) | copy-done | bytes 65560
  5.1 0.0 copy-start.5
  5.1 0.8 %copy-done.5 = f32[16,8,128]{2,1,0:T(8,128)S(1)} copy-done((f32[16,8,128]{2,1,0:T(8,128)S(1)}, f32[16,8,128]{2,1,0:T(8,128)}, u32[]{:S(2)}) %copy-start.5) | copy-done | bytes 65560
  5.9 0.0 copy-start.6
  5.9 0.8 %copy-done.6 = f32[16,8,128]{2,1,0:T(8,128)S(1)} copy-done((f32[16,8,128]{2,1,0:T(8,128)S(1)}, f32[16,8,128]{2,1,0:T(8,128)}, u32[]{:S(2)}) %copy-start.6) | copy-done | bytes 65560
  6.8 0.0 copy-start.7
  6.8 0.7 %copy-done.7 = s32[8,128]{1,0:T(8,128)S(1)} copy-done((s32[8,128]{1,0:T(8,128)S(1)}, s32[8,128]{1,0:T(8,128)}, u32[]{:S(2)}) %copy-start.7) | copy-done | bytes 4120
  7.4 0.3 prep.1
  7.8 0.5 collective-permute-start
  8.3 2.9 %collective-permute-start.1 = (f32[22,16,128]{2,1,0:T(8,128)S(1)}, f32[22,16,128]{2,1,0:T(8,128)S(1)}, u32[]{:S(2)}, u32[]{:S(2)}) collective-permute-start(f32[22,16,128]{2,1,0:T(8,128)S(1)} %get-tuple-element.51), channel_id=1, source_target_pairs={{0,7},{1,0},{2,1},{3,2},{4,3},{5,4},{6,5},{7,6},{8,15},{9,8},{10,9... | collective-permute-start | bytes 540680 | tf_op jit(solution)/shard_map/ppermute | solution.py:794
  11.3 2.2 %collective-permute-start.2 = (f32[16,128]{1,0:T(8,128)S(1)}, f32[16,128]{1,0:T(8,128)S(1)}, u32[]{:S(2)}, u32[]{:S(2)}) collective-permute-start(f32[16,128]{1,0:T(8,128)S(1)} %get-tuple-element.52.mx), channel_id=1, source_target_pairs={{0,4},{1,5},{2,6},{3,7},{4,0},{5,1},{6,2},{7,3},{8,12},{9,13},{10,... | collective-permute-start | bytes 24584 | tf_op jit(solution)/shard_map/ppermute | solution.py:812
  13.5 1.6 %collective-permute-done.2.rest_0_ = f32[16,128]{1,0:T(8,128)S(1)} collective-permute-done((f32[16,128]{1,0:T(8,128)S(1)}, f32[16,128]{1,0:T(8,128)S(1)}, u32[]{:S(2)}, u32[]{:S(2)}) %collective-permute-start.2) | collective-permute-done | bytes 8224 | tf_op jit(solution)/shard_map/ppermute | solution.py:812
  15.1 0.0 collective-permute-done.ru
  15.1 0.1 collective-permute-done.1.rd
  15.2 0.7 %pack.1 = (f32[7,4,16,128]{3,2,1,0:T(8,128)S(1)}, f32[7,4,16,128]{3,2,1,0:T(8,128)S(1)}, f32[4,16,128]{2,1,0:T(8,128)S(1)}, f32[2,16,128]{2,1,0:T(8,128)S(1)}, f...) custom-call(f32[7,8,16,128]{3,2,1,0:T(8,128)S(1)} %get-tuple-element, ...), custom_call_target="tpu_custom_call" | custom-call | tf_op jit(solution)/shard_map/pack/pallas_call | solution.py:776
  15.9 2.1 %collective-permute-start.3 = (f32[11,16,128]{2,1,0:T(8,128)S(1)}, f32[11,16,128]{2,1,0:T(8,128)S(1)}, u32[]{:S(2)}, u32[]{:S(2)}) collective-permute-start(f32[11,16,128]{2,1,0:T(8,128)S(1)} %get-tuple-element.55.cr), channel_id=1, source_target_pairs={{0,8},{8,16},{16,24},{24,0},{1,9},{9,17},{17,25},{25,1},{2,10},{10... | collective-permute-start | bytes 270344 | tf_op jit(solution)/shard_map/ppermute | solution.py:793
  17.9 2.1 %collective-permute-start.4 = (f32[11,16,128]{2,1,0:T(8,128)S(1)}, f32[11,16,128]{2,1,0:T(8,128)S(1)}, u32[]{:S(2)}, u32[]{:S(2)}) collective-permute-start(f32[11,16,128]{2,1,0:T(8,128)S(1)} %get-tuple-element.56.cl), channel_id=1, source_target_pairs={{0,24},{8,0},{16,8},{24,16},{1,25},{9,1},{17,9},{25,17},{2,26},{10... | collective-permute-start | bytes 270344 | tf_op jit(solution)/shard_map/ppermute | solution.py:794
  20.0 0.9 %collective-permute-start.5 = (f32[16,128]{1,0:T(8,128)S(1)}, f32[16,128]{1,0:T(8,128)S(1)}, u32[]{:S(2)}, u32[]{:S(2)}) collective-permute-start(f32[16,128]{1,0:T(8,128)S(1)} %get-tuple-element.63.rest_0_), channel_id=1, source_target_pairs={{0,16},{8,24},{16,0},{24,8},{1,17},{9,25},{17,1},{25,9},{2,18},{10... | collective-permute-start | bytes 24584 | tf_op jit(solution)/shard_map/ppermute | solution.py:829
  21.0 5.2 %near.1 = (f32[8,16,4,8,128]{4,3,2,1,0:T(8,128)S(1)}, f32[7,16,6,8,128]{4,3,2,1,0:T(8,128)S(1)}, f32[8,16,4,8,128]{4,3,2,1,0:T(8,128)S(1)}, f32[7,16,6,8,128]{4,3,2,1,0:T(8,128)S(1)}) custom-call(f32[7,8,16,128]{3,2,1,0:T(8,128)S(1)} %get-tuple-element.49.geo), custom_call_target="tpu_custom_call" | custom-call | tf_op jit(solution)/shard_map/near/pallas_call | solution.py:776
  26.1 2.3 %rim.1 = (f32[2,16,4,8,128]{4,3,2,1,0:T(8,128)S(1)}, f32[4,16,6,8,128]{4,3,2,1,0:T(8,128)S(1)}, f32[2,16,4,8,128]{4,3,2,1,0:T(8,128)S(1)}, f32[4,16,6,8,128]{4,3,2,1,0:T(8,128)S(1)}) custom-call(f32[7,4,16,128]{3,2,1,0:T(8,128)S(1)} %get-tuple-element.59.hi, f32[7,4,16,128]{3,2,1,0:T(8,128)S(1)} %get-tuple-element.60.hj), custom_call_target="tpu_custom_call" | custom-call | tf_op jit(solution)/shard_map/rim/pallas_call | solution.py:776
  28.4 0.0 collective-permute-done.5.rest_1_
  28.4 0.0 collective-permute-done.3.rl
  28.5 0.0 collective-permute-done.4.rr
  28.5 7.2 %first_half.1 = (f32[2,16,10,8,128]{4,3,2,1,0:T(8,128)S(1)}, f32[8,16,128]{2,1,0:T(8,128)S(1)}, f32[2,16,128]{2,1,0:T(8,128)S(1)}, f32[12,16,128]{2,1,0:T(8,128)...) custom-call(f32[6,8,16,128]{3,2,1,0:T(8,128)S(1)} %get-tuple-element, ...), custom_call_target="tpu_custom_call" | custom-call | tf_op jit(solution)/shard_map/first_half/pallas_call | solution.py:776
  35.7 0.5 collective-permute-start.6
  36.2 2.2 %collective-permute-start.7 = (f32[5,16,128]{2,1,0:T(8,128)S(1)}, f32[5,16,128]{2,1,0:T(8,128)S(1)}, u32[]{:S(2)}, u32[]{:S(2)}) collective-permute-start(f32[5,16,128]{2,1,0:T(8,128)S(1)} %get-tuple-element.71), channel_id=1, source_target_pairs={{0,7},{1,0},{2,1},{3,2},{4,3},{5,4},{6,5},{7,6},{8,15},{9,8},{10,9... | collective-permute-start | bytes 122888 | tf_op jit(solution)/shard_map/ppermute | solution.py:794
  38.4 2.8 %density.1 = (f32[8,16,128]{2,1,0:T(8,128)S(1)}, f32[2,16,128]{2,1,0:T(8,128)S(1)}, f32[8,16,128]{2,1,0:T(8,128)S(1)}, f32[2,16,128]{2,1,0:T(8,128)S(1)}) custom-call(f32[6,8,16,128]{3,2,1,0:T(8,128)S(1)} %get-tuple-element.48.aux, f32[4,2,16,128]{3,2,1,0:T(8,128)S(1)} %get-tuple-element.77.mvh, f32[2,16,128]{2,1,0:T(8,128)S(1)} %get-tuple-element.75.ict, ...), custom_call_target="tpu_custom_call" | custom-call | tf_op jit(solution)/shard_map/density/pallas_call | solution.py:776
  41.1 0.0 collective-permute-done.6.ru
  41.2 0.0 collective-permute-done.7.rd
  41.2 6.0 %second_half.1 = (f32[128,128]{1,0:T(8,128)}, f32[8,16,128]{2,1,0:T(8,128)S(1)}, f32[2,16,128]{2,1,0:T(8,128)S(1)}, f32[6,16,128]{2,1,0:T(8,128)S(1)}, f32[6,16,128]{2,1,0:T(8,128)S(1)}, /*index=5*/f32[8,128]{1,0:T(8,128)S(1)}) custom-call(f32[6,8,16,128]{3,2,1,0:T(8,128)S(1)} %get-tuple-element.48.aux, f32[8,16,128]{2,1,0:T(8,128)S(1)} %get-tuple-element.64.v1, ...), custom_call_target="tpu_custom_call" | custom-call | tf_op jit(solution)/shard_map/second_half/pallas_call | solution.py:776
  47.2 0.0 collective-permute-start.8
  47.2 2.6 %collective-permute-start.9 = (f32[6,16,128]{2,1,0:T(8,128)S(1)}, f32[6,16,128]{2,1,0:T(8,128)S(1)}, u32[]{:S(2)}, u32[]{:S(2)}) collective-permute-start(f32[6,16,128]{2,1,0:T(8,128)S(1)} %get-tuple-element.92), channel_id=1, source_target_pairs={{0,7},{1,0},{2,1},{3,2},{4,3},{5,4},{6,5},{7,6},{8,15},{9,8},{10,9... | collective-permute-start | bytes 147464 | tf_op jit(solution)/shard_map/ppermute | solution.py:794
  49.8 6.8 %kick_near.1.near = f32[3,8,16,128]{3,2,1,0:T(8,128)S(1)} custom-call(f32[7,8,16,128]{3,2,1,0:T(8,128)S(1)} %get-tuple-element.49.geo, f32[6,8,16,128]{3,2,1,0:T(8,128)S(1)} %get-tuple-element.48.aux, f32[8,16,128]{2,1,0:T(8,128)S(1)} %get-tuple-element.84.mu, f32[8,16,128]{2,1,0:T(8,128)S(1)} %get-tuple-element.89.press, ...), custom_call_target="tpu_custom_call" | custom-call | tf_op jit(solution)/shard_map/kick_near/pallas_call | solution.py:776
  56.7 0.0 collective-permute-done.8.ru
  56.7 0.0 collective-permute-done.9.rd
  56.7 3.6 %kick_rim.1 = f32[3,128,128]{2,1,0:T(8,128)} custom-call(f32[7,8,16,128]{3,2,1,0:T(8,128)S(1)} %get-tuple-element.49.geo, f32[6,8,16,128]{3,2,1,0:T(8,128)S(1)} %get-tuple-element.48.aux, f32[8,16,128]{2,1,0:T(8,128)S(1)} %get-tuple-element.84.mu, f32[8,16,128]{2,1,0:T(8,128)S(1)} %get-tuple-element.89.press, f32[7,4,16,128]{3,2,1,0:T(8,128)S(1)} %get-tuple-element.59.hi, ...), custom_call_target="tpu_custom_call" | custom-call | tf_op jit(solution)/shard_map/kick_rim/pallas_call | solution.py:776
Async XLA Ops:
  0.6 0.9 %copy-start = (f32[3,16,8,128]{3,2,1,0:T(8,128)S(1)}, f32[3,16,8,128]{3,2,1,0:T(8,128)}, u32[]{:S(2)}) copy-start(f32[3,16,8,128]{3,2,1,0:T(8,128)} %param.9) | copy-start | bytes 589828
  1.6 0.9 %copy-start.1 = (f32[3,16,8,128]{3,2,1,0:T(8,128)S(1)}, f32[3,16,8,128]{3,2,1,0:T(8,128)}, u32[]{:S(2)}) copy-start(f32[3,16,8,128]{3,2,1,0:T(8,128)} %param.15) | copy-start | bytes 589828
  2.5 0.9 %copy-start.2 = (f32[2,16,8,128]{3,2,1,0:T(8,128)S(1)}, f32[2,16,8,128]{3,2,1,0:T(8,128)}, u32[]{:S(2)}) copy-start(f32[2,16,8,128]{3,2,1,0:T(8,128)} %param.10) | copy-start | bytes 393220
  3.4 0.8 %copy-start.3 = (f32[16,8,128]{2,1,0:T(8,128)S(1)}, f32[16,8,128]{2,1,0:T(8,128)}, u32[]{:S(2)}) copy-start(f32[16,8,128]{2,1,0:T(8,128)} %param.11) | copy-start | bytes 196612
  4.2 0.8 %copy-start.4 = (f32[16,8,128]{2,1,0:T(8,128)S(1)}, f32[16,8,128]{2,1,0:T(8,128)}, u32[]{:S(2)}) copy-start(f32[16,8,128]{2,1,0:T(8,128)} %param.12) | copy-start | bytes 196612
  5.1 0.8 %copy-start.5 = (f32[16,8,128]{2,1,0:T(8,128)S(1)}, f32[16,8,128]{2,1,0:T(8,128)}, u32[]{:S(2)}) copy-start(f32[16,8,128]{2,1,0:T(8,128)} %param.13) | copy-start | bytes 196612
  5.9 0.8 %copy-start.6 = (f32[16,8,128]{2,1,0:T(8,128)S(1)}, f32[16,8,128]{2,1,0:T(8,128)}, u32[]{:S(2)}) copy-start(f32[16,8,128]{2,1,0:T(8,128)} %param.14) | copy-start | bytes 196612
  6.8 0.7 %copy-start.7 = (s32[8,128]{1,0:T(8,128)S(1)}, s32[8,128]{1,0:T(8,128)}, u32[]{:S(2)}) copy-start(s32[8,128]{1,0:T(8,128)} %pop.1) | copy-start | bytes 12292
  7.8 7.3 %collective-permute-start = (f32[22,16,128]{2,1,0:T(8,128)S(1)}, f32[22,16,128]{2,1,0:T(8,128)S(1)}, u32[]{:S(2)}, u32[]{:S(2)}) collective-permute-start(f32[22,16,128]{2,1,0:T(8,128)S(1)} %get-tuple-element.50), channel_id=1, source_target_pairs={{0,1},{1,2},{2,3},{3,4},{4,5},{5,6},{6,7},{7,0},{8,9},{9,10},{10,1... | collective-permute-start | bytes 540680 | tf_op jit(solution)/shard_map/ppermute | solution.py:793
  8.3 6.8 %collective-permute-start.1 = (f32[22,16,128]{2,1,0:T(8,128)S(1)}, f32[22,16,128]{2,1,0:T(8,128)S(1)}, u32[]{:S(2)}, u32[]{:S(2)}) collective-permute-start(f32[22,16,128]{2,1,0:T(8,128)S(1)} %get-tuple-element.51), channel_id=1, source_target_pairs={{0,7},{1,0},{2,1},{3,2},{4,3},{5,4},{6,5},{7,6},{8,15},{9,8},{10,9... | collective-permute-start | bytes 540680 | tf_op jit(solution)/shard_map/ppermute | solution.py:794
  11.3 3.8 %collective-permute-start.2 = (f32[16,128]{1,0:T(8,128)S(1)}, f32[16,128]{1,0:T(8,128)S(1)}, u32[]{:S(2)}, u32[]{:S(2)}) collective-permute-start(f32[16,128]{1,0:T(8,128)S(1)} %get-tuple-element.52.mx), channel_id=1, source_target_pairs={{0,4},{1,5},{2,6},{3,7},{4,0},{5,1},{6,2},{7,3},{8,12},{9,13},{10,... | collective-permute-start | bytes 24584 | tf_op jit(solution)/shard_map/ppermute | solution.py:812
  15.9 12.6 %collective-permute-start.3 = (f32[11,16,128]{2,1,0:T(8,128)S(1)}, f32[11,16,128]{2,1,0:T(8,128)S(1)}, u32[]{:S(2)}, u32[]{:S(2)}) collective-permute-start(f32[11,16,128]{2,1,0:T(8,128)S(1)} %get-tuple-element.55.cr), channel_id=1, source_target_pairs={{0,8},{8,16},{16,24},{24,0},{1,9},{9,17},{17,25},{25,1},{2,10},{10... | collective-permute-start | bytes 270344 | tf_op jit(solution)/shard_map/ppermute | solution.py:793
  17.9 10.5 %collective-permute-start.4 = (f32[11,16,128]{2,1,0:T(8,128)S(1)}, f32[11,16,128]{2,1,0:T(8,128)S(1)}, u32[]{:S(2)}, u32[]{:S(2)}) collective-permute-start(f32[11,16,128]{2,1,0:T(8,128)S(1)} %get-tuple-element.56.cl), channel_id=1, source_target_pairs={{0,24},{8,0},{16,8},{24,16},{1,25},{9,1},{17,9},{25,17},{2,26},{10... | collective-permute-start | bytes 270344 | tf_op jit(solution)/shard_map/ppermute | solution.py:794
  20.0 8.4 %collective-permute-start.5 = (f32[16,128]{1,0:T(8,128)S(1)}, f32[16,128]{1,0:T(8,128)S(1)}, u32[]{:S(2)}, u32[]{:S(2)}) collective-permute-start(f32[16,128]{1,0:T(8,128)S(1)} %get-tuple-element.63.rest_0_), channel_id=1, source_target_pairs={{0,16},{8,24},{16,0},{24,8},{1,17},{9,25},{17,1},{25,9},{2,18},{10... | collective-permute-start | bytes 24584 | tf_op jit(solution)/shard_map/ppermute | solution.py:829
  35.7 5.5 %collective-permute-start.6 = (f32[5,16,128]{2,1,0:T(8,128)S(1)}, f32[5,16,128]{2,1,0:T(8,128)S(1)}, u32[]{:S(2)}, u32[]{:S(2)}) collective-permute-start(f32[5,16,128]{2,1,0:T(8,128)S(1)} %get-tuple-element.70), channel_id=1, source_target_pairs={{0,1},{1,2},{2,3},{3,4},{4,5},{5,6},{6,7},{7,0},{8,9},{9,10},{10,1... | collective-permute-start | bytes 122888 | tf_op jit(solution)/shard_map/ppermute | solution.py:793
  36.2 5.0 %collective-permute-start.7 = (f32[5,16,128]{2,1,0:T(8,128)S(1)}, f32[5,16,128]{2,1,0:T(8,128)S(1)}, u32[]{:S(2)}, u32[]{:S(2)}) collective-permute-start(f32[5,16,128]{2,1,0:T(8,128)S(1)} %get-tuple-element.71), channel_id=1, source_target_pairs={{0,7},{1,0},{2,1},{3,2},{4,3},{5,4},{6,5},{7,6},{8,15},{9,8},{10,9... | collective-permute-start | bytes 122888 | tf_op jit(solution)/shard_map/ppermute | solution.py:794
  47.2 9.5 %collective-permute-start.8 = (f32[6,16,128]{2,1,0:T(8,128)S(1)}, f32[6,16,128]{2,1,0:T(8,128)S(1)}, u32[]{:S(2)}, u32[]{:S(2)}) collective-permute-start(f32[6,16,128]{2,1,0:T(8,128)S(1)} %get-tuple-element.91), channel_id=1, source_target_pairs={{0,1},{1,2},{2,3},{3,4},{4,5},{5,6},{6,7},{7,0},{8,9},{9,10},{10,1... | collective-permute-start | bytes 147464 | tf_op jit(solution)/shard_map/ppermute | solution.py:793
  47.2 9.5 %collective-permute-start.9 = (f32[6,16,128]{2,1,0:T(8,128)S(1)}, f32[6,16,128]{2,1,0:T(8,128)S(1)}, u32[]{:S(2)}, u32[]{:S(2)}) collective-permute-start(f32[6,16,128]{2,1,0:T(8,128)S(1)} %get-tuple-element.92), channel_id=1, source_target_pairs={{0,7},{1,0},{2,1},{3,2},{4,3},{5,4},{6,5},{7,6},{8,15},{9,8},{10,9... | collective-permute-start | bytes 147464 | tf_op jit(solution)/shard_map/ppermute | solution.py:794
where the time goes:
time: 60.7 us; the launch traced here: 60.3 us
  Pallas kernels  34.9 us (57%)
  starting transfers between devices  16.1 us (27%)
  local copies, waits for them, and re-layouts  6.79 us (11%)
  waiting for transfers between devices  1.71 us (3%)
  between operations  0.73 us (1%)
    pallas_call x9, Pallas kernels, call(): pl.pallas_call(kernel, in_specs=[VMEM_SPEC] * len(args), out_specs=[VMEM_...  34.9 us
    ppermute x4, starting transfers between devices, swap(): from_upper = lax.ppermute(to_lower, axis, ring(axis, -1))  9.83 us
    unnamed x16, local copies, waits for them, and re-layouts  6.79 us
    ppermute x4, starting transfers between devices, swap(): from_lower = lax.ppermute(to_upper, axis, ring(axis, 1))  3.16 us
    ppermute x1, starting transfers between devices, body(): lax.ppermute(mx, 'gy', ring('gy', k))  2.21 us
    ppermute x1, waiting for transfers between devices, body(): lax.ppermute(mx, 'gy', ring('gy', k))  1.63 us
  transfers between devices with their start and end apart: 10, of which 2 were waited for; matrix products, arithmetic and copies ran while one was open for 0% of the time, Pallas kernels for 28%

commit v1 on v0

v1 whole, which is shorter than its diff:
```python
import functools
import math

import jax
import jax.numpy as jnp
from jax import lax
from jax.experimental import pallas as pl
from jax.experimental.pallas import tpu as pltpu
from jax.sharding import PartitionSpec as P

SECTIONS = 4
ISO_PART = 0.1
HEAT_RATIO = 5.0 / 3.0
COURANT = 0.3
VISCOSITY = 0.5

F32 = jnp.float32
FAR = 1.0e4
SUB = 8
HALO = 2
STRIDE = 8
NGEO = 7

MAIN = (0, 1, 2, 0, 1)
NSAME = 2
STRIP_SHIFT = (0, 1, STRIDE - 1, STRIDE, STRIDE + 1)
STEP_X = (0, 1, -1, 0, 1)
STEP_Y = (0, 0, 1, 1, 1)


def conduction_polynomial(total):
    weight = 4.0 / (total * total + total - 2)
    c = [1.0 / 3.0] * 3 + [(j * j + j - 2) / (2.0 * j * (j + 1)) for j in range(3, total + 1)]
    older = [1.0] + [0.0] * total
    newer = [1.0, c[1] * weight] + [0.0] * (total - 1)
    for j in range(2, total + 1):
        m = (2 * j - 1) / j * c[j] / c[j - 1]
        n = -(j - 1) / j * c[j] / c[j - 2]
        fresh = [m * a + n * b for a, b in zip(newer, older)]
        fresh[0] += 1.0 - m - n
        for k in range(total):
            fresh[k + 1] += m * weight * newer[k]
        fresh[1] -= (1.0 - c[j - 1]) * m * weight
        older, newer = newer, fresh
    return newer


def roll(x, shift):
    lanes = x.shape[-1]
    return x if shift % lanes == 0 else pltpu.roll(x, shift % lanes, x.ndim - 1)


def lane_iota(shape):
    return lax.broadcasted_iota(jnp.int32, shape, len(shape) - 1)


def spread(ref, p, lanes):
    return jnp.broadcast_to(ref[p : p + 1, :], (SUB, lanes))


def duty(e, g, p):
    if e:
        return 2
    mine = p // SUB
    return 0 if g < mine else 1 if g == mine else 2


def sincos(x):
    k = jnp.floor(x * (2.0 / math.pi) + 0.5)
    r = ((x - k * 1.5703125) - k * 4.837512969970703125e-4) - k * 7.54978995489188216e-8
    z = r * r
    s = r + r * z * (-1.6666654611e-1 + z * (8.3321608736e-3 + z * -1.9515295891e-4))
    c = (
        1.0
        - 0.5 * z
        + z * z * (4.166664568298827e-2 + z * (-1.388731625493765e-3 + z * 2.443315711809948e-5))
    )
    kk = k * k
    odd = kk == 1.0
    turned = kk == 4.0
    s_neg = jnp.logical_or(turned, k == -1.0)
    c_neg = jnp.logical_or(turned, k == 1.0)
    sv = jnp.where(odd, c, s)
    cv = jnp.where(odd, s, c)
    return jnp.where(s_neg, -sv, sv), jnp.where(c_neg, -cv, cv)


def prep_kernel(*refs):
    n = 8
    sources, (geo, aux, su, sd, mx), held, sems = refs[:n], refs[n : n + 5], refs[n + 5 : -1], refs[-1]
    copies = [pltpu.make_async_copy(sources[k], held[k], sems.at[k]) for k in range(n)]
    for copy in copies:
        copy.start()
    for copy in copies:
        copy.wait()
    pop, coord, tilt, mass, kappa, cap, temp, vel = held
    rows, slots, lanes = geo.shape[2:]
    slot = lax.broadcasted_iota(jnp.int32, (slots, lanes), 0)
    best = None
    for r in range(rows):
        pick = (pl.ds(r, slots, stride=rows), slice(None))
        live = slot < pop[r : r + 1, :]
        st, ct = sincos(tilt[(0,) + pick])
        sp, cp = sincos(tilt[(1,) + pick])
        half = math.sqrt(0.5)
        st = st * half
        t = temp[pick]
        v = [vel[(k,) + pick] for k in range(3)]
        tiles = [
            jnp.where(live, coord[(0,) + pick], FAR),
            coord[(1,) + pick],
            coord[(2,) + pick],
            0.5 * kappa[pick],
            st * cp,
            st * sp,
            ct * half,
        ]
        for k, tile in enumerate(tiles):
            geo[0, k, r] = tile
        inv_cap = jnp.where(live, 1.0 / cap[pick], 0.0)
        m = mass[pick]
        side = [t, inv_cap, m] + v
        for k, tile in enumerate(side):
            aux[k, r] = tile
        for ref, first, edge in ((su, 0, 0), (sd, rows - HALO, rows - 1)):
            if first <= r < first + HALO:
                for k, tile in enumerate(tiles + [t]):
                    ref[k * HALO + r - first] = tile
            if r == edge:
                for k, tile in enumerate(side[1:]):
                    ref[(NGEO + 1) * HALO + k] = tile
        bound = jnp.sqrt(HEAT_RATIO * (HEAT_RATIO - 1.0) * t) + jnp.sqrt(
            v[0] * v[0] + v[1] * v[1] + v[2] * v[2]
        )
        bound = jnp.where(live, bound, 0.0)
        best = bound if best is None else jnp.maximum(best, bound)
    mx[...] = best
    su[(NGEO + 1) * HALO + 5] = best
    sd[(NGEO + 1) * HALO + 5] = best
    for r in range(rows):
        for k in range(NGEO):
            geo[1, k, r], geo[2, k, r] = beside(geo[0, k, r], k)


def beside(tile, k):
    lanes = tile.shape[-1]
    after, before = roll(tile, -1), roll(tile, 1)
    if k == 0:
        lane = lane_iota(tile.shape)
        after = jnp.where(lane == lanes - 1, -FAR, after + 1.0)
        before = jnp.where(lane == 0, -FAR, before - 1.0)
    return after, before


def weights(entries, own, far, w_ref, s_ref, idx):
    slots, lanes = own(0).shape
    groups = slots // SUB
    for e in entries:
        for g in range(groups):
            j = [far(e, k)[g * SUB : (g + 1) * SUB, :] for k in range(NGEO)]
            if STEP_Y[e]:
                j[1] = j[1] + float(STEP_Y[e])
            for p in range(slots):
                if not duty(e, g, p):
                    continue
                i = [spread(own(k), p, lanes) for k in range(NGEO)]
                dxx, dyy, dzz = (i[k] - j[k] for k in range(3))
                s = jnp.maximum(1.0 - (dxx * dxx + dyy * dyy + dzz * dzz), 0.0)
                a = i[4] * dxx + i[5] * dyy + i[6] * dzz
                b = j[4] * dxx + j[5] * dyy + j[6] * dzz
                w = (s * s * s) * (ISO_PART + (a * a + b * b)) * (i[3] + j[3])
                slot = e * groups + g
                w_ref[idx, p, slot] = w
                s_ref[idx, p, slot] = s


ALL = tuple(range(len(MAIN)))


def row_far(ref, row):
    return lambda e, k: ref.at[MAIN[e], k, row + (1 if e >= NSAME else 0)]


def pack_side(put, key, left, right, side, row, lanes):
    m, vx, vy, vz = side
    at = STRIDE * row
    left = put(left, m, at + 1, jnp.logical_or(key == 1, key == 2))
    right = put(right, m, at + 5 - lanes, jnp.logical_or(key == 3, key == 4))
    for k, tile in enumerate((vx, vy, vz)):
        left = put(left, tile, at + 3 + k, key == 3 + k)
        right = put(right, tile, at + 3 - k - lanes, key == 2 - k)
    return left, right


def pack_rows(cl, cr, start, feature, side, rows, side_rows):
    slots, lanes = cl.shape[1:]
    lane = lane_iota((slots, lanes))
    key = lane % STRIDE
    line = lane // STRIDE
    for k in range(NGEO + 2):
        blank = FAR if k == 0 else 0.0
        left, right = start(k, blank)
        for row in rows if k <= NGEO else side_rows:
            tile = feature(k, row) if k <= NGEO else side(0, row)
            here = line == row
            left = jnp.where(here, roll(tile, STRIDE * row + 1), left)
            right = jnp.where(here, roll(tile, STRIDE * row + 5 - lanes), right)
        cl[k] = jnp.where(jnp.logical_and(key >= 1, key <= 5), left, blank)
        cr[k] = jnp.where(key <= 4, right, blank)
    left, right = start(NGEO + 2, 0.0)
    for row in side_rows:
        here = line == row

        def put(into, tile, shift, where):
            return jnp.where(jnp.logical_and(here, where), roll(tile, shift), into)

        left, right = pack_side(put, key, left, right, [side(1 + k, row) for k in range(4)], row, lanes)
    cl[NGEO + 2] = left
    cr[NGEO + 2] = right


def near_kernel(geo, aux, w, s, cl, cr):
    rows, slots, lanes = geo.shape[2:]

    @pl.loop(0, rows - 2)
    def _(r):
        weights(ALL, lambda k: geo.at[0, k, r], row_far(geo, r), w, s, r + HALO)

    own = range(HALO, HALO + rows)
    pack_rows(
        cl,
        cr,
        lambda k, blank: (jnp.full((slots, lanes), blank, F32),) * 2,
        lambda k, row: geo[0, k, row - HALO] if k < NGEO else aux[0, row - HALO],
        lambda k, row: aux[1 + k, row - HALO],
        own,
        own,
    )


def pack_kernel(geo, ru, rd, clp, crp, mx, *rest):
    spare, (ge, th, ich, mvh, cl, cr, ma) = rest[:-7], rest[-7:]
    rows, slots, lanes = geo.shape[2:]
    at_top = lax.axis_index("gy") == 0
    at_end = lax.axis_index("gy") == lax.axis_size("gy") - 1
    base = (NGEO + 1) * HALO
    end = rows + HALO

    def feature(k, row):
        tile = ru[k * HALO + row] if row < HALO else rd[k * HALO + row - end]
        return jnp.where(at_top if row < HALO else at_end, FAR, tile) if k == 0 else tile

    def side(k, row):
        tile = ru[base + k] if row < HALO else rd[base + k]
        return jnp.where(at_top if row < HALO else at_end, 0.0, tile) if k == 0 else tile

    for k in range(NGEO):
        for n, row in enumerate((0, 1, 2, rows, rows + 1, rows + 2, rows + 3)):
            if HALO <= row < end:
                for variant in range(3):
                    ge[variant, k, n] = geo[variant, k, row - HALO]
            else:
                tile = feature(k, row)
                ge[0, k, n] = tile
                ge[1, k, n], ge[2, k, n] = beside(tile, k)
    for n, row in enumerate((0, 1, end, end + 1)):
        th[n] = feature(NGEO, row)
    for n, row in enumerate((HALO - 1, end)):
        ich[n] = side(0, row)
        for k in range(4):
            mvh[k, n] = side(1 + k, row)
    pack_rows(
        cl,
        cr,
        lambda k, blank: (clp[k], crp[k]),
        feature,
        side,
        (0, 1, end, end + 1),
        (HALO - 1, end),
    )
    best = jnp.maximum(jnp.maximum(ru[base + 5], rd[base + 5]), mx[...])
    for ref in spare:
        best = jnp.maximum(best, ref[...])
    ma[...] = best
    cl[NGEO + 3] = best
    cr[NGEO + 3] = best


def rim_kernel(ge, w_in, s_in, w, s):
    del w_in, s_in
    rows = w.shape[0] - 2 * HALO + 1
    slots = w.shape[1]
    groups = slots // SUB
    for p in range(slots):
        for slot in range(NSAME * groups):
            w[0, p, slot] = jnp.zeros(w.shape[3:], F32)
            s[0, p, slot] = jnp.zeros(w.shape[3:], F32)
    weights(ALL[NSAME:], lambda k: ge.at[0, k, 0], row_far(ge, 0), w, s, 0)

    @pl.loop(0, 4)
    def _(n):
        at = jnp.where(n > 0, n + 2, 1)
        weights(
            ALL, lambda k: ge.at[0, k, at], row_far(ge, at), w, s, jnp.where(n > 0, at + rows - 3, 1)
        )


def gathered(acc):
    slots = acc.shape[0] // SUB
    total = acc[pl.ds(0, slots, stride=SUB), :]
    for k in range(1, SUB):
        total = total + acc[pl.ds(k, slots, stride=SUB), :]
    return total


def stacked(parts, e, groups, like):
    return jnp.concatenate(
        [parts[e, g] if (e, g) in parts else jnp.zeros(like, F32) for g in range(groups)], 0
    )


def apply_block(own, far, w_ref, idx, acc, acc_d, cube):
    slots, lanes = own.shape
    groups = slots // SUB
    there = {(e, g): far(e)[g * SUB : (g + 1) * SUB, :] for e in ALL for g in range(groups)}
    back = {}
    bare = {}
    for p in range(slots):
        mine = spread(own, p, lanes)
        total = None
        total_d = None
        for e in ALL:
            for g in range(groups):
                how = duty(e, g, p)
                if not how:
                    continue
                w = w_ref[idx, p, e * groups + g]
                if cube:
                    w = w * w * w
                term = w * there[e, g]
                total = term if total is None else total + term
                if acc_d is not None:
                    total_d = w if total_d is None else total_d + w
                if how == 2:
                    term = w * mine
                    back[e, g] = back[e, g] + term if (e, g) in back else term
                    if acc_d is not None:
                        bare[e, g] = bare[e, g] + w if (e, g) in bare else w
        acc[p * SUB : (p + 1) * SUB, :] = total
        if acc_d is not None:
            acc_d[p * SUB : (p + 1) * SUB, :] = total_d
    like = (SUB, lanes)
    given = [(gathered(acc), [stacked(back, e, groups, like) for e in ALL])]
    if acc_d is not None:
        given.append((gathered(acc_d), [stacked(bare, e, groups, like) for e in ALL]))
    return given


def spread_values(val, val_t):
    for row in range(val.shape[1]):
        val[1, row] = roll(val[0, row], -1)
        val[2, row] = roll(val[0, row], 1)
    for e in ALL[1:]:
        for side in range(2):
            val_t[e, side] = roll(val_t[0, side], -STRIP_SHIFT[e])


def partner_sums(w, wt, val, val_t, outs, outs_t, accs, cube=False):
    last = w.shape[0]
    slots, lanes = val.shape[2:]
    acc, acc_d = accs if len(accs) == 2 else (accs[0], None)
    for out in outs:
        for k in range(3):
            out[k, 0] = jnp.zeros((slots, lanes), F32)

    @pl.loop(0, 2)
    def _(side):
        given = apply_block(
            val_t.at[0, side], lambda e: val_t.at[e, side], wt, side, acc, acc_d, cube
        )
        for (sums, back), out_t in zip(given, outs_t):
            out_t[0, side] = sums + back[0]
            for e in ALL[1:]:
                out_t[e, side] = back[e]

    @pl.loop(0, last)
    def _(row):
        given = apply_block(
            val.at[0, row],
            lambda e: val.at[MAIN[e], row + (1 if e >= NSAME else 0)],
            w,
            row,
            acc,
            acc_d,
            cube,
        )
        for (sums, back), out in zip(given, outs):
            out[0, row] += sums + back[0]
            out[1, row] += back[1]
            out[2, row + 1] = back[2]
            out[0, row + 1] = back[3]
            out[1, row + 1] = back[4]

    lane = lane_iota((slots, lanes))
    for out, out_t in zip(outs, outs_t):
        ends = []
        for side in range(2):
            total = out_t[0, side]
            for e in ALL[1:]:
                total = total + roll(out_t[e, side], STRIP_SHIFT[e])
            out_t[0, side] = total
            ends.append(total)
        for row in range(last + 1):
            at = STRIDE * row
            edge = jnp.where(
                lane == 0,
                roll(ends[0], -(at + 5)),
                jnp.where(lane == lanes - 1, roll(ends[1], lanes - 1 - at), 0.0),
            )
            out[0, row] = (out[0, row] + edge) + (roll(out[1, row], 1) + roll(out[2, row], -1))


def fill_strips(rows, low, high, first):
    lanes = low.shape[-1]
    lane = lane_iota(low.shape)
    for n, tile in enumerate(rows):
        at = STRIDE * (n + first)
        low = jnp.where(lane == at + 5, roll(tile, at + 5), low)
        high = jnp.where(lane == at, roll(tile, at + 1 - lanes), high)
    return low, high


def advance(val, val_t, out, out_t, diag, diag_t, ic, ict):
    fresh = []
    for row in range(val.shape[1]):
        tile = ic[row] * (out[0, row] - val[0, row] * diag[row])
        val[0, row] = tile
        fresh.append(tile)
    ends = [ict[side] * (out_t[0, side] - val_t[0, side] * diag_t[side]) for side in range(2)]
    val_t[0, 0], val_t[0, 1] = fill_strips(fresh, *ends, 0)


def first_half_kernel(aux, th, ich, rl, rr, cl, cr, w, *rest):
    spare, rest = rest[:-23], rest[-23:]
    (wt, st, v1, v1t, v2, v2t, diag, diag_t, ic, ict, tside, tt, su, sd, ma2) = rest[:15]
    tgeo, val, val_t, out, out_t, bare, bare_t, acc = rest[15:]
    rows = w.shape[0] + 1 - 2 * HALO
    slots, lanes = val.shape[2:]
    full = rows + 2 * HALO
    at_left = lax.axis_index("gx") == 0
    at_right = lax.axis_index("gx") == lax.axis_size("gx") - 1
    lane = lane_iota((slots, lanes))
    key = lane % STRIDE
    from_left = key <= 4
    from_right = jnp.logical_and(key >= 1, key <= 5)
    own_left = key == 5
    own_right = key == 0
    for k in range(NGEO + 1):
        left, right = rl[k], rr[k]
        blank = 0.0
        if k == 0:
            left = jnp.where(at_left, FAR, left)
            right = jnp.where(at_right, FAR, right)
            blank = FAR
        left = jnp.where(from_left, left, jnp.where(own_left, roll(cl[k], 4), blank))
        right = jnp.where(from_right, right, jnp.where(own_right, roll(cr[k], -4), blank))
        for side, tile in ((0, left), (1, right)):
            if k == NGEO:
                tt[side] = tile
                val_t[0, side] = tile
                continue
            tgeo[len(ALL), k, side] = tile
            mine = own_right if side else own_left
            for e in ALL:
                turned = roll(tile, -STRIP_SHIFT[e])
                if k == 0:
                    turned = turned + float(STEP_X[e])
                    if e in (0, 3):
                        turned = jnp.where(mine, -FAR, turned)
                tgeo[e, k, side] = turned
                if k < 3:
                    tside[e, k, side] = turned + float(STEP_Y[e]) if k == 1 else turned
            if k < 3:
                tside[len(ALL), k, side] = tile
    ict[0] = jnp.where(jnp.logical_and(from_left, jnp.logical_not(at_left)), rl[NGEO + 1], 0.0)
    ict[1] = jnp.where(jnp.logical_and(from_right, jnp.logical_not(at_right)), rr[NGEO + 1], 0.0)
    near_l, near_r, own_l, own_r = rl[NGEO + 2], rr[NGEO + 2], cl[NGEO + 2], cr[NGEO + 2]
    place = len(ALL)
    tside[place, 3, 0] = jnp.where(
        jnp.logical_or(key == 3, key == 4), near_l, jnp.where(own_left, roll(own_l, 4), 0.0)
    )
    tside[place, 3, 1] = jnp.where(
        jnp.logical_or(key == 1, key == 2), near_r, jnp.where(own_right, roll(own_r, -4), 0.0)
    )
    for k in range(3):
        tside[place, 4 + k, 0] = jnp.where(
            key == 4, roll(near_l, 2 + k), jnp.where(own_left, roll(own_l, 2 - k), 0.0)
        )
        tside[place, 4 + k, 1] = jnp.where(
            key == 1, roll(near_r, -2 - k), jnp.where(own_right, roll(own_r, k - 2), 0.0)
        )

    @pl.loop(0, 2)
    def _(side):
        weights(
            ALL, lambda k: tgeo.at[len(ALL), k, side], lambda e, k: tgeo.at[e, k, side], wt, st, side
        )

    for row in range(full):
        if row < HALO:
            val[0, row] = th[row]
        elif row < rows + HALO:
            val[0, row] = aux[0, row - HALO]
        else:
            val[0, row] = th[row - rows]
        if row == HALO - 1:
            ic[row] = ich[0]
        elif row == rows + HALO:
            ic[row] = ich[1]
        elif HALO <= row < rows + HALO:
            ic[row] = aux[1, row - HALO]
        else:
            ic[row] = jnp.zeros((slots, lanes), F32)
    spread_values(val, val_t)
    partner_sums(
        w, wt, val, val_t, (out, bare), (out_t, bare_t), (acc.at[0], acc.at[1])
    )
    for row in range(full):
        diag[row] = bare[0, row]
    for side in range(2):
        diag_t[side] = bare_t[0, side]
    advance(val, val_t, out, out_t, diag, diag_t, ic, ict)
    for row in range(rows):
        v1[row] = val[0, row + HALO]
    for side in range(2):
        v1t[side] = val_t[0, side]
    spread_values(val, val_t)
    partner_sums(w, wt, val, val_t, (out,), (out_t,), (acc.at[0],))
    advance(val, val_t, out, out_t, diag, diag_t, ic, ict)
    best = jnp.maximum(rl[NGEO + 3], rr[NGEO + 3])
    for ref in spare:
        best = jnp.maximum(best, ref[...])
    ma2[...] = best
    for row in range(rows):
        v2[row] = val[0, row + HALO]
    for side in range(2):
        v2t[side] = val_t[0, side]
    for ref, start in ((su, HALO), (sd, rows)):
        for n in range(HALO):
            ref[n] = val[0, start + n]
        for side in range(2):
            ref[HALO + side] = val_t[0, side]
        ref[HALO + 2] = best


def density_kernel(aux, mvh, ict, tside, s, st, kn, mut, inv, invt, val, val_t, out, out_t, acc):
    rows = aux.shape[1]
    slots, lanes = val.shape[2:]
    for row in range(rows + 2 * HALO):
        if row == HALO - 1:
            val[0, row] = mvh[0, 0]
        elif row == rows + HALO:
            val[0, row] = mvh[0, 1]
        elif HALO <= row < rows + HALO:
            val[0, row] = aux[2, row - HALO]
        else:
            val[0, row] = jnp.zeros((slots, lanes), F32)
    for side in range(2):
        val_t[0, side] = tside[len(ALL), 3, side]
    spread_values(val, val_t)
    for side in range(2):
        for e in ALL:
            tside[e, 3, side] = val_t[e, side]
            for k in range(4, 7):
                tside[e, k, side] = roll(tside[len(ALL), k, side], -STRIP_SHIFT[e])
    partner_sums(s, st, val, val_t, (out,), (out_t,), (acc,), cube=True)
    scale = math.sqrt(VISCOSITY)
    mu = []
    for row in range(rows):
        live = aux[1, row] > 0.0
        inverse = 1.0 / jnp.where(live, out[0, row + HALO], 1.0)
        inv[row] = inverse
        mu.append(scale * aux[2, row] * inverse)
    ends = []
    for side in range(2):
        live = ict[side] > 0.0
        inverse = 1.0 / jnp.where(live, out_t[0, side], 1.0)
        invt[side] = inverse
        ends.append(scale * val_t[0, side] * inverse)
    mut[0], mut[1] = fill_strips(mu, *ends, HALO)
    for row in range(rows):
        for k, tile in enumerate([mu[row]] + [aux[2 + n, row] for n in range(4)]):
            kn[0, k, row] = tile
            kn[1, k, row] = roll(tile, -1)
            kn[2, k, row] = roll(tile, 1)


def second_half_kernel(
    aux, v1, v1t, v2, v2t, tt, ma2, ru, rd, diag, diag_t, ic, ict, w, wt, kn, mut, inv, invt,
    heat, press, press_t, su, sd, dt,
    val, val_t, out, out_t, acc, hot_t,
):
    rows, slots, lanes = v1.shape
    full = rows + 2 * HALO
    coef = conduction_polynomial(SECTIONS)
    best = jnp.maximum(jnp.maximum(ru[HALO + 2], rd[HALO + 2]), ma2[...])
    best = jnp.max(jnp.max(best, axis=1, keepdims=True), axis=0, keepdims=True)
    step = COURANT / jnp.broadcast_to(best, (SUB, lanes))
    dt[...] = step
    step = jnp.concatenate([step] * (slots // SUB), 0)
    for row in range(full):
        if row < HALO:
            val[0, row] = ru[row]
        elif row < rows + HALO:
            val[0, row] = v2[row - HALO]
        else:
            val[0, row] = rd[row - rows - HALO]
    lane = lane_iota((slots, lanes))
    turn = STRIDE * rows
    for side in range(2):
        val_t[0, side] = jnp.where(
            lane < STRIDE * HALO,
            roll(ru[HALO + side], -turn),
            jnp.where(lane >= STRIDE * (rows + HALO), roll(rd[HALO + side], turn), v2t[side]),
        )
    power = [step, step * step]
    first, second = coef[1] * power[0], coef[2] * power[1]
    place = lambda row: (pl.ds(row, slots, stride=rows), slice(None))
    for row in range(rows):
        heat[place(row)] = aux[0, row] + first * v1[row] + second * v2[row]
    for side in range(2):
        hot_t[side] = tt[side] + first * v1t[side] + second * v2t[side]
    for section in (3, 4):
        spread_values(val, val_t)
        partner_sums(w, wt, val, val_t, (out,), (out_t,), (acc,))
        advance(val, val_t, out, out_t, diag, diag_t, ic, ict)
        power.append(power[-1] * step)
        factor = coef[section] * power[-1]
        for row in range(rows):
            heat[place(row)] += factor * val[0, row + HALO]
        for side in range(2):
            hot_t[side] += factor * val_t[0, side]
    scale = 6.0 * (HEAT_RATIO - 1.0)
    fresh = []
    for row in range(rows):
        tile = scale * heat[place(row)] * inv[row]
        press[0, row] = tile
        press[1, row] = roll(tile, -1)
        press[2, row] = roll(tile, 1)
        fresh.append(tile)
    ends = [scale * hot_t[side] * invt[side] for side in range(2)]
    press_t[0], press_t[1] = fill_strips(fresh, *ends, HALO)
    for ref, row in ((su, 0), (sd, rows - 1)):
        ref[0] = fresh[row]
        ref[1] = kn[0, 0, row]
        for side in range(2):
            ref[2 + side] = press_t[side]
            ref[4 + side] = mut[side]


NKICK = 9


def kick_block(entries, own, far, step_y, s_ref, idx, acc):
    slots, lanes = own(0).shape
    groups = slots // SUB
    back = {}
    for n, e in enumerate(entries):
        j = []
        for g in range(groups):
            t = [far(e, k)[g * SUB : (g + 1) * SUB, :] for k in range(NKICK)]
            if step_y and STEP_Y[e]:
                t[1] = t[1] + float(STEP_Y[e])
            j.append(t)
        sums = {}
        for p in range(slots):
            i = [spread(own(k), p, lanes) for k in range(NKICK)]
            mine = [None] * 3
            for g in range(groups):
                how = duty(e, g, p)
                if not how:
                    continue
                s = s_ref[idx, p, e * groups + g]
                s2 = s * s
                drag = (s2 * s) * (i[4] * j[g][4])
                push = (i[3] + j[g][3]) * (s2 * (i[5] * j[g][5]))
                for k in range(3):
                    term = push * (i[k] - j[g][k]) + drag * (j[g][6 + k] - i[6 + k])
                    mine[k] = term if mine[k] is None else mine[k] + term
                    if how == 2:
                        sums[k, g] = sums[k, g] + term if (k, g) in sums else term
            for k in range(3):
                at = (k, slice(p * SUB, (p + 1) * SUB), slice(None))
                acc[at] = mine[k] if n == 0 else acc[at] + mine[k]
        for k in range(3):
            back[e, k] = stacked(sums, k, groups, (SUB, lanes)) if sums else None
    return back


def kick_near_kernel(geo, kn, press, s, heat, out, heated, acc, sem):
    copy = pltpu.make_async_copy(heat, heated, sem)
    copy.start()
    rows, slots, lanes = geo.shape[2:]
    for k in range(3):
        for side in range(3):
            out[side, k, 0] = jnp.zeros((slots, lanes), F32)

    def feature(k, row, variant):
        if k < 3:
            return geo.at[variant, k, row]
        return press.at[variant, row] if k == 3 else kn.at[variant, k - 4, row]

    def far(r):
        return lambda e, k: feature(k, r + (1 if e >= NSAME else 0), MAIN[e])

    def one(entries, r):
        back = kick_block(entries, lambda k: feature(k, r, 0), far(r), True, s, r + HALO, acc)
        for k in range(3):
            out[0, k, r] += gathered(acc.at[k]) - back[0, k]
            out[1, k, r] -= back[1, k]
            if len(entries) > NSAME:
                out[2, k, r + 1] = -back[2, k]
                out[0, k, r + 1] = -back[3, k]
                out[1, k, r + 1] = -back[4, k]

    @pl.loop(0, rows - 1)
    def _(r):
        one(ALL, r)

    one(ALL[:NSAME], rows - 1)
    copy.wait()


def kick_rim_kernel(
    geo, aux, kn, press, ge, mvh, tside, mut, press_t, ru, rd, s, st, near, dt,
    moved, mine, other, strip, out, out_t, acc,
):
    rows, slots, lanes = geo.shape[2:]
    nge = ge.shape[2]
    for k in range(NKICK):
        for variant in range(3):
            if k < 3:
                other[variant, k, 0] = geo[variant, k, 0]
                other[variant, k, 1] = ge[variant, k, nge - 2]
            else:
                other[variant, k, 0] = press[variant, 0] if k == 3 else kn[variant, k - 4, 0]
                tile = rd[k - 3] if k < 5 else mvh[k - 5, 1]
                other[variant, k, 1] = roll(tile, (0, -1, 1)[variant])
        if k < 3:
            mine[k, 0] = ge[0, k, 1]
            mine[k, 1] = geo[0, k, rows - 1]
        else:
            mine[k, 0] = ru[k - 3] if k < 5 else mvh[k - 5, 0]
            mine[k, 1] = press[0, rows - 1] if k == 3 else kn[0, k - 4, rows - 1]
    lane = lane_iota((slots, lanes))
    turn = STRIDE * rows
    for k in range(3, 5):
        for side in range(2):
            at = 2 + 2 * (k - 3) + side
            tile = jnp.where(
                lane < STRIDE * HALO,
                roll(ru[at], -turn),
                jnp.where(
                    lane >= STRIDE * (rows + HALO),
                    roll(rd[at], turn),
                    (press_t, mut)[k - 3][side],
                ),
            )
            strip[len(ALL), k - 3, side] = tile
            for e in ALL:
                strip[e, k - 3, side] = roll(tile, -STRIP_SHIFT[e])

    @pl.loop(0, 2)
    def _(side):
        def feature(k, e):
            if k < 3:
                return tside.at[e, k, side]
            return strip.at[e, k - 3, side] if k < 5 else tside.at[e, k - 2, side]

        back = kick_block(
            ALL, lambda k: feature(k, len(ALL)), lambda e, k: feature(k, e), False, st, side, acc
        )
        for k in range(3):
            out_t[0, k, side] = gathered(acc.at[k]) - back[0, k]
            for e in ALL[1:]:
                out_t[e, k, side] = back[e, k]

    @pl.loop(0, 2)
    def _(n):
        back = kick_block(
            ALL[NSAME:],
            lambda k: mine.at[k, n],
            lambda e, k: other.at[MAIN[e], k, n],
            True,
            s,
            1 + n * rows,
            acc,
        )
        for k in range(3):
            out[3, k, n] = gathered(acc.at[k])
            for e in ALL[NSAME:]:
                out[MAIN[e], k, n] = -back[e, k]

    step = jnp.concatenate([dt[...]] * (slots // SUB), 0)
    ends = {}
    for k in range(3):
        for side in range(2):
            total = out_t[0, k, side]
            for e in ALL[1:]:
                total = total - roll(out_t[e, k, side], STRIP_SHIFT[e])
            ends[k, side] = total
    for row in range(rows):
        live = aux[1, row] > 0.0
        factor = jnp.where(live, step / aux[2, row], 0.0)
        at = STRIDE * (row + HALO)
        for k in range(3):
            parts = [near[variant, k, row] for variant in range(3)]
            if row == 0:
                parts = [part + out[variant, k, 0] for variant, part in enumerate(parts)]
            if row == rows - 1:
                parts[0] = parts[0] + out[3, k, 1]
            edge = jnp.where(
                lane == 0,
                roll(ends[k, 0], -(at + 5)),
                jnp.where(lane == lanes - 1, roll(ends[k, 1], lanes - 1 - at), 0.0),
            )
            total = (parts[0] + edge) + (roll(parts[1], 1) + roll(parts[2], -1))
            moved[k, pl.ds(row, slots, stride=rows), :] = aux[3 + k, row] + factor * total


VMEM_SPEC = pl.BlockSpec(memory_space=pltpu.VMEM)
HBM_SPEC = pl.BlockSpec(memory_space=pltpu.HBM)


def call(kernel, args, outs, scratch=(), name=None, limit=24, aliases=None, far_out=()):
    return pl.pallas_call(
        kernel,
        in_specs=[VMEM_SPEC] * len(args),
        out_specs=[HBM_SPEC if n in far_out else VMEM_SPEC for n in range(len(outs))],
        out_shape=[jax.ShapeDtypeStruct(o, F32) for o in outs],
        scratch_shapes=[pltpu.VMEM(s, F32) if isinstance(s, tuple) else s for s in scratch],
        input_output_aliases=aliases or {},
        compiler_params=pltpu.CompilerParams(vmem_limit_bytes=limit * 1024 * 1024),
        name=name,
    )(*args)


def ring(axis, shift):
    n = lax.axis_size(axis)
    return [(i, (i + shift) % n) for i in range(n)]


def swap(to_lower, to_upper, axis):
    from_lower = lax.ppermute(to_upper, axis, ring(axis, 1))
    from_upper = lax.ppermute(to_lower, axis, ring(axis, -1))
    return from_lower, from_upper


def body(pop, coord, tilt, mass, kappa, cap, temp, vel):
    slots, rows, lanes = temp.shape
    flat = lambda x: x.reshape(x.shape[:-3] + (slots * rows, lanes))
    tile = (slots, lanes)
    full = rows + 2 * HALO
    groups = slots // SUB
    npart = len(ALL)
    nsend = (NGEO + 1) * HALO + 6
    inputs = (pop,) + tuple(flat(x) for x in (coord, tilt, mass, kappa, cap, temp, vel))
    inputs = [pltpu.with_memory_space_constraint(x, pltpu.HBM) for x in inputs]
    geo, aux, su, sd, mx = pl.pallas_call(
        prep_kernel,
        in_specs=[HBM_SPEC] * len(inputs),
        out_specs=[VMEM_SPEC] * 5,
        out_shape=[
            jax.ShapeDtypeStruct(o, F32)
            for o in (
                (3, NGEO, rows) + tile,
                (6, rows) + tile,
                (nsend,) + tile,
                (nsend,) + tile,
                tile,
            )
        ],
        scratch_shapes=[pltpu.VMEM(x.shape, x.dtype) for x in inputs]
        + [pltpu.SemaphoreType.DMA((len(inputs),))],
        compiler_params=pltpu.CompilerParams(vmem_limit_bytes=24 * 1024 * 1024),
        name="prep",
    )(*inputs)
    ru, rd = swap(su, sd, "gy")
    spare = [lax.ppermute(mx, "gy", ring("gy", k)) for k in range(4, lax.axis_size("gy") - 2, 3)]
    pairs = (full - 1, slots, npart * groups, SUB, lanes)
    strips = (2,) + pairs[1:]
    columns = (NGEO + 4,) + tile
    two = (2,) + tile
    own = (rows,) + tile
    ext = (full,) + tile
    w, s, clp, crp = call(
        near_kernel, (geo, aux), [pairs, pairs, (NGEO + 3,) + tile, (NGEO + 3,) + tile], name="near"
    )
    ge, th, ich, mvh, cl, cr, ma = call(
        pack_kernel,
        (geo, ru, rd, clp, crp, mx, *spare),
        [(3, NGEO, 7) + tile, (4,) + tile, two, (4,) + two, columns, columns, tile],
        name="pack",
    )
    rl, rr = swap(cl, cr, "gx")
    spare = [lax.ppermute(ma, "gx", ring("gx", k)) for k in range(2, lax.axis_size("gx") - 1)]
    w, s = call(rim_kernel, (ge, w, s), [pairs, pairs], name="rim", aliases={1: 0, 2: 1})
    sums = (slots * SUB, lanes)
    work = [(3,) + ext, (npart,) + two, (3,) + ext, (npart,) + two]
    wt, st, v1, v1t, v2, v2t, diag, diag_t, ic, ict, tside, tt, su, sd, ma2 = call(
        first_half_kernel,
        (aux, th, ich, rl, rr, cl, cr, w, ma, *spare),
        [strips, strips, own, two, own, two, ext, two, ext, two, (npart + 1, 7) + two, two]
        + [(HALO + 3,) + tile] * 2
        + [tile],
        [(npart + 1, NGEO) + two] + work + work[2:] + [(2,) + sums],
        name="first_half",
    )
    ru, rd = swap(su, sd, "gy")
    tside, kn, mut, inv, invt = call(
        density_outer,
        (tside, aux, mvh, ict, s, st),
        [(npart + 1, 7) + two, (3, 5) + own, two, own, two],
        work + [sums],
        name="density",
        aliases={0: 0},
    )
    heat, press, press_t, su, sd, dt = call(
        second_half_kernel,
        (aux, v1, v1t, v2, v2t, tt, ma2, ru, rd, diag, diag_t, ic, ict, w, wt, kn, mut, inv, invt),
        [(slots * rows, lanes), (3,) + own, two, (6,) + tile, (6,) + tile, (SUB, lanes)],
        work + [sums, two],
        name="second_half",
    )
    ru, rd = swap(su, sd, "gy")
    near, heated = call(
        kick_near_kernel,
        (geo, kn, press, s, heat),
        [(3, 3) + own, (slots * rows, lanes)],
        [(3,) + sums, pltpu.SemaphoreType.DMA(())],
        name="kick_near",
        far_out=(1,),
    )
    moved = call(
        kick_rim_kernel,
        (geo, aux, kn, press, ge, mvh, tside, mut, press_t, ru, rd, s, st, near, dt),
        [(3, slots * rows, lanes)],
        [(NKICK,) + two, (3, NKICK) + two, (npart + 1, 2) + two, (4, 3) + two, (npart, 3) + two]
        + [(3,) + sums],
        name="kick_rim",
    )[0]
    return heated.reshape(temp.shape), moved.reshape(vel.shape)


def density_outer(tside_in, aux, mvh, ict, s, st, tside, *rest):
    del tside_in
    density_kernel(aux, mvh, ict, tside, s, st, *rest)


def solution(mesh):
    in_specs = (
        P("gy", "gx"),
        P(None, None, "gy", "gx"),
        P(None, None, "gy", "gx"),
        P(None, "gy", "gx"),
        P(None, "gy", "gx"),
        P(None, "gy", "gx"),
        P(None, "gy", "gx"),
        P(None, None, "gy", "gx"),
    )
    out_specs = (P(None, "gy", "gx"), P(None, None, "gy", "gx"))
    return jax.shard_map(body, mesh=mesh, in_specs=in_specs, out_specs=out_specs, check_vma=False)
```

time: 60.7 us -> 46.3 us (0.76)
  local copies, waits for them, and re-layouts: 6.79 us -> 0 us
  Pallas kernels: 34.9 us -> 28.5 us
  waiting for transfers between devices: 1.71 us -> 1.03 us
    unnamed x16 -> x0, local copies, waits for them, and re-layouts: 6.79 us -> none
    pallas_call x9, Pallas kernels: 34.9 us -> 28.5 us  [the longest x8 26.9 us: call(): pl.pallas_call(kernel, in_specs=[VMEM_SPEC] * len(args), out_specs=[HBM_S...]
    ppermute x1, waiting for transfers between devices: 1.63 us -> 0.01 us  [body(): lax.ppermute(mx, 'gy', ring('gy', k))]
    ppermute x1, waiting for transfers between devices: 0.01 us -> 1 us  [body(): lax.ppermute(ma, 'gx', ring('gx', k))]
    ppermute x4, starting transfers between devices: 3.16 us -> 2.29 us  [swap(): from_lower = lax.ppermute(to_upper, axis, ring(axis, 1))]
    ppermute x4, starting transfers between devices: 9.83 us -> 10.4 us  [swap(): from_upper = lax.ppermute(to_lower, axis, ring(axis, -1))]
  transfers between devices with their start and end apart: 10 -> 10, of which waited for: 2 -> 1; matrix products, arithmetic and copies ran while one was open for 0% -> 0% of each run, Pallas kernels for 28% -> 31%
where the time goes in v1:
time: 46.3 us; the launch traced here: 46.1 us
  Pallas kernels  28.5 us (62%)
  starting transfers between devices  15.7 us (34%)
  waiting for transfers between devices  1.03 us (2%)
  between operations  0.76 us (2%)
    pallas_call x8, Pallas kernels, call(): pl.pallas_call(kernel, in_specs=[VMEM_SPEC] * len(args), out_specs=[HBM_S...  26.9 us
    ppermute x4, starting transfers between devices, swap(): from_upper = lax.ppermute(to_lower, axis, ring(axis, -1))  10.4 us
    ppermute x4, starting transfers between devices, swap(): from_lower = lax.ppermute(to_upper, axis, ring(axis, 1))  2.29 us
    ppermute x1, starting transfers between devices, body(): lax.ppermute(mx, 'gy', ring('gy', k))  2.21 us
    pallas_call x1, Pallas kernels, body(): pl.pallas_call(prep_kernel, in_specs=[HBM_SPEC] * len(inputs), out_specs=...  1.68 us
    ppermute x1, waiting for transfers between devices, body(): lax.ppermute(ma, 'gx', ring('gx', k))  1 us
  transfers between devices with their start and end apart: 10, of which 1 were waited for; matrix products, arithmetic and copies ran while one was open for 0% of the time, Pallas kernels for 31%

profile of v1, /device:TPU:0, one launch (start us, length us, event | category | flops | bytes accessed | tf_op | source)
XLA Modules:
  0.0 46.1 jit_solution(13448328228217397406)
XLA Ops:
  0.6 1.7 %prep.1 = (f32[3,7,8,16,128]{4,3,2,1,0:T(8,128)S(1)}, f32[6,8,16,128]{3,2,1,0:T(8,128)S(1)}, f32[22,16,128]{2,1,0:T(8,128)S(1)}, f32[22,16,128]{2,1,0:T(8,128)S(1)}, f32[16,128]{1,0:T(8,128)S(1)}) custom-call(s32[8,128]{1,0:T(8,128)} %refs_0_.1, f32[3,128,128]{2,1,0:T(8,128)} %bitcast.10, f32[2,128,128]{2,1,0:T(8,128)} %bitcast.12, f32[128,128]{1,0:T(8,128)} %bitcast.13, ...), custom_call_target="tpu_custom_call" | custom-call | tf_op jit(solution)/shard_map/prep/pallas_call | solution.py:869
  2.3 0.5 %collective-permute-start = (f32[22,16,128]{2,1,0:T(8,128)S(1)}, f32[22,16,128]{2,1,0:T(8,128)S(1)}, u32[]{:S(2)}, u32[]{:S(2)}) collective-permute-start(f32[22,16,128]{2,1,0:T(8,128)S(1)} %get-tuple-element.50), channel_id=1, source_target_pairs={{0,1},{1,2},{2,3},{3,4},{4,5},{5,6},{6,7},{7,0},{8,9},{9,10},{10,1... | collective-permute-start | bytes 540680 | tf_op jit(solution)/shard_map/ppermute | solution.py:854
  2.9 2.9 %collective-permute-start.1 = (f32[22,16,128]{2,1,0:T(8,128)S(1)}, f32[22,16,128]{2,1,0:T(8,128)S(1)}, u32[]{:S(2)}, u32[]{:S(2)}) collective-permute-start(f32[22,16,128]{2,1,0:T(8,128)S(1)} %get-tuple-element.51), channel_id=1, source_target_pairs={{0,7},{1,0},{2,1},{3,2},{4,3},{5,4},{6,5},{7,6},{8,15},{9,8},{10,9... | collective-permute-start | bytes 540680 | tf_op jit(solution)/shard_map/ppermute | solution.py:855
  5.8 2.2 %collective-permute-start.2 = (f32[16,128]{1,0:T(8,128)S(1)}, f32[16,128]{1,0:T(8,128)S(1)}, u32[]{:S(2)}, u32[]{:S(2)}) collective-permute-start(f32[16,128]{1,0:T(8,128)S(1)} %get-tuple-element.54.mx), channel_id=1, source_target_pairs={{0,4},{1,5},{2,6},{3,7},{4,0},{5,1},{6,2},{7,3},{8,12},{9,13},{10,... | collective-permute-start | bytes 24584 | tf_op jit(solution)/shard_map/ppermute | solution.py:889
  8.0 4.0 %near.1 = (f32[11,16,10,8,128]{4,3,2,1,0:T(8,128)S(1)}, f32[11,16,10,8,128]{4,3,2,1,0:T(8,128)S(1)}, f32[10,16,128]{2,1,0:T(8,128)S(1)}, f32[10,16,128]{2,1,0:T(8,128)S(1)}) custom-call(f32[3,7,8,16,128]{4,3,2,1,0:T(8,128)S(1)} %get-tuple-element.48.geo, f32[6,8,16,128]{3,2,1,0:T(8,128)S(1)} %get-tuple-element.49.aux), custom_call_target="tpu_custom_call" | custom-call | tf_op jit(solution)/shard_map/near/pallas_call | solution.py:836
  12.0 0.0 collective-permute-done.2.rest_0_
  12.1 0.0 collective-permute-done.ru
  12.1 0.0 collective-permute-done.1.rd
  12.1 0.4 pack.1
  12.4 1.6 %collective-permute-start.3 = (f32[11,16,128]{2,1,0:T(8,128)S(1)}, f32[11,16,128]{2,1,0:T(8,128)S(1)}, u32[]{:S(2)}, u32[]{:S(2)}) collective-permute-start(f32[11,16,128]{2,1,0:T(8,128)S(1)} %get-tuple-element.57.cr), channel_id=1, source_target_pairs={{0,8},{8,16},{16,24},{24,0},{1,9},{9,17},{17,25},{25,1},{2,10},{10... | collective-permute-start | bytes 270344 | tf_op jit(solution)/shard_map/ppermute | solution.py:854
  14.1 2.2 %collective-permute-start.4 = (f32[11,16,128]{2,1,0:T(8,128)S(1)}, f32[11,16,128]{2,1,0:T(8,128)S(1)}, u32[]{:S(2)}, u32[]{:S(2)}) collective-permute-start(f32[11,16,128]{2,1,0:T(8,128)S(1)} %get-tuple-element.58.cl), channel_id=1, source_target_pairs={{0,24},{8,0},{16,8},{24,16},{1,25},{9,1},{17,9},{25,17},{2,26},{10... | collective-permute-start | bytes 270344 | tf_op jit(solution)/shard_map/ppermute | solution.py:855
  16.3 0.8 %collective-permute-start.5 = (f32[16,128]{1,0:T(8,128)S(1)}, f32[16,128]{1,0:T(8,128)S(1)}, u32[]{:S(2)}, u32[]{:S(2)}) collective-permute-start(f32[16,128]{1,0:T(8,128)S(1)} %get-tuple-element.63.rest_0_), channel_id=1, source_target_pairs={{0,16},{8,24},{16,0},{24,8},{1,17},{9,25},{17,1},{25,9},{2,18},{10... | collective-permute-start | bytes 24584 | tf_op jit(solution)/shard_map/ppermute | solution.py:906
  17.1 2.8 %rim.1 = (f32[11,16,10,8,128]{4,3,2,1,0:T(8,128)S(1)}, f32[11,16,10,8,128]{4,3,2,1,0:T(8,128)S(1)}) custom-call(f32[3,7,7,16,128]{4,3,2,1,0:T(8,128)S(1)} %get-tuple-element.59.ge, f32[11,16,10,8,128]{4,3,2,1,0:T(8,128)S(1)} %get-tuple-element.60.w_in, f32[11,16,10,8,128]{4,3,2,1,0:T(8,128)S(1)} %get-tuple-element.61.s_in), custom_call_target="tpu_custom_call", output_to_operand_aliasing={{0}: (1, {}), {1}: (2, {})} | custom-call | tf_op jit(solution)/shard_map/rim/pallas_call | solution.py:836
  19.9 1.0 %collective-permute-done.5.rest_1_ = f32[16,128]{1,0:T(8,128)S(1)} collective-permute-done((f32[16,128]{1,0:T(8,128)S(1)}, f32[16,128]{1,0:T(8,128)S(1)}, u32[]{:S(2)}, u32[]{:S(2)}) %collective-permute-start.5) | collective-permute-done | bytes 8224 | tf_op jit(solution)/shard_map/ppermute | solution.py:906
  20.9 0.0 collective-permute-done.3.rl
  20.9 0.0 collective-permute-done.4.rr
  20.9 5.6 %first_half.1 = (f32[2,16,10,8,128]{4,3,2,1,0:T(8,128)S(1)}, f32[2,16,10,8,128]{4,3,2,1,0:T(8,128)S(1)}, f32[8,16,128]{2,1,0:T(8,128)S(1)}, f32[2,16,128]{2,1,0:...) custom-call(f32[6,8,16,128]{3,2,1,0:T(8,128)S(1)} %get-tuple-element, ...), custom_call_target="tpu_custom_call" | custom-call | tf_op jit(solution)/shard_map/first_half/pallas_call | solution.py:836
  26.5 0.1 collective-permute-start.6
  26.5 2.6 %collective-permute-start.7 = (f32[5,16,128]{2,1,0:T(8,128)S(1)}, f32[5,16,128]{2,1,0:T(8,128)S(1)}, u32[]{:S(2)}, u32[]{:S(2)}) collective-permute-start(f32[5,16,128]{2,1,0:T(8,128)S(1)} %get-tuple-element.77), channel_id=1, source_target_pairs={{0,7},{1,0},{2,1},{3,2},{4,3},{5,4},{6,5},{7,6},{8,15},{9,8},{10,9... | collective-permute-start | bytes 122888 | tf_op jit(solution)/shard_map/ppermute | solution.py:855
  29.2 2.4 %density.1 = (f32[6,7,2,16,128]{4,3,2,1,0:T(8,128)S(1)}, f32[3,5,8,16,128]{4,3,2,1,0:T(8,128)S(1)}, f32[2,16,128]{2,1,0:T(8,128)S(1)}, f32[8,16,128]{2,1,0:T(8,128)S(1)}, f32[2,16,128]{2,1,0:T(8,128)S(1)}) custom-call(f32[6,7,2,16,128]{4,3,2,1,0:T(8,128)S(1)} %get-tuple-element.64.tside_in, ...), custom_call_target="tpu_custom_call", output_to_operand_aliasing={{0}: (0, {})} | custom-call | tf_op jit(solution)/shard_map/density/pallas_call | solution.py:836
  31.6 0.0 collective-permute-done.6.ru
  31.6 0.0 collective-permute-done.7.rd
  31.6 3.5 %second_half.1 = (f32[128,128]{1,0:T(8,128)S(1)}, f32[3,8,16,128]{3,2,1,0:T(8,128)S(1)}, f32[2,16,128]{2,1,0:T(8,128)S(1)}, f32[6,16,128]{2,1,0:T(8,128)S(1)}, f...) custom-call(f32[6,8,16,128]{3,2,1,0:T(8,128)S(1)} %get-tuple-element.49.aux, f32[8,16,128]{2,1,0:T(8,128)S(1)} %get-tuple-element.70.v1, ...), custom_call_target="tpu_custom_call" | custom-call | tf_op jit(solution)/shard_map/second_half/pallas_call | solution.py:836
  35.1 0.1 collective-permute-start.8
  35.2 2.6 %collective-permute-start.9 = (f32[6,16,128]{2,1,0:T(8,128)S(1)}, f32[6,16,128]{2,1,0:T(8,128)S(1)}, u32[]{:S(2)}, u32[]{:S(2)}) collective-permute-start(f32[6,16,128]{2,1,0:T(8,128)S(1)} %get-tuple-element.91), channel_id=1, source_target_pairs={{0,7},{1,0},{2,1},{3,2},{4,3},{5,4},{6,5},{7,6},{8,15},{9,8},{10,9... | collective-permute-start | bytes 147464 | tf_op jit(solution)/shard_map/ppermute | solution.py:855
  37.8 4.9 %kick_near.1 = (f32[3,3,8,16,128]{4,3,2,1,0:T(8,128)S(1)}, f32[128,128]{1,0:T(8,128)}) custom-call(f32[3,7,8,16,128]{4,3,2,1,0:T(8,128)S(1)} %get-tuple-element.48.geo, f32[3,5,8,16,128]{4,3,2,1,0:T(8,128)S(1)} %get-tuple-element.69.kn, f32[3,8,16,128]{3,2,1,0:T(8,128)S(1)} %get-tuple-element.85.press, f32[11,16,10,8,128]{4,3,2,1,0:T(8,128)S(1)} %get-tuple-element.67.s, ...), custom_call_target="tpu_custom_call" | custom-call | tf_op jit(solution)/shard_map/kick_near/pallas_call | solution.py:836
  42.7 0.0 collective-permute-done.8.ru
  42.7 0.0 collective-permute-done.9.rd
  42.7 3.3 %kick_rim.1 = f32[3,128,128]{2,1,0:T(8,128)} custom-call(f32[3,7,8,16,128]{4,3,2,1,0:T(8,128)S(1)} %get-tuple-element.48.geo, f32[6,8,16,128]{3,2,1,0:T(8,128)S(1)} %get-tuple-element.49.aux, f32[3,5,8,16,128]{4,3,2,1,0:T(8,128)S(1)} %get-tuple-element.69.kn, f32[3,8,16,128]{3,2,1,0:T(8,128)S(1)} %get-tuple-element.85.press, ...), custom_call_target="tpu_custom_call" | custom-call | tf_op jit(solution)/shard_map/kick_rim/pallas_call | solution.py:836
Async XLA Ops:
  2.3 9.7 %collective-permute-start = (f32[22,16,128]{2,1,0:T(8,128)S(1)}, f32[22,16,128]{2,1,0:T(8,128)S(1)}, u32[]{:S(2)}, u32[]{:S(2)}) collective-permute-start(f32[22,16,128]{2,1,0:T(8,128)S(1)} %get-tuple-element.50), channel_id=1, source_target_pairs={{0,1},{1,2},{2,3},{3,4},{4,5},{5,6},{6,7},{7,0},{8,9},{9,10},{10,1... | collective-permute-start | bytes 540680 | tf_op jit(solution)/shard_map/ppermute | solution.py:854
  2.9 9.2 %collective-permute-start.1 = (f32[22,16,128]{2,1,0:T(8,128)S(1)}, f32[22,16,128]{2,1,0:T(8,128)S(1)}, u32[]{:S(2)}, u32[]{:S(2)}) collective-permute-start(f32[22,16,128]{2,1,0:T(8,128)S(1)} %get-tuple-element.51), channel_id=1, source_target_pairs={{0,7},{1,0},{2,1},{3,2},{4,3},{5,4},{6,5},{7,6},{8,15},{9,8},{10,9... | collective-permute-start | bytes 540680 | tf_op jit(solution)/shard_map/ppermute | solution.py:855
  5.8 6.2 %collective-permute-start.2 = (f32[16,128]{1,0:T(8,128)S(1)}, f32[16,128]{1,0:T(8,128)S(1)}, u32[]{:S(2)}, u32[]{:S(2)}) collective-permute-start(f32[16,128]{1,0:T(8,128)S(1)} %get-tuple-element.54.mx), channel_id=1, source_target_pairs={{0,4},{1,5},{2,6},{3,7},{4,0},{5,1},{6,2},{7,3},{8,12},{9,13},{10,... | collective-permute-start | bytes 24584 | tf_op jit(solution)/shard_map/ppermute | solution.py:889
  12.4 8.4 %collective-permute-start.3 = (f32[11,16,128]{2,1,0:T(8,128)S(1)}, f32[11,16,128]{2,1,0:T(8,128)S(1)}, u32[]{:S(2)}, u32[]{:S(2)}) collective-permute-start(f32[11,16,128]{2,1,0:T(8,128)S(1)} %get-tuple-element.57.cr), channel_id=1, source_target_pairs={{0,8},{8,16},{16,24},{24,0},{1,9},{9,17},{17,25},{25,1},{2,10},{10... | collective-permute-start | bytes 270344 | tf_op jit(solution)/shard_map/ppermute | solution.py:854
  14.1 6.8 %collective-permute-start.4 = (f32[11,16,128]{2,1,0:T(8,128)S(1)}, f32[11,16,128]{2,1,0:T(8,128)S(1)}, u32[]{:S(2)}, u32[]{:S(2)}) collective-permute-start(f32[11,16,128]{2,1,0:T(8,128)S(1)} %get-tuple-element.58.cl), channel_id=1, source_target_pairs={{0,24},{8,0},{16,8},{24,16},{1,25},{9,1},{17,9},{25,17},{2,26},{10... | collective-permute-start | bytes 270344 | tf_op jit(solution)/shard_map/ppermute | solution.py:855
  16.3 4.6 %collective-permute-start.5 = (f32[16,128]{1,0:T(8,128)S(1)}, f32[16,128]{1,0:T(8,128)S(1)}, u32[]{:S(2)}, u32[]{:S(2)}) collective-permute-start(f32[16,128]{1,0:T(8,128)S(1)} %get-tuple-element.63.rest_0_), channel_id=1, source_target_pairs={{0,16},{8,24},{16,0},{24,8},{1,17},{9,25},{17,1},{25,9},{2,18},{10... | collective-permute-start | bytes 24584 | tf_op jit(solution)/shard_map/ppermute | solution.py:906
  26.5 5.1 %collective-permute-start.6 = (f32[5,16,128]{2,1,0:T(8,128)S(1)}, f32[5,16,128]{2,1,0:T(8,128)S(1)}, u32[]{:S(2)}, u32[]{:S(2)}) collective-permute-start(f32[5,16,128]{2,1,0:T(8,128)S(1)} %get-tuple-element.76), channel_id=1, source_target_pairs={{0,1},{1,2},{2,3},{3,4},{4,5},{5,6},{6,7},{7,0},{8,9},{9,10},{10,1... | collective-permute-start | bytes 122888 | tf_op jit(solution)/shard_map/ppermute | solution.py:854
  26.5 5.0 %collective-permute-start.7 = (f32[5,16,128]{2,1,0:T(8,128)S(1)}, f32[5,16,128]{2,1,0:T(8,128)S(1)}, u32[]{:S(2)}, u32[]{:S(2)}) collective-permute-start(f32[5,16,128]{2,1,0:T(8,128)S(1)} %get-tuple-element.77), channel_id=1, source_target_pairs={{0,7},{1,0},{2,1},{3,2},{4,3},{5,4},{6,5},{7,6},{8,15},{9,8},{10,9... | collective-permute-start | bytes 122888 | tf_op jit(solution)/shard_map/ppermute | solution.py:855
  35.1 7.6 %collective-permute-start.8 = (f32[6,16,128]{2,1,0:T(8,128)S(1)}, f32[6,16,128]{2,1,0:T(8,128)S(1)}, u32[]{:S(2)}, u32[]{:S(2)}) collective-permute-start(f32[6,16,128]{2,1,0:T(8,128)S(1)} %get-tuple-element.90), channel_id=1, source_target_pairs={{0,1},{1,2},{2,3},{3,4},{4,5},{5,6},{6,7},{7,0},{8,9},{9,10},{10,1... | collective-permute-start | bytes 147464 | tf_op jit(solution)/shard_map/ppermute | solution.py:854
  35.2 7.6 %collective-permute-start.9 = (f32[6,16,128]{2,1,0:T(8,128)S(1)}, f32[6,16,128]{2,1,0:T(8,128)S(1)}, u32[]{:S(2)}, u32[]{:S(2)}) collective-permute-start(f32[6,16,128]{2,1,0:T(8,128)S(1)} %get-tuple-element.91), channel_id=1, source_target_pairs={{0,7},{1,0},{2,1},{3,2},{4,3},{5,4},{6,5},{7,6},{8,15},{9,8},{10,9... | collective-permute-start | bytes 147464 | tf_op jit(solution)/shard_map/ppermute | solution.py:855

commit v2 on v1

--- a/solution.py
+++ b/solution.py
@@ -18,7 +18,7 @@
 FAR = 1.0e4
 SUB = 8
 HALO = 2
-STRIDE = 8
+STRIDE = 10
 NGEO = 7
 
 MAIN = (0, 1, 2, 0, 1)
@@ -181,48 +181,49 @@
     return lambda e, k: ref.at[MAIN[e], k, row + (1 if e >= NSAME else 0)]
 
 
-def pack_side(put, key, left, right, side, row, lanes):
-    m, vx, vy, vz = side
-    at = STRIDE * row
-    left = put(left, m, at + 1, jnp.logical_or(key == 1, key == 2))
-    right = put(right, m, at + 5 - lanes, jnp.logical_or(key == 3, key == 4))
-    for k, tile in enumerate((vx, vy, vz)):
-        left = put(left, tile, at + 3 + k, key == 3 + k)
-        right = put(right, tile, at + 3 - k - lanes, key == 2 - k)
-    return left, right
+def strip_place(shape):
+    lane = lane_iota(shape)
+    where = lane.astype(F32)
+    return lane, where - STRIDE * jnp.floor((where + 0.5) * (1.0 / STRIDE))
 
 
 def pack_rows(cl, cr, start, feature, side, rows, side_rows):
     slots, lanes = cl.shape[1:]
     lane = lane_iota((slots, lanes))
-    key = lane % STRIDE
-    line = lane // STRIDE
-    for k in range(NGEO + 2):
-        blank = FAR if k == 0 else 0.0
-        left, right = start(k, blank)
-        for row in rows if k <= NGEO else side_rows:
+    tiles = (NGEO + 3) // 2
+    left = [start(cl, n) for n in range(tiles)]
+    right = [start(cr, n) for n in range(tiles)]
+
+    def put(into, tile, shift, first, count):
+        here = jnp.logical_and(lane >= first, lane < first + count)
+        return jnp.where(here, roll(tile, shift), into)
+
+    for row in rows:
+        for k in range(NGEO + 2):
+            if k > NGEO and row not in side_rows:
+                continue
             tile = feature(k, row) if k <= NGEO else side(0, row)
-            here = line == row
-            left = jnp.where(here, roll(tile, STRIDE * row + 1), left)
-            right = jnp.where(here, roll(tile, STRIDE * row + 5 - lanes), right)
-        cl[k] = jnp.where(jnp.logical_and(key >= 1, key <= 5), left, blank)
-        cr[k] = jnp.where(key <= 4, right, blank)
-    left, right = start(NGEO + 2, 0.0)
-    for row in side_rows:
-        here = line == row
-
-        def put(into, tile, shift, where):
-            return jnp.where(jnp.logical_and(here, where), roll(tile, shift), into)
-
-        left, right = pack_side(put, key, left, right, [side(1 + k, row) for k in range(4)], row, lanes)
-    cl[NGEO + 2] = left
-    cr[NGEO + 2] = right
+            at = STRIDE * row + 5 * (k % 2)
+            n = k // 2
+            left[n] = put(left[n], tile, at + 1, at + 1, 5)
+            right[n] = put(right[n], tile, at + 5 - lanes, at, 5)
+        if row in side_rows:
+            m, vx, vy, vz = (side(1 + k, row) for k in range(4))
+            at = STRIDE * row + 5
+            left[-1] = put(left[-1], m, at + 1, at + 1, 2)
+            right[-1] = put(right[-1], m, at + 5 - lanes, at + 3, 2)
+            for k, tile in enumerate((vx, vy, vz)):
+                left[-1] = put(left[-1], tile, at + 3 + k, at + 3 + k, 1)
+                right[-1] = put(right[-1], tile, at + 3 - k - lanes, at + 2 - k, 1)
+    for n in range(tiles):
+        cl[n] = left[n]
+        cr[n] = right[n]
 
 
 def near_kernel(geo, aux, w, s, cl, cr):
     rows, slots, lanes = geo.shape[2:]
 
-    @pl.loop(0, rows - 2)
+    @pl.loop(0, rows - 1)
     def _(r):
         weights(ALL, lambda k: geo.at[0, k, r], row_far(geo, r), w, s, r + HALO)
 
@@ -230,7 +231,7 @@
     pack_rows(
         cl,
         cr,
-        lambda k, blank: (jnp.full((slots, lanes), blank, F32),) * 2,
+        lambda ref, n: jnp.zeros((slots, lanes), F32),
         lambda k, row: geo[0, k, row - HALO] if k < NGEO else aux[0, row - HALO],
         lambda k, row: aux[1 + k, row - HALO],
         own,
@@ -255,7 +256,7 @@
         return jnp.where(at_top if row < HALO else at_end, 0.0, tile) if k == 0 else tile
 
     for k in range(NGEO):
-        for n, row in enumerate((0, 1, 2, rows, rows + 1, rows + 2, rows + 3)):
+        for n, row in enumerate((0, 1, 2, rows + 1, rows + 2, rows + 3)):
             if HALO <= row < end:
                 for variant in range(3):
                     ge[variant, k, n] = geo[variant, k, row - HALO]
@@ -272,7 +273,7 @@
     pack_rows(
         cl,
         cr,
-        lambda k, blank: (clp[k], crp[k]),
+        lambda ref, n: (clp if ref is cl else crp)[n],
         feature,
         side,
         (0, 1, end, end + 1),
@@ -282,27 +283,52 @@
     for ref in spare:
         best = jnp.maximum(best, ref[...])
     ma[...] = best
-    cl[NGEO + 3] = best
-    cr[NGEO + 3] = best
-
-
-def rim_kernel(ge, w_in, s_in, w, s):
+    cl[(NGEO + 3) // 2] = best
+    cr[(NGEO + 3) // 2] = best
+
+
+def rim_kernel(ge, w_in, s_in, aux, th, w, s, out, bare, val, acc):
     del w_in, s_in
     rows = w.shape[0] - 2 * HALO + 1
     slots = w.shape[1]
     groups = slots // SUB
+    extended(val, lambda row: aux[0, row], lambda row: th[row])
+    spread_rows(val)
+    clear(out)
+    clear(bare)
     for p in range(slots):
         for slot in range(NSAME * groups):
             w[0, p, slot] = jnp.zeros(w.shape[3:], F32)
             s[0, p, slot] = jnp.zeros(w.shape[3:], F32)
     weights(ALL[NSAME:], lambda k: ge.at[0, k, 0], row_far(ge, 0), w, s, 0)
 
-    @pl.loop(0, 4)
+    @pl.loop(0, 3)
     def _(n):
         at = jnp.where(n > 0, n + 2, 1)
         weights(
-            ALL, lambda k: ge.at[0, k, at], row_far(ge, at), w, s, jnp.where(n > 0, at + rows - 3, 1)
+            ALL, lambda k: ge.at[0, k, at], row_far(ge, at), w, s, jnp.where(n > 0, at + rows - 2, 1)
         )
+
+    @pl.loop(0, w.shape[0])
+    def _(row):
+        row_sums(w, val, (out, bare), (acc.at[0], acc.at[1]), row)
+
+
+def extended(val, own, halo):
+    full = val.shape[1]
+    for row in range(full):
+        if row < HALO:
+            val[0, row] = halo(row)
+        elif row < full - HALO:
+            val[0, row] = own(row - HALO)
+        else:
+            val[0, row] = halo(row - full + 2 * HALO)
+
+
+def clear(out):
+    for k in range(3):
+        for row in range(out.shape[1]):
+            out[k, row] = jnp.zeros(out.shape[2:], F32)
 
 
 def gathered(acc):
@@ -356,114 +382,127 @@
     return given
 
 
-def spread_values(val, val_t):
+def spread_rows(val):
     for row in range(val.shape[1]):
         val[1, row] = roll(val[0, row], -1)
         val[2, row] = roll(val[0, row], 1)
+
+
+def spread_strips(val_t):
     for e in ALL[1:]:
         for side in range(2):
             val_t[e, side] = roll(val_t[0, side], -STRIP_SHIFT[e])
 
 
-def partner_sums(w, wt, val, val_t, outs, outs_t, accs, cube=False):
-    last = w.shape[0]
-    slots, lanes = val.shape[2:]
-    acc, acc_d = accs if len(accs) == 2 else (accs[0], None)
-    for out in outs:
-        for k in range(3):
-            out[k, 0] = jnp.zeros((slots, lanes), F32)
-
+def row_sums(w, val, outs, accs, row, cube=False):
+    given = apply_block(
+        val.at[0, row],
+        lambda e: val.at[MAIN[e], row + (1 if e >= NSAME else 0)],
+        w,
+        row,
+        accs[0],
+        accs[1] if len(accs) == 2 else None,
+        cube,
+    )
+    for (sums, back), out in zip(given, outs):
+        out[0, row] += sums + back[0]
+        out[1, row] += back[1]
+        out[2, row + 1] += back[2]
+        out[0, row + 1] += back[3]
+        out[1, row + 1] += back[4]
+
+
+def strip_sums(wt, val_t, outs_t, accs, cube=False):
     @pl.loop(0, 2)
     def _(side):
         given = apply_block(
-            val_t.at[0, side], lambda e: val_t.at[e, side], wt, side, acc, acc_d, cube
+            val_t.at[0, side],
+            lambda e: val_t.at[e, side],
+            wt,
+            side,
+            accs[0],
+            accs[1] if len(accs) == 2 else None,
+            cube,
         )
         for (sums, back), out_t in zip(given, outs_t):
             out_t[0, side] = sums + back[0]
             for e in ALL[1:]:
                 out_t[e, side] = back[e]
 
-    @pl.loop(0, last)
-    def _(row):
-        given = apply_block(
-            val.at[0, row],
-            lambda e: val.at[MAIN[e], row + (1 if e >= NSAME else 0)],
-            w,
-            row,
-            acc,
-            acc_d,
-            cube,
-        )
-        for (sums, back), out in zip(given, outs):
-            out[0, row] += sums + back[0]
-            out[1, row] += back[1]
-            out[2, row + 1] = back[2]
-            out[0, row + 1] = back[3]
-            out[1, row + 1] = back[4]
-
-    lane = lane_iota((slots, lanes))
-    for out, out_t in zip(outs, outs_t):
-        ends = []
-        for side in range(2):
-            total = out_t[0, side]
-            for e in ALL[1:]:
-                total = total + roll(out_t[e, side], STRIP_SHIFT[e])
-            out_t[0, side] = total
-            ends.append(total)
-        for row in range(last + 1):
-            at = STRIDE * row
-            edge = jnp.where(
-                lane == 0,
-                roll(ends[0], -(at + 5)),
-                jnp.where(lane == lanes - 1, roll(ends[1], lanes - 1 - at), 0.0),
-            )
-            out[0, row] = (out[0, row] + edge) + (roll(out[1, row], 1) + roll(out[2, row], -1))
-
-
-def fill_strips(rows, low, high, first):
-    lanes = low.shape[-1]
-    lane = lane_iota(low.shape)
+
+def settle(out, out_t, first, last):
+    shape = out.shape[2:]
+    lanes = shape[-1]
+    lane, key = strip_place(shape)
+    ends = []
+    for side in range(2):
+        total = out_t[0, side]
+        for e in ALL[1:]:
+            total = total + roll(out_t[e, side], STRIP_SHIFT[e])
+        out_t[0, side] = total
+        ends.append(total)
+    both = jnp.where(key == 5.0, ends[0], roll(ends[1], 4))
+    border = jnp.logical_or(lane == 0, lane == lanes - 1)
+    for row in range(first, last):
+        edge = jnp.where(border, roll(both, -(STRIDE * row + 5)), 0.0)
+        out[0, row] = (out[0, row] + edge) + (roll(out[1, row], 1) + roll(out[2, row], -1))
+
+
+def end_columns(rows, first, start=None):
+    shape = rows[0].shape
+    lane = lane_iota(shape)
+    ends = jnp.zeros(shape, F32) if start is None else start
     for n, tile in enumerate(rows):
         at = STRIDE * (n + first)
-        low = jnp.where(lane == at + 5, roll(tile, at + 5), low)
-        high = jnp.where(lane == at, roll(tile, at + 1 - lanes), high)
-    return low, high
-
-
-def advance(val, val_t, out, out_t, diag, diag_t, ic, ict):
+        here = jnp.logical_or(lane == at + 4, lane == at + 5)
+        ends = jnp.where(here, roll(tile, at + 5), ends)
+    return ends
+
+
+def advance(val, val_t, out, out_t, diag, diag_t, ic, ict, first, last):
     fresh = []
-    for row in range(val.shape[1]):
+    for row in range(first, last):
         tile = ic[row] * (out[0, row] - val[0, row] * diag[row])
         val[0, row] = tile
         fresh.append(tile)
-    ends = [ict[side] * (out_t[0, side] - val_t[0, side] * diag_t[side]) for side in range(2)]
-    val_t[0, 0], val_t[0, 1] = fill_strips(fresh, *ends, 0)
-
-
-def first_half_kernel(aux, th, ich, rl, rr, cl, cr, w, *rest):
+    key = strip_place(fresh[0].shape)[1]
+    columns = end_columns(fresh, first)
+    for side in range(2):
+        tile = ict[side] * (out_t[0, side] - val_t[0, side] * diag_t[side])
+        mine = columns if side == 0 else roll(columns, -4)
+        val_t[0, side] = jnp.where(key == (0.0 if side else 5.0), mine, tile)
+
+
+def first_half_kernel(aux, th, ich, rl, rr, cl, cr, w, out1, bare1, *rest):
     spare, rest = rest[:-23], rest[-23:]
     (wt, st, v1, v1t, v2, v2t, diag, diag_t, ic, ict, tside, tt, su, sd, ma2) = rest[:15]
-    tgeo, val, val_t, out, out_t, bare, bare_t, acc = rest[15:]
+    tgeo, val, val_t, out, out_t, bare_t, diag3, acc = rest[15:]
     rows = w.shape[0] + 1 - 2 * HALO
     slots, lanes = val.shape[2:]
     full = rows + 2 * HALO
     at_left = lax.axis_index("gx") == 0
     at_right = lax.axis_index("gx") == lax.axis_size("gx") - 1
-    lane = lane_iota((slots, lanes))
-    key = lane % STRIDE
-    from_left = key <= 4
-    from_right = jnp.logical_and(key >= 1, key <= 5)
-    own_left = key == 5
-    own_right = key == 0
+    lane, key = strip_place((slots, lanes))
+    inside = lane < STRIDE * full
+    from_left = jnp.logical_and(inside, key <= 4.0)
+    from_right = jnp.logical_and(inside, jnp.logical_and(key >= 1.0, key <= 5.0))
+    own_left = jnp.logical_and(inside, key == 5.0)
+    own_right = jnp.logical_and(inside, key == 0.0)
+
+    def got(ref, k):
+        return roll(ref[k // 2], -5) if k % 2 else ref[k // 2]
+
     for k in range(NGEO + 1):
-        left, right = rl[k], rr[k]
+        left, right = got(rl, k), got(rr, k)
         blank = 0.0
         if k == 0:
             left = jnp.where(at_left, FAR, left)
             right = jnp.where(at_right, FAR, right)
             blank = FAR
-        left = jnp.where(from_left, left, jnp.where(own_left, roll(cl[k], 4), blank))
-        right = jnp.where(from_right, right, jnp.where(own_right, roll(cr[k], -4), blank))
+        mine = roll(cl[k // 2], -1 if k % 2 else 4)
+        left = jnp.where(from_left, left, jnp.where(own_left, mine, blank))
+        mine = roll(cr[k // 2], -9 if k % 2 else -4)
+        right = jnp.where(from_right, right, jnp.where(own_right, mine, blank))
         for side, tile in ((0, left), (1, right)):
             if k == NGEO:
                 tt[side] = tile
@@ -478,26 +517,25 @@
                     if e in (0, 3):
                         turned = jnp.where(mine, -FAR, turned)
                 tgeo[e, k, side] = turned
-                if k < 3:
-                    tside[e, k, side] = turned + float(STEP_Y[e]) if k == 1 else turned
             if k < 3:
-                tside[len(ALL), k, side] = tile
-    ict[0] = jnp.where(jnp.logical_and(from_left, jnp.logical_not(at_left)), rl[NGEO + 1], 0.0)
-    ict[1] = jnp.where(jnp.logical_and(from_right, jnp.logical_not(at_right)), rr[NGEO + 1], 0.0)
-    near_l, near_r, own_l, own_r = rl[NGEO + 2], rr[NGEO + 2], cl[NGEO + 2], cr[NGEO + 2]
-    place = len(ALL)
-    tside[place, 3, 0] = jnp.where(
-        jnp.logical_or(key == 3, key == 4), near_l, jnp.where(own_left, roll(own_l, 4), 0.0)
-    )
-    tside[place, 3, 1] = jnp.where(
-        jnp.logical_or(key == 1, key == 2), near_r, jnp.where(own_right, roll(own_r, -4), 0.0)
+                tside[k, side] = tile
+    ict[0] = jnp.where(jnp.logical_and(from_left, jnp.logical_not(at_left)), got(rl, NGEO + 1), 0.0)
+    ict[1] = jnp.where(
+        jnp.logical_and(from_right, jnp.logical_not(at_right)), got(rr, NGEO + 1), 0.0
+    )
+    near_l, near_r, own_l, own_r = (got(ref, NGEO + 2) for ref in (rl, rr, cl, cr))
+    tside[3, 0] = jnp.where(
+        jnp.logical_or(key == 3.0, key == 4.0), near_l, jnp.where(own_left, roll(own_l, 4), 0.0)
+    )
+    tside[3, 1] = jnp.where(
+        jnp.logical_or(key == 1.0, key == 2.0), near_r, jnp.where(own_right, roll(own_r, -4), 0.0)
     )
     for k in range(3):
-        tside[place, 4 + k, 0] = jnp.where(
-            key == 4, roll(near_l, 2 + k), jnp.where(own_left, roll(own_l, 2 - k), 0.0)
+        tside[4 + k, 0] = jnp.where(
+            key == 4.0, roll(near_l, 2 + k), jnp.where(own_left, roll(own_l, 2 - k), 0.0)
         )
-        tside[place, 4 + k, 1] = jnp.where(
-            key == 1, roll(near_r, -2 - k), jnp.where(own_right, roll(own_r, k - 2), 0.0)
+        tside[4 + k, 1] = jnp.where(
+            key == 1.0, roll(near_r, -2 - k), jnp.where(own_right, roll(own_r, k - 2), 0.0)
         )
 
     @pl.loop(0, 2)
@@ -506,13 +544,8 @@
             ALL, lambda k: tgeo.at[len(ALL), k, side], lambda e, k: tgeo.at[e, k, side], wt, st, side
         )
 
+    extended(val, lambda row: aux[0, row], lambda row: th[row])
     for row in range(full):
-        if row < HALO:
-            val[0, row] = th[row]
-        elif row < rows + HALO:
-            val[0, row] = aux[0, row - HALO]
-        else:
-            val[0, row] = th[row - rows]
         if row == HALO - 1:
             ic[row] = ich[0]
         elif row == rows + HALO:
@@ -521,23 +554,38 @@
             ic[row] = aux[1, row - HALO]
         else:
             ic[row] = jnp.zeros((slots, lanes), F32)
-    spread_values(val, val_t)
-    partner_sums(
-        w, wt, val, val_t, (out, bare), (out_t, bare_t), (acc.at[0], acc.at[1])
-    )
+    spread_strips(val_t)
+    strip_sums(wt, val_t, (out_t, bare_t), (acc.at[0], acc.at[1]))
+    for k in range(3):
+        for row in range(full):
+            out[k, row] = out1[k, row]
+    settle(out, out_t, 1, full - 1)
     for row in range(full):
-        diag[row] = bare[0, row]
+        diag3[0, row] = bare1[0, row]
+        diag3[1, row] = bare1[1, row]
+        diag3[2, row] = bare1[2, row]
+    settle(diag3, bare_t, 1, full - 1)
+    for row in range(full):
+        diag[row] = diag3[0, row] if 0 < row < full - 1 else jnp.zeros((slots, lanes), F32)
     for side in range(2):
         diag_t[side] = bare_t[0, side]
-    advance(val, val_t, out, out_t, diag, diag_t, ic, ict)
+    advance(val, val_t, out, out_t, diag, diag_t, ic, ict, 1, full - 1)
     for row in range(rows):
         v1[row] = val[0, row + HALO]
     for side in range(2):
         v1t[side] = val_t[0, side]
-    spread_values(val, val_t)
-    partner_sums(w, wt, val, val_t, (out,), (out_t,), (acc.at[0],))
-    advance(val, val_t, out, out_t, diag, diag_t, ic, ict)
-    best = jnp.maximum(rl[NGEO + 3], rr[NGEO + 3])
+    spread_rows(val)
+    spread_strips(val_t)
+    clear(out)
+    strip_sums(wt, val_t, (out_t,), (acc.at[0],))
+
+    @pl.loop(HALO - 1, rows + HALO)
+    def _(row):
+        row_sums(w, val, (out,), (acc.at[0],), row)
+
+    settle(out, out_t, HALO, rows + HALO)
+    advance(val, val_t, out, out_t, diag, diag_t, ic, ict, HALO, rows + HALO)
+    best = jnp.maximum(rl[(NGEO + 3) // 2], rr[(NGEO + 3) // 2])
     for ref in spare:
         best = jnp.maximum(best, ref[...])
     ma2[...] = best
@@ -553,27 +601,25 @@
         ref[HALO + 2] = best
 
 
-def density_kernel(aux, mvh, ict, tside, s, st, kn, mut, inv, invt, val, val_t, out, out_t, acc):
+def density_kernel(
+    aux, mvh, ict, tside, s, st, v2, w, kn, kst, inv, invt, out3, val, val_t, out, out_t, acc
+):
     rows = aux.shape[1]
     slots, lanes = val.shape[2:]
-    for row in range(rows + 2 * HALO):
-        if row == HALO - 1:
-            val[0, row] = mvh[0, 0]
-        elif row == rows + HALO:
-            val[0, row] = mvh[0, 1]
-        elif HALO <= row < rows + HALO:
-            val[0, row] = aux[2, row - HALO]
-        else:
-            val[0, row] = jnp.zeros((slots, lanes), F32)
+    blank = jnp.zeros((slots, lanes), F32)
+    extended(val, lambda row: aux[2, row], lambda n: mvh[0, n - 1] if n in (1, 2) else blank)
     for side in range(2):
-        val_t[0, side] = tside[len(ALL), 3, side]
-    spread_values(val, val_t)
-    for side in range(2):
-        for e in ALL:
-            tside[e, 3, side] = val_t[e, side]
-            for k in range(4, 7):
-                tside[e, k, side] = roll(tside[len(ALL), k, side], -STRIP_SHIFT[e])
-    partner_sums(s, st, val, val_t, (out,), (out_t,), (acc,), cube=True)
+        val_t[0, side] = tside[3, side]
+    spread_rows(val)
+    spread_strips(val_t)
+    clear(out)
+    strip_sums(st, val_t, (out_t,), (acc,), cube=True)
+
+    @pl.loop(HALO - 1, rows + HALO)
+    def _(row):
+        row_sums(s, val, (out,), (acc,), row, cube=True)
+
+    settle(out, out_t, HALO, rows + HALO)
     scale = math.sqrt(VISCOSITY)
     mu = []
     for row in range(rows):
@@ -587,16 +633,48 @@
         inverse = 1.0 / jnp.where(live, out_t[0, side], 1.0)
         invt[side] = inverse
         ends.append(scale * val_t[0, side] * inverse)
-    mut[0], mut[1] = fill_strips(mu, *ends, HALO)
+    key = strip_place((slots, lanes))[1]
+    merged = [merge(key, tside[k, 0], tside[k, 1]) for k in range(3)]
+    merged += [with_ends(key, merge(key, *ends), mu)]
+    merged += [merge(key, tside[k, 0], tside[k, 1]) for k in range(3, 7)]
+    for k, tile in zip((0, 1, 2, 4, 5, 6, 7, 8), merged):
+        kst[len(ALL), k] = tile
+        for e in ALL:
+            turned = roll(tile, -STRIP_SHIFT[e])
+            if k < 2:
+                turned = turned + float((STEP_X, STEP_Y)[k][e])
+            kst[e, k] = turned
     for row in range(rows):
         for k, tile in enumerate([mu[row]] + [aux[2 + n, row] for n in range(4)]):
             kn[0, k, row] = tile
             kn[1, k, row] = roll(tile, -1)
             kn[2, k, row] = roll(tile, 1)
+    for row in range(rows):
+        for k in range(3):
+            val[k, row + HALO] = roll(v2[row], (0, -1, 1)[k])
+    clear(out3)
+
+    @pl.loop(HALO, rows + HALO - 1)
+    def _(row):
+        row_sums(w, val, (out3,), (acc,), row)
+
+
+def merge(key, low, high):
+    low = jnp.where(jnp.logical_or(key == 4.0, key == 5.0), low, 0.0)
+    return jnp.where(key <= 1.0, high, low)
+
+
+def with_ends(key, tile, rows):
+    lanes = tile.shape[-1]
+    columns = end_columns(rows, HALO)
+    lane = lane_iota(tile.shape)
+    inside = jnp.logical_and(lane >= STRIDE * HALO, lane < STRIDE * (HALO + len(rows)))
+    low = jnp.where(jnp.logical_and(inside, key == 5.0), columns, tile)
+    return jnp.where(jnp.logical_and(inside, key == 0.0), roll(columns, -4), low)
 
 
 def second_half_kernel(
-    aux, v1, v1t, v2, v2t, tt, ma2, ru, rd, diag, diag_t, ic, ict, w, wt, kn, mut, inv, invt,
+    aux, v1, v1t, v2, v2t, tt, ma2, ru, rd, diag, diag_t, ic, ict, w, wt, kn, kst, inv, invt, out3,
     heat, press, press_t, su, sd, dt,
     val, val_t, out, out_t, acc, hot_t,
 ):
@@ -608,14 +686,8 @@
     step = COURANT / jnp.broadcast_to(best, (SUB, lanes))
     dt[...] = step
     step = jnp.concatenate([step] * (slots // SUB), 0)
-    for row in range(full):
-        if row < HALO:
-            val[0, row] = ru[row]
-        elif row < rows + HALO:
-            val[0, row] = v2[row - HALO]
-        else:
-            val[0, row] = rd[row - rows - HALO]
-    lane = lane_iota((slots, lanes))
+    extended(val, lambda row: v2[row], lambda n: ru[n] if n < HALO else rd[n - HALO])
+    lane, key = strip_place((slots, lanes))
     turn = STRIDE * rows
     for side in range(2):
         val_t[0, side] = jnp.where(
@@ -631,9 +703,31 @@
     for side in range(2):
         hot_t[side] = tt[side] + first * v1t[side] + second * v2t[side]
     for section in (3, 4):
-        spread_values(val, val_t)
-        partner_sums(w, wt, val, val_t, (out,), (out_t,), (acc,))
-        advance(val, val_t, out, out_t, diag, diag_t, ic, ict)
+        spread_rows(val)
+        spread_strips(val_t)
+        if section == 3:
+            for k in range(3):
+                for row in range(full):
+                    out[k, row] = out3[k, row]
+        else:
+            clear(out)
+        strip_sums(wt, val_t, (out_t,), (acc,))
+        if section == 3:
+
+            @pl.loop(0, 2 * HALO)
+            def _(n):
+                row = jnp.where(n < HALO, n, n + rows - 1)
+                row_sums(w, val, (out,), (acc,), jnp.minimum(row, full - 2))
+
+        else:
+
+            @pl.loop(HALO - 1, rows + HALO)
+            def _(row):
+                row_sums(w, val, (out,), (acc,), row)
+
+        reach = (1, full - 1) if section == 3 else (HALO, rows + HALO)
+        settle(out, out_t, *reach)
+        advance(val, val_t, out, out_t, diag, diag_t, ic, ict, *reach)
         power.append(power[-1] * step)
         factor = coef[section] * power[-1]
         for row in range(rows):
@@ -649,19 +743,19 @@
         press[2, row] = roll(tile, 1)
         fresh.append(tile)
     ends = [scale * hot_t[side] * invt[side] for side in range(2)]
-    press_t[0], press_t[1] = fill_strips(fresh, *ends, HALO)
+    merged = with_ends(key, merge(key, *ends), fresh)
+    press_t[...] = merged
     for ref, row in ((su, 0), (sd, rows - 1)):
         ref[0] = fresh[row]
         ref[1] = kn[0, 0, row]
-        for side in range(2):
-            ref[2 + side] = press_t[side]
-            ref[4 + side] = mut[side]
+        ref[2] = merged
+        ref[3] = kst[len(ALL), 4]
 
 
 NKICK = 9
 
 
-def kick_block(entries, own, far, step_y, s_ref, idx, acc):
+def kick_block(entries, own, far, step_y, s_of, acc):
     slots, lanes = own(0).shape
     groups = slots // SUB
     back = {}
@@ -680,7 +774,7 @@
                 how = duty(e, g, p)
                 if not how:
                     continue
-                s = s_ref[idx, p, e * groups + g]
+                s = s_of(p, e * groups + g)
                 s2 = s * s
                 drag = (s2 * s) * (i[4] * j[g][4])
                 push = (i[3] + j[g][3]) * (s2 * (i[5] * j[g][5]))
@@ -714,7 +808,9 @@
         return lambda e, k: feature(k, r + (1 if e >= NSAME else 0), MAIN[e])
 
     def one(entries, r):
-        back = kick_block(entries, lambda k: feature(k, r, 0), far(r), True, s, r + HALO, acc)
+        back = kick_block(
+            entries, lambda k: feature(k, r, 0), far(r), True, lambda p, n: s[r + HALO, p, n], acc
+        )
         for k in range(3):
             out[0, k, r] += gathered(acc.at[k]) - back[0, k]
             out[1, k, r] -= back[1, k]
@@ -732,7 +828,7 @@
 
 
 def kick_rim_kernel(
-    geo, aux, kn, press, ge, mvh, tside, mut, press_t, ru, rd, s, st, near, dt,
+    geo, aux, kn, press, ge, mvh, kst, press_t, ru, rd, s, st, near, dt,
     moved, mine, other, strip, out, out_t, acc,
 ):
     rows, slots, lanes = geo.shape[2:]
@@ -754,36 +850,36 @@
             mine[k, 1] = press[0, rows - 1] if k == 3 else kn[0, k - 4, rows - 1]
     lane = lane_iota((slots, lanes))
     turn = STRIDE * rows
-    for k in range(3, 5):
-        for side in range(2):
-            at = 2 + 2 * (k - 3) + side
-            tile = jnp.where(
-                lane < STRIDE * HALO,
-                roll(ru[at], -turn),
-                jnp.where(
-                    lane >= STRIDE * (rows + HALO),
-                    roll(rd[at], turn),
-                    (press_t, mut)[k - 3][side],
-                ),
-            )
-            strip[len(ALL), k - 3, side] = tile
-            for e in ALL:
-                strip[e, k - 3, side] = roll(tile, -STRIP_SHIFT[e])
-
-    @pl.loop(0, 2)
-    def _(side):
-        def feature(k, e):
-            if k < 3:
-                return tside.at[e, k, side]
-            return strip.at[e, k - 3, side] if k < 5 else tside.at[e, k - 2, side]
-
-        back = kick_block(
-            ALL, lambda k: feature(k, len(ALL)), lambda e, k: feature(k, e), False, st, side, acc
+    for k in range(2):
+        tile = jnp.where(
+            lane < STRIDE * HALO,
+            roll(ru[2 + k], -turn),
+            jnp.where(
+                lane >= STRIDE * (rows + HALO),
+                roll(rd[2 + k], turn),
+                press_t[...] if k == 0 else kst[len(ALL), 4],
+            ),
         )
-        for k in range(3):
-            out_t[0, k, side] = gathered(acc.at[k]) - back[0, k]
-            for e in ALL[1:]:
-                out_t[e, k, side] = back[e, k]
+        strip[len(ALL), k] = tile
+        for e in ALL:
+            strip[e, k] = roll(tile, -STRIP_SHIFT[e])
+    high = strip_place((SUB, lanes))[1] <= 1.0
+
+    def strip_feature(k, e):
+        return strip.at[e, k - 3] if k in (3, 4) else kst.at[e, k]
+
+    back = kick_block(
+        ALL,
+        lambda k: strip_feature(k, len(ALL)),
+        lambda e, k: strip_feature(k, e),
+        False,
+        lambda p, n: jnp.where(high, st[1, p, n], st[0, p, n]),
+        acc,
+    )
+    for k in range(3):
+        out_t[0, k] = gathered(acc.at[k]) - back[0, k]
+        for e in ALL[1:]:
+            out_t[e, k] = back[e, k]
 
     @pl.loop(0, 2)
     def _(n):
@@ -792,8 +888,7 @@
             lambda k: mine.at[k, n],
             lambda e, k: other.at[MAIN[e], k, n],
             True,
-            s,
-            1 + n * rows,
+            lambda p, m: s[1 + n * rows, p, m],
             acc,
         )
         for k in range(3):
@@ -802,28 +897,24 @@
                 out[MAIN[e], k, n] = -back[e, k]
 
     step = jnp.concatenate([dt[...]] * (slots // SUB), 0)
-    ends = {}
+    key = strip_place((slots, lanes))[1]
+    border = jnp.logical_or(lane == 0, lane == lanes - 1)
+    ends = []
     for k in range(3):
-        for side in range(2):
-            total = out_t[0, k, side]
-            for e in ALL[1:]:
-                total = total - roll(out_t[e, k, side], STRIP_SHIFT[e])
-            ends[k, side] = total
+        total = out_t[0, k]
+        for e in ALL[1:]:
+            total = total - roll(out_t[e, k], STRIP_SHIFT[e])
+        ends.append(jnp.where(key == 5.0, total, roll(total, 4)))
     for row in range(rows):
         live = aux[1, row] > 0.0
         factor = jnp.where(live, step / aux[2, row], 0.0)
-        at = STRIDE * (row + HALO)
         for k in range(3):
             parts = [near[variant, k, row] for variant in range(3)]
             if row == 0:
                 parts = [part + out[variant, k, 0] for variant, part in enumerate(parts)]
             if row == rows - 1:
                 parts[0] = parts[0] + out[3, k, 1]
-            edge = jnp.where(
-                lane == 0,
-                roll(ends[k, 0], -(at + 5)),
-                jnp.where(lane == lanes - 1, roll(ends[k, 1], lanes - 1 - at), 0.0),
-            )
+            edge = jnp.where(border, roll(ends[k], -(STRIDE * (row + HALO) + 5)), 0.0)
             total = (parts[0] + edge) + (roll(parts[1], 1) + roll(parts[2], -1))
             moved[k, pl.ds(row, slots, stride=rows), :] = aux[3 + k, row] + factor * total
 
@@ -889,46 +980,56 @@
     spare = [lax.ppermute(mx, "gy", ring("gy", k)) for k in range(4, lax.axis_size("gy") - 2, 3)]
     pairs = (full - 1, slots, npart * groups, SUB, lanes)
     strips = (2,) + pairs[1:]
-    columns = (NGEO + 4,) + tile
+    columns = ((NGEO + 3) // 2 + 1,) + tile
     two = (2,) + tile
     own = (rows,) + tile
     ext = (full,) + tile
     w, s, clp, crp = call(
-        near_kernel, (geo, aux), [pairs, pairs, (NGEO + 3,) + tile, (NGEO + 3,) + tile], name="near"
+        near_kernel,
+        (geo, aux),
+        [pairs, pairs, ((NGEO + 3) // 2,) + tile, ((NGEO + 3) // 2,) + tile],
+        name="near",
     )
     ge, th, ich, mvh, cl, cr, ma = call(
         pack_kernel,
         (geo, ru, rd, clp, crp, mx, *spare),
-        [(3, NGEO, 7) + tile, (4,) + tile, two, (4,) + two, columns, columns, tile],
+        [(3, NGEO, 6) + tile, (4,) + tile, two, (4,) + two, columns, columns, tile],
         name="pack",
     )
     rl, rr = swap(cl, cr, "gx")
     spare = [lax.ppermute(ma, "gx", ring("gx", k)) for k in range(2, lax.axis_size("gx") - 1)]
-    w, s = call(rim_kernel, (ge, w, s), [pairs, pairs], name="rim", aliases={1: 0, 2: 1})
     sums = (slots * SUB, lanes)
+    w, s, out1, bare1 = call(
+        rim_kernel,
+        (ge, w, s, aux, th),
+        [pairs, pairs, (3,) + ext, (3,) + ext],
+        [(3,) + ext, (2,) + sums],
+        name="rim",
+        aliases={1: 0, 2: 1},
+    )
     work = [(3,) + ext, (npart,) + two, (3,) + ext, (npart,) + two]
     wt, st, v1, v1t, v2, v2t, diag, diag_t, ic, ict, tside, tt, su, sd, ma2 = call(
         first_half_kernel,
-        (aux, th, ich, rl, rr, cl, cr, w, ma, *spare),
-        [strips, strips, own, two, own, two, ext, two, ext, two, (npart + 1, 7) + two, two]
+        (aux, th, ich, rl, rr, cl, cr, w, out1, bare1, ma, *spare),
+        [strips, strips, own, two, own, two, ext, two, ext, two, (7,) + two, two]
         + [(HALO + 3,) + tile] * 2
         + [tile],
-        [(npart + 1, NGEO) + two] + work + work[2:] + [(2,) + sums],
+        [(npart + 1, NGEO) + two] + work + [(npart,) + two, (3,) + ext, (2,) + sums],
         name="first_half",
     )
     ru, rd = swap(su, sd, "gy")
-    tside, kn, mut, inv, invt = call(
-        density_outer,
-        (tside, aux, mvh, ict, s, st),
-        [(npart + 1, 7) + two, (3, 5) + own, two, own, two],
+    kn, kst, inv, invt, out3 = call(
+        density_kernel,
+        (aux, mvh, ict, tside, s, st, v2, w),
+        [(3, 5) + own, (npart + 1, NKICK) + tile, own, two, (3,) + ext],
         work + [sums],
         name="density",
-        aliases={0: 0},
     )
     heat, press, press_t, su, sd, dt = call(
         second_half_kernel,
-        (aux, v1, v1t, v2, v2t, tt, ma2, ru, rd, diag, diag_t, ic, ict, w, wt, kn, mut, inv, invt),
-        [(slots * rows, lanes), (3,) + own, two, (6,) + tile, (6,) + tile, (SUB, lanes)],
+        (aux, v1, v1t, v2, v2t, tt, ma2, ru, rd, diag, diag_t, ic, ict, w, wt, kn, kst, inv, invt)
+        + (out3,),
+        [(slots * rows, lanes), (3,) + own, tile, (4,) + tile, (4,) + tile, (SUB, lanes)],
         work + [sums, two],
         name="second_half",
     )
@@ -943,18 +1044,13 @@
     )
     moved = call(
         kick_rim_kernel,
-        (geo, aux, kn, press, ge, mvh, tside, mut, press_t, ru, rd, s, st, near, dt),
+        (geo, aux, kn, press, ge, mvh, kst, press_t, ru, rd, s, st, near, dt),
         [(3, slots * rows, lanes)],
-        [(NKICK,) + two, (3, NKICK) + two, (npart + 1, 2) + two, (4, 3) + two, (npart, 3) + two]
+        [(NKICK,) + two, (3, NKICK) + two, (npart + 1, 2) + tile, (4, 3) + two, (npart, 3) + tile]
         + [(3,) + sums],
         name="kick_rim",
     )[0]
     return heated.reshape(temp.shape), moved.reshape(vel.shape)
-
-
-def density_outer(tside_in, aux, mvh, ict, s, st, tside, *rest):
-    del tside_in
-    density_kernel(aux, mvh, ict, tside, s, st, *rest)
 
 
 def solution(mesh):

time: 46.3 us -> 44 us (0.950)
  Pallas kernels: 28.5 us -> 27.2 us
  waiting for transfers between devices: 1.03 us -> 0.07 us
    pallas_call x8, Pallas kernels: 26.9 us -> 25.6 us  [call(): pl.pallas_call(kernel, in_specs=[VMEM_SPEC] * len(args), out_specs=[HBM_S...]
    ppermute x1, waiting for transfers between devices: 1 us -> 0.05 us  [body(): lax.ppermute(ma, 'gx', ring('gx', k))]
  transfers between devices with their start and end apart: 10 -> 10, of which waited for: 1 -> 0; matrix products, arithmetic and copies ran while one was open for 0% -> 0% of each run, Pallas kernels for 31% -> 36%
where the time goes in v2:
time: 44 us; the launch traced here: 43.8 us
  Pallas kernels  27.2 us (62%)
  starting transfers between devices  15.7 us (36%)
  between operations  0.75 us (2%)
    pallas_call x8, Pallas kernels, call(): pl.pallas_call(kernel, in_specs=[VMEM_SPEC] * len(args), out_specs=[HBM_S...  25.6 us
    ppermute x4, starting transfers between devices, swap(): from_upper = lax.ppermute(to_lower, axis, ring(axis, -1))  10.5 us
    ppermute x4, starting transfers between devices, swap(): from_lower = lax.ppermute(to_upper, axis, ring(axis, 1))  2.23 us
    ppermute x1, starting transfers between devices, body(): lax.ppermute(mx, 'gy', ring('gy', k))  2.21 us
    pallas_call x1, Pallas kernels, body(): pl.pallas_call(prep_kernel, in_specs=[HBM_SPEC] * len(inputs), out_specs=...  1.68 us
  transfers between devices with their start and end apart: 10, of which 0 were waited for; matrix products, arithmetic and copies ran while one was open for 0% of the time, Pallas kernels for 36%

profile of v2, /device:TPU:0, one launch (start us, length us, event | category | flops | bytes accessed | tf_op | source)
XLA Modules:
  0.0 43.8 jit_solution(6592930630994596280)
XLA Ops:
  0.6 1.7 %prep.1 = (f32[3,7,8,16,128]{4,3,2,1,0:T(8,128)S(1)}, f32[6,8,16,128]{3,2,1,0:T(8,128)S(1)}, f32[22,16,128]{2,1,0:T(8,128)S(1)}, f32[22,16,128]{2,1,0:T(8,128)S(1)}, f32[16,128]{1,0:T(8,128)S(1)}) custom-call(s32[8,128]{1,0:T(8,128)} %refs_0_.1, f32[3,128,128]{2,1,0:T(8,128)} %bitcast.9, f32[2,128,128]{2,1,0:T(8,128)} %bitcast.12, f32[128,128]{1,0:T(8,128)} %bitcast.13, ...), custom_call_target="tpu_custom_call" | custom-call | tf_op jit(solution)/shard_map/prep/pallas_call | solution.py:960
  2.3 0.5 %collective-permute-start = (f32[22,16,128]{2,1,0:T(8,128)S(1)}, f32[22,16,128]{2,1,0:T(8,128)S(1)}, u32[]{:S(2)}, u32[]{:S(2)}) collective-permute-start(f32[22,16,128]{2,1,0:T(8,128)S(1)} %get-tuple-element.52), channel_id=1, source_target_pairs={{0,1},{1,2},{2,3},{3,4},{4,5},{5,6},{6,7},{7,0},{8,9},{9,10},{10,1... | collective-permute-start | bytes 540680 | tf_op jit(solution)/shard_map/ppermute | solution.py:945
  2.9 2.9 %collective-permute-start.1 = (f32[22,16,128]{2,1,0:T(8,128)S(1)}, f32[22,16,128]{2,1,0:T(8,128)S(1)}, u32[]{:S(2)}, u32[]{:S(2)}) collective-permute-start(f32[22,16,128]{2,1,0:T(8,128)S(1)} %get-tuple-element.53), channel_id=1, source_target_pairs={{0,7},{1,0},{2,1},{3,2},{4,3},{5,4},{6,5},{7,6},{8,15},{9,8},{10,9... | collective-permute-start | bytes 540680 | tf_op jit(solution)/shard_map/ppermute | solution.py:946
  5.8 2.2 %collective-permute-start.2 = (f32[16,128]{1,0:T(8,128)S(1)}, f32[16,128]{1,0:T(8,128)S(1)}, u32[]{:S(2)}, u32[]{:S(2)}) collective-permute-start(f32[16,128]{1,0:T(8,128)S(1)} %get-tuple-element.56.mx), channel_id=1, source_target_pairs={{0,4},{1,5},{2,6},{3,7},{4,0},{5,1},{6,2},{7,3},{8,12},{9,13},{10,... | collective-permute-start | bytes 24584 | tf_op jit(solution)/shard_map/ppermute | solution.py:980
  8.0 4.6 %near.1 = (f32[11,16,10,8,128]{4,3,2,1,0:T(8,128)S(1)}, f32[11,16,10,8,128]{4,3,2,1,0:T(8,128)S(1)}, f32[5,16,128]{2,1,0:T(8,128)S(1)}, f32[5,16,128]{2,1,0:T(8,128)S(1)}) custom-call(f32[3,7,8,16,128]{4,3,2,1,0:T(8,128)S(1)} %get-tuple-element.50.geo, f32[6,8,16,128]{3,2,1,0:T(8,128)S(1)} %get-tuple-element.51.aux), custom_call_target="tpu_custom_call" | custom-call | tf_op jit(solution)/shard_map/near/pallas_call | solution.py:927
  12.6 0.0 collective-permute-done.2.rest_0_
  12.6 0.0 collective-permute-done.ru
  12.7 0.0 collective-permute-done.1.rd
  12.7 0.4 pack.1
  13.1 1.6 %collective-permute-start.3 = (f32[6,16,128]{2,1,0:T(8,128)S(1)}, f32[6,16,128]{2,1,0:T(8,128)S(1)}, u32[]{:S(2)}, u32[]{:S(2)}) collective-permute-start(f32[6,16,128]{2,1,0:T(8,128)S(1)} %get-tuple-element.60.cr), channel_id=1, source_target_pairs={{0,8},{8,16},{16,24},{24,0},{1,9},{9,17},{17,25},{25,1},{2,10},{10... | collective-permute-start | bytes 147464 | tf_op jit(solution)/shard_map/ppermute | solution.py:945
  14.7 2.2 %collective-permute-start.4 = (f32[6,16,128]{2,1,0:T(8,128)S(1)}, f32[6,16,128]{2,1,0:T(8,128)S(1)}, u32[]{:S(2)}, u32[]{:S(2)}) collective-permute-start(f32[6,16,128]{2,1,0:T(8,128)S(1)} %get-tuple-element.61.cl), channel_id=1, source_target_pairs={{0,24},{8,0},{16,8},{24,16},{1,25},{9,1},{17,9},{25,17},{2,26},{10... | collective-permute-start | bytes 147464 | tf_op jit(solution)/shard_map/ppermute | solution.py:946
  16.9 0.8 %collective-permute-start.5 = (f32[16,128]{1,0:T(8,128)S(1)}, f32[16,128]{1,0:T(8,128)S(1)}, u32[]{:S(2)}, u32[]{:S(2)}) collective-permute-start(f32[16,128]{1,0:T(8,128)S(1)} %get-tuple-element.68.rest_0_), channel_id=1, source_target_pairs={{0,16},{8,24},{16,0},{24,8},{1,17},{9,25},{17,1},{25,9},{2,18},{10... | collective-permute-start | bytes 24584 | tf_op jit(solution)/shard_map/ppermute | solution.py:1000
  17.7 3.7 %rim.1 = (f32[11,16,10,8,128]{4,3,2,1,0:T(8,128)S(1)}, f32[11,16,10,8,128]{4,3,2,1,0:T(8,128)S(1)}, f32[3,12,16,128]{3,2,1,0:T(8,128)S(1)}, f32[3,12,16,128]{3,2,1,0:T(8,128)S(1)}) custom-call(f32[3,7,6,16,128]{4,3,2,1,0:T(8,128)S(1)} %get-tuple-element.62.ge, ...), custom_call_target="tpu_custom_call", output_to_operand_aliasing={{0}: (1, {}), {1}: (2, {})} | custom-call | tf_op jit(solution)/shard_map/rim/pallas_call | solution.py:927
  21.4 0.0 collective-permute-done.5.rest_1_
  21.5 0.0 collective-permute-done.3.rl
  21.5 0.0 collective-permute-done.4.rr
  21.5 4.0 %first_half.1 = (f32[2,16,10,8,128]{4,3,2,1,0:T(8,128)S(1)}, f32[2,16,10,8,128]{4,3,2,1,0:T(8,128)S(1)}, f32[8,16,128]{2,1,0:T(8,128)S(1)}, f32[2,16,128]{2,1,0:...) custom-call(f32[6,8,16,128]{3,2,1,0:T(8,128)S(1)} %get-tuple-element, ...), custom_call_target="tpu_custom_call" | custom-call | tf_op jit(solution)/shard_map/first_half/pallas_call | solution.py:927
  25.5 0.0 collective-permute-start.6
  25.5 2.6 %collective-permute-start.7 = (f32[5,16,128]{2,1,0:T(8,128)S(1)}, f32[5,16,128]{2,1,0:T(8,128)S(1)}, u32[]{:S(2)}, u32[]{:S(2)}) collective-permute-start(f32[5,16,128]{2,1,0:T(8,128)S(1)} %get-tuple-element.81), channel_id=1, source_target_pairs={{0,7},{1,0},{2,1},{3,2},{4,3},{5,4},{6,5},{7,6},{8,15},{9,8},{10,9... | collective-permute-start | bytes 122888 | tf_op jit(solution)/shard_map/ppermute | solution.py:946
  28.1 2.8 %density.1 = (f32[3,5,8,16,128]{4,3,2,1,0:T(8,128)S(1)}, f32[6,9,16,128]{3,2,1,0:T(8,128)S(1)}, f32[8,16,128]{2,1,0:T(8,128)S(1)}, f32[2,16,128]{2,1,0:T(8,128)S(1)}, f32[3,12,16,128]{3,2,1,0:T(8,128)S(1)}) custom-call(f32[6,8,16,128]{3,2,1,0:T(8,128)S(1)} %get-tuple-element.51.aux, f32[4,2,16,128]{3,2,1,0:T(8,128)S(1)} %get-tuple-element.57.mvh, ...), custom_call_target="tpu_custom_call" | custom-call | tf_op jit(solution)/shard_map/density/pallas_call | solution.py:927
  30.9 0.0 collective-permute-done.6.ru
  30.9 0.0 collective-permute-done.7.rd
  30.9 2.7 %second_half.1 = (f32[128,128]{1,0:T(8,128)S(1)}, f32[3,8,16,128]{3,2,1,0:T(8,128)S(1)}, f32[16,128]{1,0:T(8,128)S(1)}, f32[4,16,128]{2,1,0:T(8,128)S(1)}, f32[4...) custom-call(f32[6,8,16,128]{3,2,1,0:T(8,128)S(1)} %get-tuple-element.51.aux, f32[8,16,128]{2,1,0:T(8,128)S(1)} %get-tuple-element.75.v1, ...), custom_call_target="tpu_custom_call" | custom-call | tf_op jit(solution)/shard_map/second_half/pallas_call | solution.py:927
  33.6 0.1 collective-permute-start.8
  33.7 2.6 %collective-permute-start.9 = (f32[4,16,128]{2,1,0:T(8,128)S(1)}, f32[4,16,128]{2,1,0:T(8,128)S(1)}, u32[]{:S(2)}, u32[]{:S(2)}) collective-permute-start(f32[4,16,128]{2,1,0:T(8,128)S(1)} %get-tuple-element.95), channel_id=1, source_target_pairs={{0,7},{1,0},{2,1},{3,2},{4,3},{5,4},{6,5},{7,6},{8,15},{9,8},{10,9... | collective-permute-start | bytes 98312 | tf_op jit(solution)/shard_map/ppermute | solution.py:946
  36.3 4.9 %kick_near.1 = (f32[3,3,8,16,128]{4,3,2,1,0:T(8,128)S(1)}, f32[128,128]{1,0:T(8,128)}) custom-call(f32[3,7,8,16,128]{4,3,2,1,0:T(8,128)S(1)} %get-tuple-element.50.geo, f32[3,5,8,16,128]{4,3,2,1,0:T(8,128)S(1)} %get-tuple-element.74.kn, f32[3,8,16,128]{3,2,1,0:T(8,128)S(1)} %get-tuple-element.90.press, f32[11,16,10,8,128]{4,3,2,1,0:T(8,128)S(1)} %get-tuple-element.71.s, ...), custom_call_target="tpu_custom_call" | custom-call | tf_op jit(solution)/shard_map/kick_near/pallas_call | solution.py:927
  41.2 0.0 collective-permute-done.8.ru
  41.2 0.0 collective-permute-done.9.rd
  41.2 2.5 %kick_rim.1 = f32[3,128,128]{2,1,0:T(8,128)} custom-call(f32[3,7,8,16,128]{4,3,2,1,0:T(8,128)S(1)} %get-tuple-element.50.geo, f32[6,8,16,128]{3,2,1,0:T(8,128)S(1)} %get-tuple-element.51.aux, f32[3,5,8,16,128]{4,3,2,1,0:T(8,128)S(1)} %get-tuple-element.74.kn, f32[3,8,16,128]{3,2,1,0:T(8,128)S(1)} %get-tuple-element.90.press, ...), custom_call_target="tpu_custom_call" | custom-call | tf_op jit(solution)/shard_map/kick_rim/pallas_call | solution.py:927
Async XLA Ops:
  2.3 10.3 %collective-permute-start = (f32[22,16,128]{2,1,0:T(8,128)S(1)}, f32[22,16,128]{2,1,0:T(8,128)S(1)}, u32[]{:S(2)}, u32[]{:S(2)}) collective-permute-start(f32[22,16,128]{2,1,0:T(8,128)S(1)} %get-tuple-element.52), channel_id=1, source_target_pairs={{0,1},{1,2},{2,3},{3,4},{4,5},{5,6},{6,7},{7,0},{8,9},{9,10},{10,1... | collective-permute-start | bytes 540680 | tf_op jit(solution)/shard_map/ppermute | solution.py:945
  2.9 9.8 %collective-permute-start.1 = (f32[22,16,128]{2,1,0:T(8,128)S(1)}, f32[22,16,128]{2,1,0:T(8,128)S(1)}, u32[]{:S(2)}, u32[]{:S(2)}) collective-permute-start(f32[22,16,128]{2,1,0:T(8,128)S(1)} %get-tuple-element.53), channel_id=1, source_target_pairs={{0,7},{1,0},{2,1},{3,2},{4,3},{5,4},{6,5},{7,6},{8,15},{9,8},{10,9... | collective-permute-start | bytes 540680 | tf_op jit(solution)/shard_map/ppermute | solution.py:946
  5.8 6.8 %collective-permute-start.2 = (f32[16,128]{1,0:T(8,128)S(1)}, f32[16,128]{1,0:T(8,128)S(1)}, u32[]{:S(2)}, u32[]{:S(2)}) collective-permute-start(f32[16,128]{1,0:T(8,128)S(1)} %get-tuple-element.56.mx), channel_id=1, source_target_pairs={{0,4},{1,5},{2,6},{3,7},{4,0},{5,1},{6,2},{7,3},{8,12},{9,13},{10,... | collective-permute-start | bytes 24584 | tf_op jit(solution)/shard_map/ppermute | solution.py:980
  13.1 8.4 %collective-permute-start.3 = (f32[6,16,128]{2,1,0:T(8,128)S(1)}, f32[6,16,128]{2,1,0:T(8,128)S(1)}, u32[]{:S(2)}, u32[]{:S(2)}) collective-permute-start(f32[6,16,128]{2,1,0:T(8,128)S(1)} %get-tuple-element.60.cr), channel_id=1, source_target_pairs={{0,8},{8,16},{16,24},{24,0},{1,9},{9,17},{17,25},{25,1},{2,10},{10... | collective-permute-start | bytes 147464 | tf_op jit(solution)/shard_map/ppermute | solution.py:945
  14.7 6.8 %collective-permute-start.4 = (f32[6,16,128]{2,1,0:T(8,128)S(1)}, f32[6,16,128]{2,1,0:T(8,128)S(1)}, u32[]{:S(2)}, u32[]{:S(2)}) collective-permute-start(f32[6,16,128]{2,1,0:T(8,128)S(1)} %get-tuple-element.61.cl), channel_id=1, source_target_pairs={{0,24},{8,0},{16,8},{24,16},{1,25},{9,1},{17,9},{25,17},{2,26},{10... | collective-permute-start | bytes 147464 | tf_op jit(solution)/shard_map/ppermute | solution.py:946
  16.9 4.5 %collective-permute-start.5 = (f32[16,128]{1,0:T(8,128)S(1)}, f32[16,128]{1,0:T(8,128)S(1)}, u32[]{:S(2)}, u32[]{:S(2)}) collective-permute-start(f32[16,128]{1,0:T(8,128)S(1)} %get-tuple-element.68.rest_0_), channel_id=1, source_target_pairs={{0,16},{8,24},{16,0},{24,8},{1,17},{9,25},{17,1},{25,9},{2,18},{10... | collective-permute-start | bytes 24584 | tf_op jit(solution)/shard_map/ppermute | solution.py:1000
  25.5 5.4 %collective-permute-start.6 = (f32[5,16,128]{2,1,0:T(8,128)S(1)}, f32[5,16,128]{2,1,0:T(8,128)S(1)}, u32[]{:S(2)}, u32[]{:S(2)}) collective-permute-start(f32[5,16,128]{2,1,0:T(8,128)S(1)} %get-tuple-element.80), channel_id=1, source_target_pairs={{0,1},{1,2},{2,3},{3,4},{4,5},{5,6},{6,7},{7,0},{8,9},{9,10},{10,1... | collective-permute-start | bytes 122888 | tf_op jit(solution)/shard_map/ppermute | solution.py:945
  25.5 5.4 %collective-permute-start.7 = (f32[5,16,128]{2,1,0:T(8,128)S(1)}, f32[5,16,128]{2,1,0:T(8,128)S(1)}, u32[]{:S(2)}, u32[]{:S(2)}) collective-permute-start(f32[5,16,128]{2,1,0:T(8,128)S(1)} %get-tuple-element.81), channel_id=1, source_target_pairs={{0,7},{1,0},{2,1},{3,2},{4,3},{5,4},{6,5},{7,6},{8,15},{9,8},{10,9... | collective-permute-start | bytes 122888 | tf_op jit(solution)/shard_map/ppermute | solution.py:946
  33.6 7.6 %collective-permute-start.8 = (f32[4,16,128]{2,1,0:T(8,128)S(1)}, f32[4,16,128]{2,1,0:T(8,128)S(1)}, u32[]{:S(2)}, u32[]{:S(2)}) collective-permute-start(f32[4,16,128]{2,1,0:T(8,128)S(1)} %get-tuple-element.94), channel_id=1, source_target_pairs={{0,1},{1,2},{2,3},{3,4},{4,5},{5,6},{6,7},{7,0},{8,9},{9,10},{10,1... | collective-permute-start | bytes 98312 | tf_op jit(solution)/shard_map/ppermute | solution.py:945
  33.7 7.5 %collective-permute-start.9 = (f32[4,16,128]{2,1,0:T(8,128)S(1)}, f32[4,16,128]{2,1,0:T(8,128)S(1)}, u32[]{:S(2)}, u32[]{:S(2)}) collective-permute-start(f32[4,16,128]{2,1,0:T(8,128)S(1)} %get-tuple-element.95), channel_id=1, source_target_pairs={{0,7},{1,0},{2,1},{3,2},{4,3},{5,4},{6,5},{7,6},{8,15},{9,8},{10,9... | collective-permute-start | bytes 98312 | tf_op jit(solution)/shard_map/ppermute | solution.py:946

commit v3 on v2

--- a/solution.py
+++ b/solution.py
@@ -85,9 +85,22 @@
     return jnp.where(s_neg, -sv, sv), jnp.where(c_neg, -cv, cv)
 
 
+def even_row():
+    return lax.axis_index("gy") % 2 == 0
+
+
+def send(sa, sb, even, k, to_lower, to_upper):
+    sa[k] = jnp.where(even, to_upper, to_lower)
+    sb[k] = jnp.where(even, to_lower, to_upper)
+
+
+def receive(ra, rb, even):
+    return (lambda k: jnp.where(even, rb[k], ra[k])), (lambda k: jnp.where(even, ra[k], rb[k]))
+
+
 def prep_kernel(*refs):
     n = 8
-    sources, (geo, aux, su, sd, mx), held, sems = refs[:n], refs[n : n + 5], refs[n + 5 : -1], refs[-1]
+    sources, (geo, aux, sa, sb, mx), held, sems = refs[:n], refs[n : n + 5], refs[n + 5 : -1], refs[-1]
     copies = [pltpu.make_async_copy(sources[k], held[k], sems.at[k]) for k in range(n)]
     for copy in copies:
         copy.start()
@@ -122,21 +135,21 @@
         side = [t, inv_cap, m] + v
         for k, tile in enumerate(side):
             aux[k, r] = tile
-        for ref, first, edge in ((su, 0, 0), (sd, rows - HALO, rows - 1)):
-            if first <= r < first + HALO:
-                for k, tile in enumerate(tiles + [t]):
-                    ref[k * HALO + r - first] = tile
-            if r == edge:
-                for k, tile in enumerate(side[1:]):
-                    ref[(NGEO + 1) * HALO + k] = tile
         bound = jnp.sqrt(HEAT_RATIO * (HEAT_RATIO - 1.0) * t) + jnp.sqrt(
             v[0] * v[0] + v[1] * v[1] + v[2] * v[2]
         )
         bound = jnp.where(live, bound, 0.0)
         best = bound if best is None else jnp.maximum(best, bound)
     mx[...] = best
-    su[(NGEO + 1) * HALO + 5] = best
-    sd[(NGEO + 1) * HALO + 5] = best
+    even = even_row()
+    for k in range(NGEO + 1):
+        for n in range(HALO):
+            r = rows - HALO + n
+            pair = (geo[0, k, n], geo[0, k, r]) if k < NGEO else (aux[0, n], aux[0, r])
+            send(sa, sb, even, k * HALO + n, *pair)
+    for k in range(5):
+        send(sa, sb, even, (NGEO + 1) * HALO + k, aux[1 + k, 0], aux[1 + k, rows - 1])
+    send(sa, sb, even, (NGEO + 1) * HALO + 5, best, best)
     for r in range(rows):
         for k in range(NGEO):
             geo[1, k, r], geo[2, k, r] = beside(geo[0, k, r], k)
@@ -239,7 +252,8 @@
     )
 
 
-def pack_kernel(geo, ru, rd, clp, crp, mx, *rest):
+def pack_kernel(geo, ra, rb, clp, crp, mx, *rest):
+    ru, rd = receive(ra, rb, even_row())
     spare, (ge, th, ich, mvh, cl, cr, ma) = rest[:-7], rest[-7:]
     rows, slots, lanes = geo.shape[2:]
     at_top = lax.axis_index("gy") == 0
@@ -248,11 +262,11 @@
     end = rows + HALO
 
     def feature(k, row):
-        tile = ru[k * HALO + row] if row < HALO else rd[k * HALO + row - end]
+        tile = ru(k * HALO + row) if row < HALO else rd(k * HALO + row - end)
         return jnp.where(at_top if row < HALO else at_end, FAR, tile) if k == 0 else tile
 
     def side(k, row):
-        tile = ru[base + k] if row < HALO else rd[base + k]
+        tile = ru(base + k) if row < HALO else rd(base + k)
         return jnp.where(at_top if row < HALO else at_end, 0.0, tile) if k == 0 else tile
 
     for k in range(NGEO):
@@ -279,7 +293,7 @@
         (0, 1, end, end + 1),
         (HALO - 1, end),
     )
-    best = jnp.maximum(jnp.maximum(ru[base + 5], rd[base + 5]), mx[...])
+    best = jnp.maximum(jnp.maximum(ru(base + 5), rd(base + 5)), mx[...])
     for ref in spare:
         best = jnp.maximum(best, ref[...])
     ma[...] = best
@@ -475,7 +489,7 @@
 
 def first_half_kernel(aux, th, ich, rl, rr, cl, cr, w, out1, bare1, *rest):
     spare, rest = rest[:-23], rest[-23:]
-    (wt, st, v1, v1t, v2, v2t, diag, diag_t, ic, ict, tside, tt, su, sd, ma2) = rest[:15]
+    (wt, st, v1, v1t, v2, v2t, diag, diag_t, ic, ict, tside, tt, sa, sb, ma2) = rest[:15]
     tgeo, val, val_t, out, out_t, bare_t, diag3, acc = rest[15:]
     rows = w.shape[0] + 1 - 2 * HALO
     slots, lanes = val.shape[2:]
@@ -593,9 +607,10 @@
         v2[row] = val[0, row + HALO]
     for side in range(2):
         v2t[side] = val_t[0, side]
-    for ref, start in ((su, HALO), (sd, rows)):
-        for n in range(HALO):
-            ref[n] = val[0, start + n]
+    even = even_row()
+    for n in range(HALO):
+        send(sa, sb, even, n, val[0, HALO + n], val[0, rows + n])
+    for ref in (sa, sb):
         for side in range(2):
             ref[HALO + side] = val_t[0, side]
         ref[HALO + 2] = best
@@ -674,26 +689,28 @@
 
 
 def second_half_kernel(
-    aux, v1, v1t, v2, v2t, tt, ma2, ru, rd, diag, diag_t, ic, ict, w, wt, kn, kst, inv, invt, out3,
-    heat, press, press_t, su, sd, dt,
+    aux, v1, v1t, v2, v2t, tt, ma2, ra, rb, diag, diag_t, ic, ict, w, wt, kn, kst, inv, invt, out3,
+    heat, press, press_t, sa, sb, dt,
     val, val_t, out, out_t, acc, hot_t,
 ):
     rows, slots, lanes = v1.shape
     full = rows + 2 * HALO
     coef = conduction_polynomial(SECTIONS)
-    best = jnp.maximum(jnp.maximum(ru[HALO + 2], rd[HALO + 2]), ma2[...])
+    even = even_row()
+    ru, rd = receive(ra, rb, even)
+    best = jnp.maximum(jnp.maximum(ra[HALO + 2], rb[HALO + 2]), ma2[...])
     best = jnp.max(jnp.max(best, axis=1, keepdims=True), axis=0, keepdims=True)
     step = COURANT / jnp.broadcast_to(best, (SUB, lanes))
     dt[...] = step
     step = jnp.concatenate([step] * (slots // SUB), 0)
-    extended(val, lambda row: v2[row], lambda n: ru[n] if n < HALO else rd[n - HALO])
+    extended(val, lambda row: v2[row], lambda n: ru(n) if n < HALO else rd(n - HALO))
     lane, key = strip_place((slots, lanes))
     turn = STRIDE * rows
     for side in range(2):
         val_t[0, side] = jnp.where(
             lane < STRIDE * HALO,
-            roll(ru[HALO + side], -turn),
-            jnp.where(lane >= STRIDE * (rows + HALO), roll(rd[HALO + side], turn), v2t[side]),
+            roll(ru(HALO + side), -turn),
+            jnp.where(lane >= STRIDE * (rows + HALO), roll(rd(HALO + side), turn), v2t[side]),
         )
     power = [step, step * step]
     first, second = coef[1] * power[0], coef[2] * power[1]
@@ -745,9 +762,9 @@
     ends = [scale * hot_t[side] * invt[side] for side in range(2)]
     merged = with_ends(key, merge(key, *ends), fresh)
     press_t[...] = merged
-    for ref, row in ((su, 0), (sd, rows - 1)):
-        ref[0] = fresh[row]
-        ref[1] = kn[0, 0, row]
+    send(sa, sb, even, 0, fresh[0], fresh[rows - 1])
+    send(sa, sb, even, 1, kn[0, 0, 0], kn[0, 0, rows - 1])
+    for ref in (sa, sb):
         ref[2] = merged
         ref[3] = kst[len(ALL), 4]
 
@@ -828,11 +845,12 @@
 
 
 def kick_rim_kernel(
-    geo, aux, kn, press, ge, mvh, kst, press_t, ru, rd, s, st, near, dt,
+    geo, aux, kn, press, ge, mvh, kst, press_t, ra, rb, s, st, near, dt,
     moved, mine, other, strip, out, out_t, acc,
 ):
     rows, slots, lanes = geo.shape[2:]
     nge = ge.shape[2]
+    ru, rd = receive(ra, rb, even_row())
     for k in range(NKICK):
         for variant in range(3):
             if k < 3:
@@ -840,23 +858,23 @@
                 other[variant, k, 1] = ge[variant, k, nge - 2]
             else:
                 other[variant, k, 0] = press[variant, 0] if k == 3 else kn[variant, k - 4, 0]
-                tile = rd[k - 3] if k < 5 else mvh[k - 5, 1]
+                tile = rd(k - 3) if k < 5 else mvh[k - 5, 1]
                 other[variant, k, 1] = roll(tile, (0, -1, 1)[variant])
         if k < 3:
             mine[k, 0] = ge[0, k, 1]
             mine[k, 1] = geo[0, k, rows - 1]
         else:
-            mine[k, 0] = ru[k - 3] if k < 5 else mvh[k - 5, 0]
+            mine[k, 0] = ru(k - 3) if k < 5 else mvh[k - 5, 0]
             mine[k, 1] = press[0, rows - 1] if k == 3 else kn[0, k - 4, rows - 1]
     lane = lane_iota((slots, lanes))
     turn = STRIDE * rows
     for k in range(2):
         tile = jnp.where(
             lane < STRIDE * HALO,
-            roll(ru[2 + k], -turn),
+            roll(ru(2 + k), -turn),
             jnp.where(
                 lane >= STRIDE * (rows + HALO),
-                roll(rd[2 + k], turn),
+                roll(rd(2 + k), turn),
                 press_t[...] if k == 0 else kst[len(ALL), 4],
             ),
         )
@@ -947,6 +965,13 @@
     return from_lower, from_upper
 
 
+def paired(sa, sb, axis):
+    n = lax.axis_size(axis)
+    ra = lax.ppermute(sa, axis, [(i, i ^ 1) for i in range(n)])
+    rb = lax.ppermute(sb, axis, [(i, (((i + 1) % n ^ 1) - 1) % n) for i in range(n)])
+    return ra, rb
+
+
 def body(pop, coord, tilt, mass, kappa, cap, temp, vel):
     slots, rows, lanes = temp.shape
     flat = lambda x: x.reshape(x.shape[:-3] + (slots * rows, lanes))
@@ -957,7 +982,7 @@
     nsend = (NGEO + 1) * HALO + 6
     inputs = (pop,) + tuple(flat(x) for x in (coord, tilt, mass, kappa, cap, temp, vel))
     inputs = [pltpu.with_memory_space_constraint(x, pltpu.HBM) for x in inputs]
-    geo, aux, su, sd, mx = pl.pallas_call(
+    geo, aux, sa, sb, mx = pl.pallas_call(
         prep_kernel,
         in_specs=[HBM_SPEC] * len(inputs),
         out_specs=[VMEM_SPEC] * 5,
@@ -976,7 +1001,7 @@
         compiler_params=pltpu.CompilerParams(vmem_limit_bytes=24 * 1024 * 1024),
         name="prep",
     )(*inputs)
-    ru, rd = swap(su, sd, "gy")
+    ra, rb = paired(sa, sb, "gy")
     spare = [lax.ppermute(mx, "gy", ring("gy", k)) for k in range(4, lax.axis_size("gy") - 2, 3)]
     pairs = (full - 1, slots, npart * groups, SUB, lanes)
     strips = (2,) + pairs[1:]
@@ -992,7 +1017,7 @@
     )
     ge, th, ich, mvh, cl, cr, ma = call(
         pack_kernel,
-        (geo, ru, rd, clp, crp, mx, *spare),
+        (geo, ra, rb, clp, crp, mx, *spare),
         [(3, NGEO, 6) + tile, (4,) + tile, two, (4,) + two, columns, columns, tile],
         name="pack",
     )
@@ -1008,7 +1033,7 @@
         aliases={1: 0, 2: 1},
     )
     work = [(3,) + ext, (npart,) + two, (3,) + ext, (npart,) + two]
-    wt, st, v1, v1t, v2, v2t, diag, diag_t, ic, ict, tside, tt, su, sd, ma2 = call(
+    wt, st, v1, v1t, v2, v2t, diag, diag_t, ic, ict, tside, tt, sa, sb, ma2 = call(
         first_half_kernel,
         (aux, th, ich, rl, rr, cl, cr, w, out1, bare1, ma, *spare),
         [strips, strips, own, two, own, two, ext, two, ext, two, (7,) + two, two]
@@ -1017,7 +1042,7 @@
         [(npart + 1, NGEO) + two] + work + [(npart,) + two, (3,) + ext, (2,) + sums],
         name="first_half",
     )
-    ru, rd = swap(su, sd, "gy")
+    ra, rb = paired(sa, sb, "gy")
     kn, kst, inv, invt, out3 = call(
         density_kernel,
         (aux, mvh, ict, tside, s, st, v2, w),
@@ -1025,15 +1050,15 @@
         work + [sums],
         name="density",
     )
-    heat, press, press_t, su, sd, dt = call(
+    heat, press, press_t, sa, sb, dt = call(
         second_half_kernel,
-        (aux, v1, v1t, v2, v2t, tt, ma2, ru, rd, diag, diag_t, ic, ict, w, wt, kn, kst, inv, invt)
+        (aux, v1, v1t, v2, v2t, tt, ma2, ra, rb, diag, diag_t, ic, ict, w, wt, kn, kst, inv, invt)
         + (out3,),
         [(slots * rows, lanes), (3,) + own, tile, (4,) + tile, (4,) + tile, (SUB, lanes)],
         work + [sums, two],
         name="second_half",
     )
-    ru, rd = swap(su, sd, "gy")
+    ra, rb = paired(sa, sb, "gy")
     near, heated = call(
         kick_near_kernel,
         (geo, kn, press, s, heat),
@@ -1044,7 +1069,7 @@
     )
     moved = call(
         kick_rim_kernel,
-        (geo, aux, kn, press, ge, mvh, kst, press_t, ru, rd, s, st, near, dt),
+        (geo, aux, kn, press, ge, mvh, kst, press_t, ra, rb, s, st, near, dt),
         [(3, slots * rows, lanes)],
         [(NKICK,) + two, (3, NKICK) + two, (npart + 1, 2) + tile, (4, 3) + two, (npart, 3) + tile]
         + [(3,) + sums],

time: 44 us -> 40.9 us (0.930)
  starting transfers between devices: 15.7 us -> 12.2 us
    ppermute x4 -> x1, starting transfers between devices: 10.5 us -> 2.25 us  [swap(): from_upper = lax.ppermute(to_lower, axis, ring(axis, -1))]
    ppermute x0 -> x6, starting transfers between devices: none -> 6.98 us  [the longest x3 6.33 us: paired(): lax.ppermute(sb, axis, [(i, (((i + 1) % n ^ 1) - 1) % n) for i in range(n)])]
    ppermute x1, starting transfers between devices: 2.21 us -> 0.51 us  [body(): lax.ppermute(mx, 'gy', ring('gy', k))]
    ppermute x4 -> x1, starting transfers between devices: 2.23 us -> 1.63 us  [swap(): from_lower = lax.ppermute(to_upper, axis, ring(axis, 1))]
  transfers between devices with their start and end apart: 10 -> 10, of which waited for: 0 -> 1; matrix products, arithmetic and copies ran while one was open for 0% -> 0% of each run, Pallas kernels for 36% -> 39%
where the time goes in v3:
time: 40.9 us; the launch traced here: 40.7 us
  Pallas kernels  27.3 us (67%)
  starting transfers between devices  12.2 us (30%)
  between operations  0.74 us (2%)
  waiting for transfers between devices  0.48 us (1%)
    pallas_call x8, Pallas kernels, call(): pl.pallas_call(kernel, in_specs=[VMEM_SPEC] * len(args), out_specs=[HBM_S...  25.6 us
    ppermute x3, starting transfers between devices, paired(): lax.ppermute(sb, axis, [(i, (((i + 1) % n ^ 1) - 1) % n) for i in range(n)])  6.33 us
    ppermute x1, starting transfers between devices, swap(): from_upper = lax.ppermute(to_lower, axis, ring(axis, -1))  2.25 us
    pallas_call x1, Pallas kernels, body(): pl.pallas_call(prep_kernel, in_specs=[HBM_SPEC] * len(inputs), out_specs=...  1.69 us
    ppermute x1, starting transfers between devices, swap(): from_lower = lax.ppermute(to_upper, axis, ring(axis, 1))  1.63 us
  transfers between devices with their start and end apart: 10, of which 1 were waited for; matrix products, arithmetic and copies ran while one was open for 0% of the time, Pallas kernels for 39%

profile of v3, /device:TPU:0, one launch (start us, length us, event | category | flops | bytes accessed | tf_op | source)
XLA Modules:
  0.0 40.7 jit_solution(577007343540709096)
XLA Ops:
  0.6 1.7 %prep.1 = (f32[3,7,8,16,128]{4,3,2,1,0:T(8,128)S(1)}, f32[6,8,16,128]{3,2,1,0:T(8,128)S(1)}, f32[22,16,128]{2,1,0:T(8,128)S(1)}, f32[22,16,128]{2,1,0:T(8,128)S(1)}, f32[16,128]{1,0:T(8,128)S(1)}) custom-call(s32[8,128]{1,0:T(8,128)} %refs_0_.1, f32[3,128,128]{2,1,0:T(8,128)} %bitcast.9, f32[2,128,128]{2,1,0:T(8,128)} %bitcast.12, f32[128,128]{1,0:T(8,128)} %bitcast.13, ...), custom_call_target="tpu_custom_call" | custom-call | tf_op jit(solution)/shard_map/prep/pallas_call | solution.py:985
  2.3 0.6 %collective-permute-start = (f32[22,16,128]{2,1,0:T(8,128)S(1)}, f32[22,16,128]{2,1,0:T(8,128)S(1)}, u32[]{:S(2)}, u32[]{:S(2)}) collective-permute-start(f32[22,16,128]{2,1,0:T(8,128)S(1)} %get-tuple-element.52), channel_id=1, source_target_pairs={{0,1},{1,0},{2,3},{3,2},{4,5},{5,4},{6,7},{7,6},{8,9},{9,8},{10,11... | collective-permute-start | bytes 540680 | tf_op jit(solution)/shard_map/ppermute | solution.py:970
  2.9 3.5 %collective-permute-start.1 = (f32[22,16,128]{2,1,0:T(8,128)S(1)}, f32[22,16,128]{2,1,0:T(8,128)S(1)}, u32[]{:S(2)}, u32[]{:S(2)}) collective-permute-start(f32[22,16,128]{2,1,0:T(8,128)S(1)} %get-tuple-element.53), channel_id=1, source_target_pairs={{0,7},{1,2},{2,1},{3,4},{4,3},{5,6},{6,5},{7,0},{8,15},{9,10},{10,... | collective-permute-start | bytes 540680 | tf_op jit(solution)/shard_map/ppermute | solution.py:971
  6.4 0.5 %collective-permute-start.2 = (f32[16,128]{1,0:T(8,128)S(1)}, f32[16,128]{1,0:T(8,128)S(1)}, u32[]{:S(2)}, u32[]{:S(2)}) collective-permute-start(f32[16,128]{1,0:T(8,128)S(1)} %get-tuple-element.56.mx), channel_id=1, source_target_pairs={{0,4},{1,5},{2,6},{3,7},{4,0},{5,1},{6,2},{7,3},{8,12},{9,13},{10,... | collective-permute-start | bytes 24584 | tf_op jit(solution)/shard_map/ppermute | solution.py:1005
  6.9 4.6 %near.1 = (f32[11,16,10,8,128]{4,3,2,1,0:T(8,128)S(1)}, f32[11,16,10,8,128]{4,3,2,1,0:T(8,128)S(1)}, f32[5,16,128]{2,1,0:T(8,128)S(1)}, f32[5,16,128]{2,1,0:T(8,128)S(1)}) custom-call(f32[3,7,8,16,128]{4,3,2,1,0:T(8,128)S(1)} %get-tuple-element.50.geo, f32[6,8,16,128]{3,2,1,0:T(8,128)S(1)} %get-tuple-element.51.aux), custom_call_target="tpu_custom_call" | custom-call | tf_op jit(solution)/shard_map/near/pallas_call | solution.py:945
  11.6 0.0 collective-permute-done.2.rest_0_
  11.6 0.0 collective-permute-done.ra
  11.6 0.0 collective-permute-done.1.rb
  11.6 0.4 pack.1
  12.0 1.6 %collective-permute-start.3 = (f32[6,16,128]{2,1,0:T(8,128)S(1)}, f32[6,16,128]{2,1,0:T(8,128)S(1)}, u32[]{:S(2)}, u32[]{:S(2)}) collective-permute-start(f32[6,16,128]{2,1,0:T(8,128)S(1)} %get-tuple-element.60.cr), channel_id=1, source_target_pairs={{0,8},{8,16},{16,24},{24,0},{1,9},{9,17},{17,25},{25,1},{2,10},{10... | collective-permute-start | bytes 147464 | tf_op jit(solution)/shard_map/ppermute | solution.py:963
  13.6 2.2 %collective-permute-start.4 = (f32[6,16,128]{2,1,0:T(8,128)S(1)}, f32[6,16,128]{2,1,0:T(8,128)S(1)}, u32[]{:S(2)}, u32[]{:S(2)}) collective-permute-start(f32[6,16,128]{2,1,0:T(8,128)S(1)} %get-tuple-element.61.cl), channel_id=1, source_target_pairs={{0,24},{8,0},{16,8},{24,16},{1,25},{9,1},{17,9},{25,17},{2,26},{10... | collective-permute-start | bytes 147464 | tf_op jit(solution)/shard_map/ppermute | solution.py:964
  15.9 0.8 %collective-permute-start.5 = (f32[16,128]{1,0:T(8,128)S(1)}, f32[16,128]{1,0:T(8,128)S(1)}, u32[]{:S(2)}, u32[]{:S(2)}) collective-permute-start(f32[16,128]{1,0:T(8,128)S(1)} %get-tuple-element.68.rest_0_), channel_id=1, source_target_pairs={{0,16},{8,24},{16,0},{24,8},{1,17},{9,25},{17,1},{25,9},{2,18},{10... | collective-permute-start | bytes 24584 | tf_op jit(solution)/shard_map/ppermute | solution.py:1025
  16.7 3.7 %rim.1 = (f32[11,16,10,8,128]{4,3,2,1,0:T(8,128)S(1)}, f32[11,16,10,8,128]{4,3,2,1,0:T(8,128)S(1)}, f32[3,12,16,128]{3,2,1,0:T(8,128)S(1)}, f32[3,12,16,128]{3,2,1,0:T(8,128)S(1)}) custom-call(f32[3,7,6,16,128]{4,3,2,1,0:T(8,128)S(1)} %get-tuple-element.62.ge, ...), custom_call_target="tpu_custom_call", output_to_operand_aliasing={{0}: (1, {}), {1}: (2, {})} | custom-call | tf_op jit(solution)/shard_map/rim/pallas_call | solution.py:945
  20.4 0.0 collective-permute-done.5.rest_1_
  20.4 0.0 collective-permute-done.3.rl
  20.4 0.0 collective-permute-done.4.rr
  20.4 4.0 %first_half.1 = (f32[2,16,10,8,128]{4,3,2,1,0:T(8,128)S(1)}, f32[2,16,10,8,128]{4,3,2,1,0:T(8,128)S(1)}, f32[8,16,128]{2,1,0:T(8,128)S(1)}, f32[2,16,128]{2,1,0:...) custom-call(f32[6,8,16,128]{3,2,1,0:T(8,128)S(1)} %get-tuple-element, ...), custom_call_target="tpu_custom_call" | custom-call | tf_op jit(solution)/shard_map/first_half/pallas_call | solution.py:945
  24.4 0.0 collective-permute-start.6
  24.5 1.2 %collective-permute-start.7 = (f32[5,16,128]{2,1,0:T(8,128)S(1)}, f32[5,16,128]{2,1,0:T(8,128)S(1)}, u32[]{:S(2)}, u32[]{:S(2)}) collective-permute-start(f32[5,16,128]{2,1,0:T(8,128)S(1)} %get-tuple-element.81), channel_id=1, source_target_pairs={{0,7},{1,2},{2,1},{3,4},{4,3},{5,6},{6,5},{7,0},{8,15},{9,10},{10,... | collective-permute-start | bytes 122888 | tf_op jit(solution)/shard_map/ppermute | solution.py:971
  25.6 2.8 %density.1 = (f32[3,5,8,16,128]{4,3,2,1,0:T(8,128)S(1)}, f32[6,9,16,128]{3,2,1,0:T(8,128)S(1)}, f32[8,16,128]{2,1,0:T(8,128)S(1)}, f32[2,16,128]{2,1,0:T(8,128)S(1)}, f32[3,12,16,128]{3,2,1,0:T(8,128)S(1)}) custom-call(f32[6,8,16,128]{3,2,1,0:T(8,128)S(1)} %get-tuple-element.51.aux, f32[4,2,16,128]{3,2,1,0:T(8,128)S(1)} %get-tuple-element.57.mvh, ...), custom_call_target="tpu_custom_call" | custom-call | tf_op jit(solution)/shard_map/density/pallas_call | solution.py:945
  28.4 0.0 collective-permute-done.6.ra
  28.4 0.4 %collective-permute-done.7.rb = f32[5,16,128]{2,1,0:T(8,128)S(1)} collective-permute-done((f32[5,16,128]{2,1,0:T(8,128)S(1)}, f32[5,16,128]{2,1,0:T(8,128)S(1)}, u32[]{:S(2)}, u32[]{:S(2)}) %collective-permute-start.7) | collective-permute-done | bytes 40992 | tf_op jit(solution)/shard_map/ppermute | solution.py:971
  28.8 2.7 %second_half.1 = (f32[128,128]{1,0:T(8,128)S(1)}, f32[3,8,16,128]{3,2,1,0:T(8,128)S(1)}, f32[16,128]{1,0:T(8,128)S(1)}, f32[4,16,128]{2,1,0:T(8,128)S(1)}, f32[4...) custom-call(f32[6,8,16,128]{3,2,1,0:T(8,128)S(1)} %get-tuple-element.51.aux, f32[8,16,128]{2,1,0:T(8,128)S(1)} %get-tuple-element.75.v1, ...), custom_call_target="tpu_custom_call" | custom-call | tf_op jit(solution)/shard_map/second_half/pallas_call | solution.py:945
  31.5 0.1 collective-permute-start.8
  31.6 1.6 %collective-permute-start.9 = (f32[4,16,128]{2,1,0:T(8,128)S(1)}, f32[4,16,128]{2,1,0:T(8,128)S(1)}, u32[]{:S(2)}, u32[]{:S(2)}) collective-permute-start(f32[4,16,128]{2,1,0:T(8,128)S(1)} %get-tuple-element.95), channel_id=1, source_target_pairs={{0,7},{1,2},{2,1},{3,4},{4,3},{5,6},{6,5},{7,0},{8,15},{9,10},{10,... | collective-permute-start | bytes 98312 | tf_op jit(solution)/shard_map/ppermute | solution.py:971
  33.2 4.9 %kick_near.1 = (f32[3,3,8,16,128]{4,3,2,1,0:T(8,128)S(1)}, f32[128,128]{1,0:T(8,128)}) custom-call(f32[3,7,8,16,128]{4,3,2,1,0:T(8,128)S(1)} %get-tuple-element.50.geo, f32[3,5,8,16,128]{4,3,2,1,0:T(8,128)S(1)} %get-tuple-element.74.kn, f32[3,8,16,128]{3,2,1,0:T(8,128)S(1)} %get-tuple-element.90.press, f32[11,16,10,8,128]{4,3,2,1,0:T(8,128)S(1)} %get-tuple-element.71.s, ...), custom_call_target="tpu_custom_call" | custom-call | tf_op jit(solution)/shard_map/kick_near/pallas_call | solution.py:945
  38.1 0.0 collective-permute-done.8.ra
  38.1 0.0 collective-permute-done.9.rb
  38.1 2.6 %kick_rim.1 = f32[3,128,128]{2,1,0:T(8,128)} custom-call(f32[3,7,8,16,128]{4,3,2,1,0:T(8,128)S(1)} %get-tuple-element.50.geo, f32[6,8,16,128]{3,2,1,0:T(8,128)S(1)} %get-tuple-element.51.aux, f32[3,5,8,16,128]{4,3,2,1,0:T(8,128)S(1)} %get-tuple-element.74.kn, f32[3,8,16,128]{3,2,1,0:T(8,128)S(1)} %get-tuple-element.90.press, ...), custom_call_target="tpu_custom_call" | custom-call | tf_op jit(solution)/shard_map/kick_rim/pallas_call | solution.py:945
Async XLA Ops:
  2.3 9.2 %collective-permute-start = (f32[22,16,128]{2,1,0:T(8,128)S(1)}, f32[22,16,128]{2,1,0:T(8,128)S(1)}, u32[]{:S(2)}, u32[]{:S(2)}) collective-permute-start(f32[22,16,128]{2,1,0:T(8,128)S(1)} %get-tuple-element.52), channel_id=1, source_target_pairs={{0,1},{1,0},{2,3},{3,2},{4,5},{5,4},{6,7},{7,6},{8,9},{9,8},{10,11... | collective-permute-start | bytes 540680 | tf_op jit(solution)/shard_map/ppermute | solution.py:970
  2.9 8.7 %collective-permute-start.1 = (f32[22,16,128]{2,1,0:T(8,128)S(1)}, f32[22,16,128]{2,1,0:T(8,128)S(1)}, u32[]{:S(2)}, u32[]{:S(2)}) collective-permute-start(f32[22,16,128]{2,1,0:T(8,128)S(1)} %get-tuple-element.53), channel_id=1, source_target_pairs={{0,7},{1,2},{2,1},{3,4},{4,3},{5,6},{6,5},{7,0},{8,15},{9,10},{10,... | collective-permute-start | bytes 540680 | tf_op jit(solution)/shard_map/ppermute | solution.py:971
  6.4 5.1 %collective-permute-start.2 = (f32[16,128]{1,0:T(8,128)S(1)}, f32[16,128]{1,0:T(8,128)S(1)}, u32[]{:S(2)}, u32[]{:S(2)}) collective-permute-start(f32[16,128]{1,0:T(8,128)S(1)} %get-tuple-element.56.mx), channel_id=1, source_target_pairs={{0,4},{1,5},{2,6},{3,7},{4,0},{5,1},{6,2},{7,3},{8,12},{9,13},{10,... | collective-permute-start | bytes 24584 | tf_op jit(solution)/shard_map/ppermute | solution.py:1005
  12.0 8.4 %collective-permute-start.3 = (f32[6,16,128]{2,1,0:T(8,128)S(1)}, f32[6,16,128]{2,1,0:T(8,128)S(1)}, u32[]{:S(2)}, u32[]{:S(2)}) collective-permute-start(f32[6,16,128]{2,1,0:T(8,128)S(1)} %get-tuple-element.60.cr), channel_id=1, source_target_pairs={{0,8},{8,16},{16,24},{24,0},{1,9},{9,17},{17,25},{25,1},{2,10},{10... | collective-permute-start | bytes 147464 | tf_op jit(solution)/shard_map/ppermute | solution.py:963
  13.6 6.8 %collective-permute-start.4 = (f32[6,16,128]{2,1,0:T(8,128)S(1)}, f32[6,16,128]{2,1,0:T(8,128)S(1)}, u32[]{:S(2)}, u32[]{:S(2)}) collective-permute-start(f32[6,16,128]{2,1,0:T(8,128)S(1)} %get-tuple-element.61.cl), channel_id=1, source_target_pairs={{0,24},{8,0},{16,8},{24,16},{1,25},{9,1},{17,9},{25,17},{2,26},{10... | collective-permute-start | bytes 147464 | tf_op jit(solution)/shard_map/ppermute | solution.py:964
  15.9 4.5 %collective-permute-start.5 = (f32[16,128]{1,0:T(8,128)S(1)}, f32[16,128]{1,0:T(8,128)S(1)}, u32[]{:S(2)}, u32[]{:S(2)}) collective-permute-start(f32[16,128]{1,0:T(8,128)S(1)} %get-tuple-element.68.rest_0_), channel_id=1, source_target_pairs={{0,16},{8,24},{16,0},{24,8},{1,17},{9,25},{17,1},{25,9},{2,18},{10... | collective-permute-start | bytes 24584 | tf_op jit(solution)/shard_map/ppermute | solution.py:1025
  24.4 4.0 %collective-permute-start.6 = (f32[5,16,128]{2,1,0:T(8,128)S(1)}, f32[5,16,128]{2,1,0:T(8,128)S(1)}, u32[]{:S(2)}, u32[]{:S(2)}) collective-permute-start(f32[5,16,128]{2,1,0:T(8,128)S(1)} %get-tuple-element.80), channel_id=1, source_target_pairs={{0,1},{1,0},{2,3},{3,2},{4,5},{5,4},{6,7},{7,6},{8,9},{9,8},{10,11... | collective-permute-start | bytes 122888 | tf_op jit(solution)/shard_map/ppermute | solution.py:970
  24.5 4.4 %collective-permute-start.7 = (f32[5,16,128]{2,1,0:T(8,128)S(1)}, f32[5,16,128]{2,1,0:T(8,128)S(1)}, u32[]{:S(2)}, u32[]{:S(2)}) collective-permute-start(f32[5,16,128]{2,1,0:T(8,128)S(1)} %get-tuple-element.81), channel_id=1, source_target_pairs={{0,7},{1,2},{2,1},{3,4},{4,3},{5,6},{6,5},{7,0},{8,15},{9,10},{10,... | collective-permute-start | bytes 122888 | tf_op jit(solution)/shard_map/ppermute | solution.py:971
  31.5 6.5 %collective-permute-start.8 = (f32[4,16,128]{2,1,0:T(8,128)S(1)}, f32[4,16,128]{2,1,0:T(8,128)S(1)}, u32[]{:S(2)}, u32[]{:S(2)}) collective-permute-start(f32[4,16,128]{2,1,0:T(8,128)S(1)} %get-tuple-element.94), channel_id=1, source_target_pairs={{0,1},{1,0},{2,3},{3,2},{4,5},{5,4},{6,7},{7,6},{8,9},{9,8},{10,11... | collective-permute-start | bytes 98312 | tf_op jit(solution)/shard_map/ppermute | solution.py:970
  31.6 6.5 %collective-permute-start.9 = (f32[4,16,128]{2,1,0:T(8,128)S(1)}, f32[4,16,128]{2,1,0:T(8,128)S(1)}, u32[]{:S(2)}, u32[]{:S(2)}) collective-permute-start(f32[4,16,128]{2,1,0:T(8,128)S(1)} %get-tuple-element.95), channel_id=1, source_target_pairs={{0,7},{1,2},{2,1},{3,4},{4,3},{5,6},{6,5},{7,0},{8,15},{9,10},{10,... | collective-permute-start | bytes 98312 | tf_op jit(solution)/shard_map/ppermute | solution.py:971

commit v4 on v3

--- a/solution.py
+++ b/solution.py
@@ -102,21 +102,31 @@
     n = 8
     sources, (geo, aux, sa, sb, mx), held, sems = refs[:n], refs[n : n + 5], refs[n + 5 : -1], refs[-1]
     copies = [pltpu.make_async_copy(sources[k], held[k], sems.at[k]) for k in range(n)]
+    early = copies[2]
+    early.start()
     for copy in copies:
-        copy.start()
-    for copy in copies:
-        copy.wait()
+        if copy is not early:
+            copy.start()
     pop, coord, tilt, mass, kappa, cap, temp, vel = held
     rows, slots, lanes = geo.shape[2:]
+    early.wait()
+    half = math.sqrt(0.5)
+    for r in range(rows):
+        pick = (pl.ds(r, slots, stride=rows), slice(None))
+        st, ct = sincos(tilt[(0,) + pick])
+        sp, cp = sincos(tilt[(1,) + pick])
+        st = st * half
+        for k, tile in enumerate((st * cp, st * sp, ct * half)):
+            geo[0, 4 + k, r] = tile
+            geo[1, 4 + k, r], geo[2, 4 + k, r] = beside(tile, 4 + k)
+    for copy in copies:
+        if copy is not early:
+            copy.wait()
     slot = lax.broadcasted_iota(jnp.int32, (slots, lanes), 0)
     best = None
     for r in range(rows):
         pick = (pl.ds(r, slots, stride=rows), slice(None))
         live = slot < pop[r : r + 1, :]
-        st, ct = sincos(tilt[(0,) + pick])
-        sp, cp = sincos(tilt[(1,) + pick])
-        half = math.sqrt(0.5)
-        st = st * half
         t = temp[pick]
         v = [vel[(k,) + pick] for k in range(3)]
         tiles = [
@@ -124,12 +134,10 @@
             coord[(1,) + pick],
             coord[(2,) + pick],
             0.5 * kappa[pick],
-            st * cp,
-            st * sp,
-            ct * half,
         ]
         for k, tile in enumerate(tiles):
             geo[0, k, r] = tile
+            geo[1, k, r], geo[2, k, r] = beside(tile, k)
         inv_cap = jnp.where(live, 1.0 / cap[pick], 0.0)
         m = mass[pick]
         side = [t, inv_cap, m] + v
@@ -150,9 +158,6 @@
     for k in range(5):
         send(sa, sb, even, (NGEO + 1) * HALO + k, aux[1 + k, 0], aux[1 + k, rows - 1])
     send(sa, sb, even, (NGEO + 1) * HALO + 5, best, best)
-    for r in range(rows):
-        for k in range(NGEO):
-            geo[1, k, r], geo[2, k, r] = beside(geo[0, k, r], k)
 
 
 def beside(tile, k):
@@ -617,7 +622,7 @@
 
 
 def density_kernel(
-    aux, mvh, ict, tside, s, st, v2, w, kn, kst, inv, invt, out3, val, val_t, out, out_t, acc
+    aux, mvh, ict, tside, s, st, v2, w, kn, kst, inv, invt, out3, qm, qd, val, val_t, out, out_t, acc
 ):
     rows = aux.shape[1]
     slots, lanes = val.shape[2:]
@@ -672,6 +677,28 @@
     @pl.loop(HALO, rows + HALO - 1)
     def _(row):
         row_sums(w, val, (out3,), (acc,), row)
+
+    def factors(entries, r):
+        for e in entries:
+            for g in range(slots // SUB):
+                far = [
+                    kn[MAIN[e], k, r + (1 if e >= NSAME else 0), g * SUB : (g + 1) * SUB, :]
+                    for k in range(2)
+                ]
+                for p in range(slots):
+                    if not duty(e, g, p):
+                        continue
+                    n = e * (slots // SUB) + g
+                    one = s[r + HALO, p, n]
+                    two = one * one
+                    qd[r, p, n] = (two * one) * (spread(kn.at[0, 0, r], p, lanes) * far[0])
+                    qm[r, p, n] = two * (spread(kn.at[0, 1, r], p, lanes) * far[1])
+
+    @pl.loop(0, rows - 1)
+    def _(r):
+        factors(ALL, r)
+
+    factors(ALL[:NSAME], rows - 1)
 
 
 def merge(key, low, high):
@@ -772,7 +799,7 @@
 NKICK = 9
 
 
-def kick_block(entries, own, far, step_y, s_of, acc):
+def kick_block(entries, own, far, step_y, s_of, acc, ready=False):
     slots, lanes = own(0).shape
     groups = slots // SUB
     back = {}
@@ -791,10 +818,14 @@
                 how = duty(e, g, p)
                 if not how:
                     continue
-                s = s_of(p, e * groups + g)
-                s2 = s * s
-                drag = (s2 * s) * (i[4] * j[g][4])
-                push = (i[3] + j[g][3]) * (s2 * (i[5] * j[g][5]))
+                if ready:
+                    both, drag = s_of(p, e * groups + g)
+                else:
+                    s = s_of(p, e * groups + g)
+                    s2 = s * s
+                    drag = (s2 * s) * (i[4] * j[g][4])
+                    both = s2 * (i[5] * j[g][5])
+                push = (i[3] + j[g][3]) * both
                 for k in range(3):
                     term = push * (i[k] - j[g][k]) + drag * (j[g][6 + k] - i[6 + k])
                     mine[k] = term if mine[k] is None else mine[k] + term
@@ -808,7 +839,7 @@
     return back
 
 
-def kick_near_kernel(geo, kn, press, s, heat, out, heated, acc, sem):
+def kick_near_kernel(geo, kn, press, qm, qd, heat, out, heated, acc, sem):
     copy = pltpu.make_async_copy(heat, heated, sem)
     copy.start()
     rows, slots, lanes = geo.shape[2:]
@@ -826,7 +857,13 @@
 
     def one(entries, r):
         back = kick_block(
-            entries, lambda k: feature(k, r, 0), far(r), True, lambda p, n: s[r + HALO, p, n], acc
+            entries,
+            lambda k: feature(k, r, 0),
+            far(r),
+            True,
+            lambda p, n: (qm[r, p, n], qd[r, p, n]),
+            acc,
+            ready=True,
         )
         for k in range(3):
             out[0, k, r] += gathered(acc.at[k]) - back[0, k]
@@ -886,8 +923,9 @@
     def strip_feature(k, e):
         return strip.at[e, k - 3] if k in (3, 4) else kst.at[e, k]
 
+    crossing = tuple(e for e in ALL if STEP_X[e])
     back = kick_block(
-        ALL,
+        crossing,
         lambda k: strip_feature(k, len(ALL)),
         lambda e, k: strip_feature(k, e),
         False,
@@ -895,8 +933,8 @@
         acc,
     )
     for k in range(3):
-        out_t[0, k] = gathered(acc.at[k]) - back[0, k]
-        for e in ALL[1:]:
+        out_t[0, k] = gathered(acc.at[k])
+        for e in crossing:
             out_t[e, k] = back[e, k]
 
     @pl.loop(0, 2)
@@ -920,7 +958,7 @@
     ends = []
     for k in range(3):
         total = out_t[0, k]
-        for e in ALL[1:]:
+        for e in crossing:
             total = total - roll(out_t[e, k], STRIP_SHIFT[e])
         ends.append(jnp.where(key == 5.0, total, roll(total, 4)))
     for row in range(rows):
@@ -941,7 +979,7 @@
 HBM_SPEC = pl.BlockSpec(memory_space=pltpu.HBM)
 
 
-def call(kernel, args, outs, scratch=(), name=None, limit=24, aliases=None, far_out=()):
+def call(kernel, args, outs, scratch=(), name=None, limit=6, aliases=None, far_out=()):
     return pl.pallas_call(
         kernel,
         in_specs=[VMEM_SPEC] * len(args),
@@ -998,7 +1036,7 @@
         ],
         scratch_shapes=[pltpu.VMEM(x.shape, x.dtype) for x in inputs]
         + [pltpu.SemaphoreType.DMA((len(inputs),))],
-        compiler_params=pltpu.CompilerParams(vmem_limit_bytes=24 * 1024 * 1024),
+        compiler_params=pltpu.CompilerParams(vmem_limit_bytes=6 * 1024 * 1024),
         name="prep",
     )(*inputs)
     ra, rb = paired(sa, sb, "gy")
@@ -1043,10 +1081,11 @@
         name="first_half",
     )
     ra, rb = paired(sa, sb, "gy")
-    kn, kst, inv, invt, out3 = call(
+    kn, kst, inv, invt, out3, qm, qd = call(
         density_kernel,
         (aux, mvh, ict, tside, s, st, v2, w),
-        [(3, 5) + own, (npart + 1, NKICK) + tile, own, two, (3,) + ext],
+        [(3, 5) + own, (npart + 1, NKICK) + tile, own, two, (3,) + ext]
+        + [(rows,) + pairs[1:]] * 2,
         work + [sums],
         name="density",
     )
@@ -1061,7 +1100,7 @@
     ra, rb = paired(sa, sb, "gy")
     near, heated = call(
         kick_near_kernel,
-        (geo, kn, press, s, heat),
+        (geo, kn, press, qm, qd, heat),
         [(3, 3) + own, (slots * rows, lanes)],
         [(3,) + sums, pltpu.SemaphoreType.DMA(())],
         name="kick_near",

time: 40.9 us -> 40.6 us (level)
  waiting for transfers between devices: 0.48 us -> 0.07 us
    ppermute x3, waiting for transfers between devices: 0.42 us -> 0.01 us  [paired(): lax.ppermute(sb, axis, [(i, (((i + 1) % n ^ 1) - 1) % n) for i in range(n)])]
  transfers between devices with their start and end apart: 10 -> 10, of which waited for: 1 -> 0; matrix products, arithmetic and copies ran while one was open for 0% -> 0% of each run, Pallas kernels for 39% -> 40%
where the time goes in v4:
time: 40.6 us; the launch traced here: 40.5 us
  Pallas kernels  27.1 us (67%)
  starting transfers between devices  12.5 us (31%)
  between operations  0.75 us (2%)
    pallas_call x8, Pallas kernels, call(): pl.pallas_call(kernel, in_specs=[VMEM_SPEC] * len(args), out_specs=[HBM_S...  25.6 us
    ppermute x3, starting transfers between devices, paired(): lax.ppermute(sb, axis, [(i, (((i + 1) % n ^ 1) - 1) % n) for i in range(n)])  6.73 us
    ppermute x1, starting transfers between devices, swap(): from_upper = lax.ppermute(to_lower, axis, ring(axis, -1))  2.25 us
    ppermute x1, starting transfers between devices, swap(): from_lower = lax.ppermute(to_upper, axis, ring(axis, 1))  1.63 us
    pallas_call x1, Pallas kernels, body(): pl.pallas_call(prep_kernel, in_specs=[HBM_SPEC] * len(inputs), out_specs=...  1.54 us
  transfers between devices with their start and end apart: 10, of which 0 were waited for; matrix products, arithmetic and copies ran while one was open for 0% of the time, Pallas kernels for 40%

profile of v4, /device:TPU:0, one launch (start us, length us, event | category | flops | bytes accessed | tf_op | source)
XLA Modules:
  0.0 40.5 jit_solution(14021295929031587164)
XLA Ops:
  0.6 1.5 %prep.1 = (f32[3,7,8,16,128]{4,3,2,1,0:T(8,128)S(1)}, f32[6,8,16,128]{3,2,1,0:T(8,128)S(1)}, f32[22,16,128]{2,1,0:T(8,128)S(1)}, f32[22,16,128]{2,1,0:T(8,128)S(1)}, f32[16,128]{1,0:T(8,128)S(1)}) custom-call(s32[8,128]{1,0:T(8,128)} %refs_0_.1, f32[3,128,128]{2,1,0:T(8,128)} %bitcast.9, f32[2,128,128]{2,1,0:T(8,128)} %bitcast.12, f32[128,128]{1,0:T(8,128)} %bitcast.13, ...), custom_call_target="tpu_custom_call" | custom-call | tf_op jit(solution)/shard_map/prep/pallas_call | solution.py:1023
  2.2 0.6 %collective-permute-start = (f32[22,16,128]{2,1,0:T(8,128)S(1)}, f32[22,16,128]{2,1,0:T(8,128)S(1)}, u32[]{:S(2)}, u32[]{:S(2)}) collective-permute-start(f32[22,16,128]{2,1,0:T(8,128)S(1)} %get-tuple-element.54), channel_id=1, source_target_pairs={{0,1},{1,0},{2,3},{3,2},{4,5},{5,4},{6,7},{7,6},{8,9},{9,8},{10,11... | collective-permute-start | bytes 540680 | tf_op jit(solution)/shard_map/ppermute | solution.py:1008
  2.7 3.5 %collective-permute-start.1 = (f32[22,16,128]{2,1,0:T(8,128)S(1)}, f32[22,16,128]{2,1,0:T(8,128)S(1)}, u32[]{:S(2)}, u32[]{:S(2)}) collective-permute-start(f32[22,16,128]{2,1,0:T(8,128)S(1)} %get-tuple-element.55), channel_id=1, source_target_pairs={{0,7},{1,2},{2,1},{3,4},{4,3},{5,6},{6,5},{7,0},{8,15},{9,10},{10,... | collective-permute-start | bytes 540680 | tf_op jit(solution)/shard_map/ppermute | solution.py:1009
  6.3 0.5 %collective-permute-start.2 = (f32[16,128]{1,0:T(8,128)S(1)}, f32[16,128]{1,0:T(8,128)S(1)}, u32[]{:S(2)}, u32[]{:S(2)}) collective-permute-start(f32[16,128]{1,0:T(8,128)S(1)} %get-tuple-element.58.mx), channel_id=1, source_target_pairs={{0,4},{1,5},{2,6},{3,7},{4,0},{5,1},{6,2},{7,3},{8,12},{9,13},{10,... | collective-permute-start | bytes 24584 | tf_op jit(solution)/shard_map/ppermute | solution.py:1043
  6.8 4.6 %near.1 = (f32[11,16,10,8,128]{4,3,2,1,0:T(8,128)S(1)}, f32[11,16,10,8,128]{4,3,2,1,0:T(8,128)S(1)}, f32[5,16,128]{2,1,0:T(8,128)S(1)}, f32[5,16,128]{2,1,0:T(8,128)S(1)}) custom-call(f32[3,7,8,16,128]{4,3,2,1,0:T(8,128)S(1)} %get-tuple-element.52.geo, f32[6,8,16,128]{3,2,1,0:T(8,128)S(1)} %get-tuple-element.53.aux), custom_call_target="tpu_custom_call" | custom-call | tf_op jit(solution)/shard_map/near/pallas_call | solution.py:983
  11.4 0.0 collective-permute-done.2.rest_0_
  11.4 0.0 collective-permute-done.ra
  11.4 0.0 collective-permute-done.1.rb
  11.4 0.4 pack.1
  11.8 1.6 %collective-permute-start.3 = (f32[6,16,128]{2,1,0:T(8,128)S(1)}, f32[6,16,128]{2,1,0:T(8,128)S(1)}, u32[]{:S(2)}, u32[]{:S(2)}) collective-permute-start(f32[6,16,128]{2,1,0:T(8,128)S(1)} %get-tuple-element.62.cr), channel_id=1, source_target_pairs={{0,8},{8,16},{16,24},{24,0},{1,9},{9,17},{17,25},{25,1},{2,10},{10... | collective-permute-start | bytes 147464 | tf_op jit(solution)/shard_map/ppermute | solution.py:1001
  13.5 2.2 %collective-permute-start.4 = (f32[6,16,128]{2,1,0:T(8,128)S(1)}, f32[6,16,128]{2,1,0:T(8,128)S(1)}, u32[]{:S(2)}, u32[]{:S(2)}) collective-permute-start(f32[6,16,128]{2,1,0:T(8,128)S(1)} %get-tuple-element.63.cl), channel_id=1, source_target_pairs={{0,24},{8,0},{16,8},{24,16},{1,25},{9,1},{17,9},{25,17},{2,26},{10... | collective-permute-start | bytes 147464 | tf_op jit(solution)/shard_map/ppermute | solution.py:1002
  15.7 0.8 %collective-permute-start.5 = (f32[16,128]{1,0:T(8,128)S(1)}, f32[16,128]{1,0:T(8,128)S(1)}, u32[]{:S(2)}, u32[]{:S(2)}) collective-permute-start(f32[16,128]{1,0:T(8,128)S(1)} %get-tuple-element.70.rest_0_), channel_id=1, source_target_pairs={{0,16},{8,24},{16,0},{24,8},{1,17},{9,25},{17,1},{25,9},{2,18},{10... | collective-permute-start | bytes 24584 | tf_op jit(solution)/shard_map/ppermute | solution.py:1063
  16.5 3.7 %rim.1 = (f32[11,16,10,8,128]{4,3,2,1,0:T(8,128)S(1)}, f32[11,16,10,8,128]{4,3,2,1,0:T(8,128)S(1)}, f32[3,12,16,128]{3,2,1,0:T(8,128)S(1)}, f32[3,12,16,128]{3,2,1,0:T(8,128)S(1)}) custom-call(f32[3,7,6,16,128]{4,3,2,1,0:T(8,128)S(1)} %get-tuple-element.64.ge, ...), custom_call_target="tpu_custom_call", output_to_operand_aliasing={{0}: (1, {}), {1}: (2, {})} | custom-call | tf_op jit(solution)/shard_map/rim/pallas_call | solution.py:983
  20.2 0.0 collective-permute-done.5.rest_1_
  20.3 0.0 collective-permute-done.3.rl
  20.3 0.0 collective-permute-done.4.rr
  20.3 4.0 %first_half.1 = (f32[2,16,10,8,128]{4,3,2,1,0:T(8,128)S(1)}, f32[2,16,10,8,128]{4,3,2,1,0:T(8,128)S(1)}, f32[8,16,128]{2,1,0:T(8,128)S(1)}, f32[2,16,128]{2,1,0:...) custom-call(f32[6,8,16,128]{3,2,1,0:T(8,128)S(1)} %get-tuple-element, ...), custom_call_target="tpu_custom_call" | custom-call | tf_op jit(solution)/shard_map/first_half/pallas_call | solution.py:983
  24.3 0.0 collective-permute-start.6
  24.3 1.2 %collective-permute-start.7 = (f32[5,16,128]{2,1,0:T(8,128)S(1)}, f32[5,16,128]{2,1,0:T(8,128)S(1)}, u32[]{:S(2)}, u32[]{:S(2)}) collective-permute-start(f32[5,16,128]{2,1,0:T(8,128)S(1)} %get-tuple-element.83), channel_id=1, source_target_pairs={{0,7},{1,2},{2,1},{3,4},{4,3},{5,6},{6,5},{7,0},{8,15},{9,10},{10,... | collective-permute-start | bytes 122888 | tf_op jit(solution)/shard_map/ppermute | solution.py:1009
  25.5 3.8 %density.1 = (f32[3,5,8,16,128]{4,3,2,1,0:T(8,128)S(1)}, f32[6,9,16,128]{3,2,1,0:T(8,128)S(1)}, f32[8,16,128]{2,1,0:T(8,128)S(1)}, f32[2,16,128]{2,1,0:T(8,128)S...) custom-call(f32[6,8,16,128]{3,2,1,0:T(8,128)S(1)} %get-tuple-element.53., ...), custom_call_target="tpu_custom_call" | custom-call | tf_op jit(solution)/shard_map/density/pallas_call | solution.py:983
  29.3 0.0 collective-permute-done.6.ra
  29.3 0.0 collective-permute-done.7.rb
  29.3 2.7 %second_half.1 = (f32[128,128]{1,0:T(8,128)S(1)}, f32[3,8,16,128]{3,2,1,0:T(8,128)S(1)}, f32[16,128]{1,0:T(8,128)S(1)}, f32[4,16,128]{2,1,0:T(8,128)S(1)}, f32[4...) custom-call(f32[6,8,16,128]{3,2,1,0:T(8,128)S(1)} %get-tuple-element.53.aux, f32[8,16,128]{2,1,0:T(8,128)S(1)} %get-tuple-element.77.v1, ...), custom_call_target="tpu_custom_call" | custom-call | tf_op jit(solution)/shard_map/second_half/pallas_call | solution.py:983
  32.0 0.1 collective-permute-start.8
  32.1 2.0 %collective-permute-start.9 = (f32[4,16,128]{2,1,0:T(8,128)S(1)}, f32[4,16,128]{2,1,0:T(8,128)S(1)}, u32[]{:S(2)}, u32[]{:S(2)}) collective-permute-start(f32[4,16,128]{2,1,0:T(8,128)S(1)} %get-tuple-element.99), channel_id=1, source_target_pairs={{0,7},{1,2},{2,1},{3,4},{4,3},{5,6},{6,5},{7,0},{8,15},{9,10},{10,... | collective-permute-start | bytes 98312 | tf_op jit(solution)/shard_map/ppermute | solution.py:1009
  34.1 3.9 %kick_near.1 = (f32[3,3,8,16,128]{4,3,2,1,0:T(8,128)S(1)}, f32[128,128]{1,0:T(8,128)}) custom-call(f32[3,7,8,16,128]{4,3,2,1,0:T(8,128)S(1)} %get-tuple-element.52.geo, f32[3,5,8,16,128]{4,3,2,1,0:T(8,128)S(1)} %get-tuple-element.76.kn, f32[3,8,16,128]{3,2,1,0:T(8,128)S(1)} %get-tuple-element.92.press, f32[8,16,10,8,128]{4,3,2,1,0:T(8,128)S(1)} %get-tuple-element.93.qm, ...), custom_call_target="tpu_custom_call" | custom-call | tf_op jit(solution)/shard_map/kick_near/pallas_call | solution.py:983
  38.0 0.0 collective-permute-done.8.ra
  38.0 0.0 collective-permute-done.9.rb
  38.0 2.5 %kick_rim.1 = f32[3,128,128]{2,1,0:T(8,128)} custom-call(f32[3,7,8,16,128]{4,3,2,1,0:T(8,128)S(1)} %get-tuple-element.52.geo, f32[6,8,16,128]{3,2,1,0:T(8,128)S(1)} %get-tuple-element.53.aux, f32[3,5,8,16,128]{4,3,2,1,0:T(8,128)S(1)} %get-tuple-element.76.kn, f32[3,8,16,128]{3,2,1,0:T(8,128)S(1)} %get-tuple-element.92.press, ...), custom_call_target="tpu_custom_call" | custom-call | tf_op jit(solution)/shard_map/kick_rim/pallas_call | solution.py:983
Async XLA Ops:
  2.2 9.2 %collective-permute-start = (f32[22,16,128]{2,1,0:T(8,128)S(1)}, f32[22,16,128]{2,1,0:T(8,128)S(1)}, u32[]{:S(2)}, u32[]{:S(2)}) collective-permute-start(f32[22,16,128]{2,1,0:T(8,128)S(1)} %get-tuple-element.54), channel_id=1, source_target_pairs={{0,1},{1,0},{2,3},{3,2},{4,5},{5,4},{6,7},{7,6},{8,9},{9,8},{10,11... | collective-permute-start | bytes 540680 | tf_op jit(solution)/shard_map/ppermute | solution.py:1008
  2.7 8.7 %collective-permute-start.1 = (f32[22,16,128]{2,1,0:T(8,128)S(1)}, f32[22,16,128]{2,1,0:T(8,128)S(1)}, u32[]{:S(2)}, u32[]{:S(2)}) collective-permute-start(f32[22,16,128]{2,1,0:T(8,128)S(1)} %get-tuple-element.55), channel_id=1, source_target_pairs={{0,7},{1,2},{2,1},{3,4},{4,3},{5,6},{6,5},{7,0},{8,15},{9,10},{10,... | collective-permute-start | bytes 540680 | tf_op jit(solution)/shard_map/ppermute | solution.py:1009
  6.3 5.1 %collective-permute-start.2 = (f32[16,128]{1,0:T(8,128)S(1)}, f32[16,128]{1,0:T(8,128)S(1)}, u32[]{:S(2)}, u32[]{:S(2)}) collective-permute-start(f32[16,128]{1,0:T(8,128)S(1)} %get-tuple-element.58.mx), channel_id=1, source_target_pairs={{0,4},{1,5},{2,6},{3,7},{4,0},{5,1},{6,2},{7,3},{8,12},{9,13},{10,... | collective-permute-start | bytes 24584 | tf_op jit(solution)/shard_map/ppermute | solution.py:1043
  11.8 8.4 %collective-permute-start.3 = (f32[6,16,128]{2,1,0:T(8,128)S(1)}, f32[6,16,128]{2,1,0:T(8,128)S(1)}, u32[]{:S(2)}, u32[]{:S(2)}) collective-permute-start(f32[6,16,128]{2,1,0:T(8,128)S(1)} %get-tuple-element.62.cr), channel_id=1, source_target_pairs={{0,8},{8,16},{16,24},{24,0},{1,9},{9,17},{17,25},{25,1},{2,10},{10... | collective-permute-start | bytes 147464 | tf_op jit(solution)/shard_map/ppermute | solution.py:1001
  13.5 6.8 %collective-permute-start.4 = (f32[6,16,128]{2,1,0:T(8,128)S(1)}, f32[6,16,128]{2,1,0:T(8,128)S(1)}, u32[]{:S(2)}, u32[]{:S(2)}) collective-permute-start(f32[6,16,128]{2,1,0:T(8,128)S(1)} %get-tuple-element.63.cl), channel_id=1, source_target_pairs={{0,24},{8,0},{16,8},{24,16},{1,25},{9,1},{17,9},{25,17},{2,26},{10... | collective-permute-start | bytes 147464 | tf_op jit(solution)/shard_map/ppermute | solution.py:1002
  15.7 4.5 %collective-permute-start.5 = (f32[16,128]{1,0:T(8,128)S(1)}, f32[16,128]{1,0:T(8,128)S(1)}, u32[]{:S(2)}, u32[]{:S(2)}) collective-permute-start(f32[16,128]{1,0:T(8,128)S(1)} %get-tuple-element.70.rest_0_), channel_id=1, source_target_pairs={{0,16},{8,24},{16,0},{24,8},{1,17},{9,25},{17,1},{25,9},{2,18},{10... | collective-permute-start | bytes 24584 | tf_op jit(solution)/shard_map/ppermute | solution.py:1063
  24.3 5.0 %collective-permute-start.6 = (f32[5,16,128]{2,1,0:T(8,128)S(1)}, f32[5,16,128]{2,1,0:T(8,128)S(1)}, u32[]{:S(2)}, u32[]{:S(2)}) collective-permute-start(f32[5,16,128]{2,1,0:T(8,128)S(1)} %get-tuple-element.82), channel_id=1, source_target_pairs={{0,1},{1,0},{2,3},{3,2},{4,5},{5,4},{6,7},{7,6},{8,9},{9,8},{10,11... | collective-permute-start | bytes 122888 | tf_op jit(solution)/shard_map/ppermute | solution.py:1008
  24.3 5.0 %collective-permute-start.7 = (f32[5,16,128]{2,1,0:T(8,128)S(1)}, f32[5,16,128]{2,1,0:T(8,128)S(1)}, u32[]{:S(2)}, u32[]{:S(2)}) collective-permute-start(f32[5,16,128]{2,1,0:T(8,128)S(1)} %get-tuple-element.83), channel_id=1, source_target_pairs={{0,7},{1,2},{2,1},{3,4},{4,3},{5,6},{6,5},{7,0},{8,15},{9,10},{10,... | collective-permute-start | bytes 122888 | tf_op jit(solution)/shard_map/ppermute | solution.py:1009
  32.0 6.0 %collective-permute-start.8 = (f32[4,16,128]{2,1,0:T(8,128)S(1)}, f32[4,16,128]{2,1,0:T(8,128)S(1)}, u32[]{:S(2)}, u32[]{:S(2)}) collective-permute-start(f32[4,16,128]{2,1,0:T(8,128)S(1)} %get-tuple-element.98), channel_id=1, source_target_pairs={{0,1},{1,0},{2,3},{3,2},{4,5},{5,4},{6,7},{7,6},{8,9},{9,8},{10,11... | collective-permute-start | bytes 98312 | tf_op jit(solution)/shard_map/ppermute | solution.py:1008
  32.1 5.9 %collective-permute-start.9 = (f32[4,16,128]{2,1,0:T(8,128)S(1)}, f32[4,16,128]{2,1,0:T(8,128)S(1)}, u32[]{:S(2)}, u32[]{:S(2)}) collective-permute-start(f32[4,16,128]{2,1,0:T(8,128)S(1)} %get-tuple-element.99), channel_id=1, source_target_pairs={{0,7},{1,2},{2,1},{3,4},{4,3},{5,6},{6,5},{7,0},{8,15},{9,10},{10,... | collective-permute-start | bytes 98312 | tf_op jit(solution)/shard_map/ppermute | solution.py:1009

commit v5 on v4

--- a/solution.py
+++ b/solution.py
@@ -205,40 +205,34 @@
     return lane, where - STRIDE * jnp.floor((where + 0.5) * (1.0 / STRIDE))
 
 
-def pack_rows(cl, cr, start, feature, side, rows, side_rows):
-    slots, lanes = cl.shape[1:]
+def pack_rows(cols, mixed, feature, side, rows, side_rows):
+    slots, lanes = mixed[0].shape
     lane = lane_iota((slots, lanes))
-    tiles = (NGEO + 3) // 2
-    left = [start(cl, n) for n in range(tiles)]
-    right = [start(cr, n) for n in range(tiles)]
 
     def put(into, tile, shift, first, count):
-        here = jnp.logical_and(lane >= first, lane < first + count)
+        here = lane == first
+        if count > 1:
+            here = jnp.logical_and(lane >= first, lane < first + count)
         return jnp.where(here, roll(tile, shift), into)
 
+    (both,) = mixed
     for row in rows:
+        at = STRIDE * row
         for k in range(NGEO + 2):
             if k > NGEO and row not in side_rows:
                 continue
             tile = feature(k, row) if k <= NGEO else side(0, row)
-            at = STRIDE * row + 5 * (k % 2)
-            n = k // 2
-            left[n] = put(left[n], tile, at + 1, at + 1, 5)
-            right[n] = put(right[n], tile, at + 5 - lanes, at, 5)
+            cols[k] = put(cols[k], tile, at + 5, at, 10)
         if row in side_rows:
             m, vx, vy, vz = (side(1 + k, row) for k in range(4))
-            at = STRIDE * row + 5
-            left[-1] = put(left[-1], m, at + 1, at + 1, 2)
-            right[-1] = put(right[-1], m, at + 5 - lanes, at + 3, 2)
+            both = put(both, m, at + 5, at + 3, 4)
             for k, tile in enumerate((vx, vy, vz)):
-                left[-1] = put(left[-1], tile, at + 3 + k, at + 3 + k, 1)
-                right[-1] = put(right[-1], tile, at + 3 - k - lanes, at + 2 - k, 1)
-    for n in range(tiles):
-        cl[n] = left[n]
-        cr[n] = right[n]
-
-
-def near_kernel(geo, aux, w, s, cl, cr):
+                both = put(both, tile, at + 3 - k - lanes, at + 2 - k, 1)
+                both = put(both, tile, at + 7 + k, at + 7 + k, 1)
+    mixed[0] = both
+
+
+def near_kernel(geo, aux, w, s, cols_out):
     rows, slots, lanes = geo.shape[2:]
 
     @pl.loop(0, rows - 1)
@@ -246,20 +240,23 @@
         weights(ALL, lambda k: geo.at[0, k, r], row_far(geo, r), w, s, r + HALO)
 
     own = range(HALO, HALO + rows)
+    cols = [jnp.zeros((slots, lanes), F32)] * (NGEO + 2)
+    mixed = [jnp.zeros((slots, lanes), F32)]
     pack_rows(
-        cl,
-        cr,
-        lambda ref, n: jnp.zeros((slots, lanes), F32),
+        cols,
+        mixed,
         lambda k, row: geo[0, k, row - HALO] if k < NGEO else aux[0, row - HALO],
         lambda k, row: aux[1 + k, row - HALO],
         own,
         own,
     )
-
-
-def pack_kernel(geo, ra, rb, clp, crp, mx, *rest):
+    for k, tile in enumerate(cols + mixed):
+        cols_out[k] = tile
+
+
+def pack_kernel(geo, ra, rb, colp, mx, *rest):
     ru, rd = receive(ra, rb, even_row())
-    spare, (ge, th, ich, mvh, cl, cr, ma) = rest[:-7], rest[-7:]
+    spare, (ge, th, ich, mvh, col, cl, cr, ma) = rest[:-8], rest[-8:]
     rows, slots, lanes = geo.shape[2:]
     at_top = lax.axis_index("gy") == 0
     at_end = lax.axis_index("gy") == lax.axis_size("gy") - 1
@@ -289,15 +286,18 @@
         ich[n] = side(0, row)
         for k in range(4):
             mvh[k, n] = side(1 + k, row)
-    pack_rows(
-        cl,
-        cr,
-        lambda ref, n: (clp if ref is cl else crp)[n],
-        feature,
-        side,
-        (0, 1, end, end + 1),
-        (HALO - 1, end),
-    )
+    cols = [colp[k] for k in range(NGEO + 2)]
+    mixed = [colp[NGEO + 2]]
+    pack_rows(cols, mixed, feature, side, (0, 1, end, end + 1), (HALO - 1, end))
+    cols = cols + mixed
+    key = strip_place((slots, lanes))[1]
+    lower = key <= 4.0
+    for k, tile in enumerate(cols):
+        col[k] = tile
+    for n in range(len(cols) // 2):
+        one, two = cols[2 * n], cols[2 * n + 1]
+        cl[n] = jnp.where(lower, roll(two, -5), one)
+        cr[n] = jnp.where(lower, one, roll(two, 5))
     best = jnp.maximum(jnp.maximum(ru(base + 5), rd(base + 5)), mx[...])
     for ref in spare:
         best = jnp.maximum(best, ref[...])
@@ -453,29 +453,32 @@
     shape = out.shape[2:]
     lanes = shape[-1]
     lane, key = strip_place(shape)
+    parts = [[out_t[e, side] for e in ALL] for side in range(2)]
     ends = []
-    for side in range(2):
-        total = out_t[0, side]
+    for side, turn in ((0, 0), (1, 0), (1, 4)):
+        total = roll(parts[side][0], turn)
         for e in ALL[1:]:
-            total = total + roll(out_t[e, side], STRIP_SHIFT[e])
-        out_t[0, side] = total
+            total = total + roll(parts[side][e], STRIP_SHIFT[e] + turn)
         ends.append(total)
-    both = jnp.where(key == 5.0, ends[0], roll(ends[1], 4))
+    out_t[0, 0], out_t[0, 1] = ends[0], ends[1]
+    both = jnp.where(key == 5.0, ends[0], ends[2])
     border = jnp.logical_or(lane == 0, lane == lanes - 1)
     for row in range(first, last):
         edge = jnp.where(border, roll(both, -(STRIDE * row + 5)), 0.0)
         out[0, row] = (out[0, row] + edge) + (roll(out[1, row], 1) + roll(out[2, row], -1))
 
 
-def end_columns(rows, first, start=None):
+def end_columns(rows, first):
     shape = rows[0].shape
+    lanes = shape[-1]
     lane = lane_iota(shape)
-    ends = jnp.zeros(shape, F32) if start is None else start
+    low = jnp.zeros(shape, F32)
+    high = low
     for n, tile in enumerate(rows):
         at = STRIDE * (n + first)
-        here = jnp.logical_or(lane == at + 4, lane == at + 5)
-        ends = jnp.where(here, roll(tile, at + 5), ends)
-    return ends
+        low = jnp.where(lane == at + 5, roll(tile, at + 5), low)
+        high = jnp.where(lane == at, roll(tile, at + 1 - lanes), high)
+    return low, high
 
 
 def advance(val, val_t, out, out_t, diag, diag_t, ic, ict, first, last):
@@ -488,11 +491,10 @@
     columns = end_columns(fresh, first)
     for side in range(2):
         tile = ict[side] * (out_t[0, side] - val_t[0, side] * diag_t[side])
-        mine = columns if side == 0 else roll(columns, -4)
-        val_t[0, side] = jnp.where(key == (0.0 if side else 5.0), mine, tile)
-
-
-def first_half_kernel(aux, th, ich, rl, rr, cl, cr, w, out1, bare1, *rest):
+        val_t[0, side] = jnp.where(key == (0.0 if side else 5.0), columns[side], tile)
+
+
+def first_half_kernel(aux, th, ich, rl, rr, col, w, out1, bare1, *rest):
     spare, rest = rest[:-23], rest[-23:]
     (wt, st, v1, v1t, v2, v2t, diag, diag_t, ic, ict, tside, tt, sa, sb, ma2) = rest[:15]
     tgeo, val, val_t, out, out_t, bare_t, diag3, acc = rest[15:]
@@ -508,19 +510,21 @@
     own_left = jnp.logical_and(inside, key == 5.0)
     own_right = jnp.logical_and(inside, key == 0.0)
 
-    def got(ref, k):
-        return roll(ref[k // 2], -5) if k % 2 else ref[k // 2]
+    def from_lower(k):
+        return roll(rl[k // 2], -5) if k % 2 else rl[k // 2]
+
+    def from_upper(k):
+        return roll(rr[k // 2], 1 if k % 2 else -4)
 
     for k in range(NGEO + 1):
-        left, right = got(rl, k), got(rr, k)
+        left, right = from_lower(k), from_upper(k)
         blank = 0.0
         if k == 0:
             left = jnp.where(at_left, FAR, left)
             right = jnp.where(at_right, FAR, right)
             blank = FAR
-        mine = roll(cl[k // 2], -1 if k % 2 else 4)
-        left = jnp.where(from_left, left, jnp.where(own_left, mine, blank))
-        mine = roll(cr[k // 2], -9 if k % 2 else -4)
+        left = jnp.where(from_left, left, jnp.where(own_left, col[k], blank))
+        mine = roll(col[k], -4)
         right = jnp.where(from_right, right, jnp.where(own_right, mine, blank))
         for side, tile in ((0, left), (1, right)):
             if k == NGEO:
@@ -538,11 +542,12 @@
                 tgeo[e, k, side] = turned
             if k < 3:
                 tside[k, side] = tile
-    ict[0] = jnp.where(jnp.logical_and(from_left, jnp.logical_not(at_left)), got(rl, NGEO + 1), 0.0)
+    ict[0] = jnp.where(jnp.logical_and(from_left, jnp.logical_not(at_left)), from_lower(NGEO + 1), 0.0)
     ict[1] = jnp.where(
-        jnp.logical_and(from_right, jnp.logical_not(at_right)), got(rr, NGEO + 1), 0.0
-    )
-    near_l, near_r, own_l, own_r = (got(ref, NGEO + 2) for ref in (rl, rr, cl, cr))
+        jnp.logical_and(from_right, jnp.logical_not(at_right)), from_upper(NGEO + 1), 0.0
+    )
+    near_l, near_r = from_lower(NGEO + 2), from_upper(NGEO + 2)
+    own_l, own_r = roll(col[NGEO + 2], -4), col[NGEO + 2]
     tside[3, 0] = jnp.where(
         jnp.logical_or(key == 3.0, key == 4.0), near_l, jnp.where(own_left, roll(own_l, 4), 0.0)
     )
@@ -707,12 +712,11 @@
 
 
 def with_ends(key, tile, rows):
-    lanes = tile.shape[-1]
-    columns = end_columns(rows, HALO)
+    low, high = end_columns(rows, HALO)
     lane = lane_iota(tile.shape)
     inside = jnp.logical_and(lane >= STRIDE * HALO, lane < STRIDE * (HALO + len(rows)))
-    low = jnp.where(jnp.logical_and(inside, key == 5.0), columns, tile)
-    return jnp.where(jnp.logical_and(inside, key == 0.0), roll(columns, -4), low)
+    tile = jnp.where(jnp.logical_and(inside, key == 5.0), low, tile)
+    return jnp.where(jnp.logical_and(inside, key == 0.0), high, tile)
 
 
 def second_half_kernel(
@@ -1047,16 +1051,16 @@
     two = (2,) + tile
     own = (rows,) + tile
     ext = (full,) + tile
-    w, s, clp, crp = call(
+    w, s, colp = call(
         near_kernel,
         (geo, aux),
-        [pairs, pairs, ((NGEO + 3) // 2,) + tile, ((NGEO + 3) // 2,) + tile],
+        [pairs, pairs, (NGEO + 3,) + tile],
         name="near",
     )
-    ge, th, ich, mvh, cl, cr, ma = call(
+    ge, th, ich, mvh, col, cl, cr, ma = call(
         pack_kernel,
-        (geo, ra, rb, clp, crp, mx, *spare),
-        [(3, NGEO, 6) + tile, (4,) + tile, two, (4,) + two, columns, columns, tile],
+        (geo, ra, rb, colp, mx, *spare),
+        [(3, NGEO, 6) + tile, (4,) + tile, two, (4,) + two, (NGEO + 3,) + tile, columns, columns, tile],
         name="pack",
     )
     rl, rr = swap(cl, cr, "gx")
@@ -1073,7 +1077,7 @@
     work = [(3,) + ext, (npart,) + two, (3,) + ext, (npart,) + two]
     wt, st, v1, v1t, v2, v2t, diag, diag_t, ic, ict, tside, tt, sa, sb, ma2 = call(
         first_half_kernel,
-        (aux, th, ich, rl, rr, cl, cr, w, out1, bare1, ma, *spare),
+        (aux, th, ich, rl, rr, col, w, out1, bare1, ma, *spare),
         [strips, strips, own, two, own, two, ext, two, ext, two, (7,) + two, two]
         + [(HALO + 3,) + tile] * 2
         + [tile],

time: 40.6 us -> 40.2 us (level)
  Pallas kernels: 27.1 us -> 26.6 us
    pallas_call x8, Pallas kernels: 25.6 us -> 25.1 us  [call(): pl.pallas_call(kernel, in_specs=[VMEM_SPEC] * len(args), out_specs=[HBM_S...]
where the time goes in v5:
time: 40.2 us; the launch traced here: 40.1 us
  Pallas kernels  26.6 us (66%)
  starting transfers between devices  12.6 us (31%)
  between operations  0.77 us (2%)
    pallas_call x8, Pallas kernels, call(): pl.pallas_call(kernel, in_specs=[VMEM_SPEC] * len(args), out_specs=[HBM_S...  25.1 us
    ppermute x3, starting transfers between devices, paired(): lax.ppermute(sb, axis, [(i, (((i + 1) % n ^ 1) - 1) % n) for i in range(n)])  6.73 us
    ppermute x1, starting transfers between devices, swap(): from_upper = lax.ppermute(to_lower, axis, ring(axis, -1))  2.25 us
    ppermute x1, starting transfers between devices, swap(): from_lower = lax.ppermute(to_upper, axis, ring(axis, 1))  1.63 us
    pallas_call x1, Pallas kernels, body(): pl.pallas_call(prep_kernel, in_specs=[HBM_SPEC] * len(inputs), out_specs=...  1.54 us
  transfers between devices with their start and end apart: 10, of which 0 were waited for; matrix products, arithmetic and copies ran while one was open for 0% of the time, Pallas kernels for 40%

profile of v5, /device:TPU:0, one launch (start us, length us, event | category | flops | bytes accessed | tf_op | source)
XLA Modules:
  0.0 40.1 jit_solution(17001728203145673929)
XLA Ops:
  0.6 1.5 %prep.1 = (f32[3,7,8,16,128]{4,3,2,1,0:T(8,128)S(1)}, f32[6,8,16,128]{3,2,1,0:T(8,128)S(1)}, f32[22,16,128]{2,1,0:T(8,128)S(1)}, f32[22,16,128]{2,1,0:T(8,128)S(1)}, f32[16,128]{1,0:T(8,128)S(1)}) custom-call(s32[8,128]{1,0:T(8,128)} %refs_0_.1, f32[3,128,128]{2,1,0:T(8,128)} %bitcast.9, f32[2,128,128]{2,1,0:T(8,128)} %bitcast.12, f32[128,128]{1,0:T(8,128)} %bitcast.13, ...), custom_call_target="tpu_custom_call" | custom-call | tf_op jit(solution)/shard_map/prep/pallas_call | solution.py:1027
  2.2 0.6 %collective-permute-start = (f32[22,16,128]{2,1,0:T(8,128)S(1)}, f32[22,16,128]{2,1,0:T(8,128)S(1)}, u32[]{:S(2)}, u32[]{:S(2)}) collective-permute-start(f32[22,16,128]{2,1,0:T(8,128)S(1)} %get-tuple-element.54), channel_id=1, source_target_pairs={{0,1},{1,0},{2,3},{3,2},{4,5},{5,4},{6,7},{7,6},{8,9},{9,8},{10,11... | collective-permute-start | bytes 540680 | tf_op jit(solution)/shard_map/ppermute | solution.py:1012
  2.7 3.5 %collective-permute-start.1 = (f32[22,16,128]{2,1,0:T(8,128)S(1)}, f32[22,16,128]{2,1,0:T(8,128)S(1)}, u32[]{:S(2)}, u32[]{:S(2)}) collective-permute-start(f32[22,16,128]{2,1,0:T(8,128)S(1)} %get-tuple-element.55), channel_id=1, source_target_pairs={{0,7},{1,2},{2,1},{3,4},{4,3},{5,6},{6,5},{7,0},{8,15},{9,10},{10,... | collective-permute-start | bytes 540680 | tf_op jit(solution)/shard_map/ppermute | solution.py:1013
  6.3 0.5 %collective-permute-start.2 = (f32[16,128]{1,0:T(8,128)S(1)}, f32[16,128]{1,0:T(8,128)S(1)}, u32[]{:S(2)}, u32[]{:S(2)}) collective-permute-start(f32[16,128]{1,0:T(8,128)S(1)} %get-tuple-element.57.mx), channel_id=1, source_target_pairs={{0,4},{1,5},{2,6},{3,7},{4,0},{5,1},{6,2},{7,3},{8,12},{9,13},{10,... | collective-permute-start | bytes 24584 | tf_op jit(solution)/shard_map/ppermute | solution.py:1047
  6.8 4.5 %near.1 = (f32[11,16,10,8,128]{4,3,2,1,0:T(8,128)S(1)}, f32[11,16,10,8,128]{4,3,2,1,0:T(8,128)S(1)}, f32[10,16,128]{2,1,0:T(8,128)S(1)}) custom-call(f32[3,7,8,16,128]{4,3,2,1,0:T(8,128)S(1)} %get-tuple-element.52.geo, f32[6,8,16,128]{3,2,1,0:T(8,128)S(1)} %get-tuple-element.53.aux), custom_call_target="tpu_custom_call" | custom-call | tf_op jit(solution)/shard_map/near/pallas_call | solution.py:987
  11.3 0.0 collective-permute-done.2.rest_0_
  11.3 0.0 collective-permute-done.ra
  11.3 0.0 collective-permute-done.1.rb
  11.3 0.4 pack.1
  11.7 1.6 %collective-permute-start.3 = (f32[6,16,128]{2,1,0:T(8,128)S(1)}, f32[6,16,128]{2,1,0:T(8,128)S(1)}, u32[]{:S(2)}, u32[]{:S(2)}) collective-permute-start(f32[6,16,128]{2,1,0:T(8,128)S(1)} %get-tuple-element.61), channel_id=1, source_target_pairs={{0,8},{8,16},{16,24},{24,0},{1,9},{9,17},{17,25},{25,1},{2,10},{10... | collective-permute-start | bytes 147464 | tf_op jit(solution)/shard_map/ppermute | solution.py:1005
  13.3 2.2 %collective-permute-start.4 = (f32[6,16,128]{2,1,0:T(8,128)S(1)}, f32[6,16,128]{2,1,0:T(8,128)S(1)}, u32[]{:S(2)}, u32[]{:S(2)}) collective-permute-start(f32[6,16,128]{2,1,0:T(8,128)S(1)} %get-tuple-element.62), channel_id=1, source_target_pairs={{0,24},{8,0},{16,8},{24,16},{1,25},{9,1},{17,9},{25,17},{2,26},{10... | collective-permute-start | bytes 147464 | tf_op jit(solution)/shard_map/ppermute | solution.py:1006
  15.5 0.8 %collective-permute-start.5 = (f32[16,128]{1,0:T(8,128)S(1)}, f32[16,128]{1,0:T(8,128)S(1)}, u32[]{:S(2)}, u32[]{:S(2)}) collective-permute-start(f32[16,128]{1,0:T(8,128)S(1)} %get-tuple-element.70.rest_0_), channel_id=1, source_target_pairs={{0,16},{8,24},{16,0},{24,8},{1,17},{9,25},{17,1},{25,9},{2,18},{10... | collective-permute-start | bytes 24584 | tf_op jit(solution)/shard_map/ppermute | solution.py:1067
  16.3 3.7 %rim.1 = (f32[11,16,10,8,128]{4,3,2,1,0:T(8,128)S(1)}, f32[11,16,10,8,128]{4,3,2,1,0:T(8,128)S(1)}, f32[3,12,16,128]{3,2,1,0:T(8,128)S(1)}, f32[3,12,16,128]{3,2,1,0:T(8,128)S(1)}) custom-call(f32[3,7,6,16,128]{4,3,2,1,0:T(8,128)S(1)} %get-tuple-element.64.ge, ...), custom_call_target="tpu_custom_call", output_to_operand_aliasing={{0}: (1, {}), {1}: (2, {})} | custom-call | tf_op jit(solution)/shard_map/rim/pallas_call | solution.py:987
  20.0 0.0 collective-permute-done.5.rest_1_
  20.1 0.0 collective-permute-done.3.rl
  20.1 0.0 collective-permute-done.4.rr
  20.1 3.8 %first_half.1 = (f32[2,16,10,8,128]{4,3,2,1,0:T(8,128)S(1)}, f32[2,16,10,8,128]{4,3,2,1,0:T(8,128)S(1)}, f32[8,16,128]{2,1,0:T(8,128)S(1)}, f32[2,16,128]{2,1,0:...) custom-call(f32[6,8,16,128]{3,2,1,0:T(8,128)S(1)} %get-tuple-element, ...), custom_call_target="tpu_custom_call" | custom-call | tf_op jit(solution)/shard_map/first_half/pallas_call | solution.py:987
  23.9 0.1 collective-permute-start.6
  24.0 1.3 %collective-permute-start.7 = (f32[5,16,128]{2,1,0:T(8,128)S(1)}, f32[5,16,128]{2,1,0:T(8,128)S(1)}, u32[]{:S(2)}, u32[]{:S(2)}) collective-permute-start(f32[5,16,128]{2,1,0:T(8,128)S(1)} %get-tuple-element.83), channel_id=1, source_target_pairs={{0,7},{1,2},{2,1},{3,4},{4,3},{5,6},{6,5},{7,0},{8,15},{9,10},{10,... | collective-permute-start | bytes 122888 | tf_op jit(solution)/shard_map/ppermute | solution.py:1013
  25.4 3.8 %density.1 = (f32[3,5,8,16,128]{4,3,2,1,0:T(8,128)S(1)}, f32[6,9,16,128]{3,2,1,0:T(8,128)S(1)}, f32[8,16,128]{2,1,0:T(8,128)S(1)}, f32[2,16,128]{2,1,0:T(8,128)S...) custom-call(f32[6,8,16,128]{3,2,1,0:T(8,128)S(1)} %get-tuple-element.53., ...), custom_call_target="tpu_custom_call" | custom-call | tf_op jit(solution)/shard_map/density/pallas_call | solution.py:987
  29.2 0.0 collective-permute-done.6.ra
  29.2 0.0 collective-permute-done.7.rb
  29.2 2.5 %second_half.1 = (f32[128,128]{1,0:T(8,128)S(1)}, f32[3,8,16,128]{3,2,1,0:T(8,128)S(1)}, f32[16,128]{1,0:T(8,128)S(1)}, f32[4,16,128]{2,1,0:T(8,128)S(1)}, f32[4...) custom-call(f32[6,8,16,128]{3,2,1,0:T(8,128)S(1)} %get-tuple-element.53.aux, f32[8,16,128]{2,1,0:T(8,128)S(1)} %get-tuple-element.77.v1, ...), custom_call_target="tpu_custom_call" | custom-call | tf_op jit(solution)/shard_map/second_half/pallas_call | solution.py:987
  31.7 0.1 collective-permute-start.8
  31.8 1.8 %collective-permute-start.9 = (f32[4,16,128]{2,1,0:T(8,128)S(1)}, f32[4,16,128]{2,1,0:T(8,128)S(1)}, u32[]{:S(2)}, u32[]{:S(2)}) collective-permute-start(f32[4,16,128]{2,1,0:T(8,128)S(1)} %get-tuple-element.99), channel_id=1, source_target_pairs={{0,7},{1,2},{2,1},{3,4},{4,3},{5,6},{6,5},{7,0},{8,15},{9,10},{10,... | collective-permute-start | bytes 98312 | tf_op jit(solution)/shard_map/ppermute | solution.py:1013
  33.6 3.9 %kick_near.1 = (f32[3,3,8,16,128]{4,3,2,1,0:T(8,128)S(1)}, f32[128,128]{1,0:T(8,128)}) custom-call(f32[3,7,8,16,128]{4,3,2,1,0:T(8,128)S(1)} %get-tuple-element.52.geo, f32[3,5,8,16,128]{4,3,2,1,0:T(8,128)S(1)} %get-tuple-element.76.kn, f32[3,8,16,128]{3,2,1,0:T(8,128)S(1)} %get-tuple-element.92.press, f32[8,16,10,8,128]{4,3,2,1,0:T(8,128)S(1)} %get-tuple-element.93.qm, ...), custom_call_target="tpu_custom_call" | custom-call | tf_op jit(solution)/shard_map/kick_near/pallas_call | solution.py:987
  37.6 0.0 collective-permute-done.8.ra
  37.6 0.0 collective-permute-done.9.rb
  37.6 2.5 %kick_rim.1 = f32[3,128,128]{2,1,0:T(8,128)} custom-call(f32[3,7,8,16,128]{4,3,2,1,0:T(8,128)S(1)} %get-tuple-element.52.geo, f32[6,8,16,128]{3,2,1,0:T(8,128)S(1)} %get-tuple-element.53.aux, f32[3,5,8,16,128]{4,3,2,1,0:T(8,128)S(1)} %get-tuple-element.76.kn, f32[3,8,16,128]{3,2,1,0:T(8,128)S(1)} %get-tuple-element.92.press, ...), custom_call_target="tpu_custom_call" | custom-call | tf_op jit(solution)/shard_map/kick_rim/pallas_call | solution.py:987
Async XLA Ops:
  2.2 9.1 %collective-permute-start = (f32[22,16,128]{2,1,0:T(8,128)S(1)}, f32[22,16,128]{2,1,0:T(8,128)S(1)}, u32[]{:S(2)}, u32[]{:S(2)}) collective-permute-start(f32[22,16,128]{2,1,0:T(8,128)S(1)} %get-tuple-element.54), channel_id=1, source_target_pairs={{0,1},{1,0},{2,3},{3,2},{4,5},{5,4},{6,7},{7,6},{8,9},{9,8},{10,11... | collective-permute-start | bytes 540680 | tf_op jit(solution)/shard_map/ppermute | solution.py:1012
  2.7 8.5 %collective-permute-start.1 = (f32[22,16,128]{2,1,0:T(8,128)S(1)}, f32[22,16,128]{2,1,0:T(8,128)S(1)}, u32[]{:S(2)}, u32[]{:S(2)}) collective-permute-start(f32[22,16,128]{2,1,0:T(8,128)S(1)} %get-tuple-element.55), channel_id=1, source_target_pairs={{0,7},{1,2},{2,1},{3,4},{4,3},{5,6},{6,5},{7,0},{8,15},{9,10},{10,... | collective-permute-start | bytes 540680 | tf_op jit(solution)/shard_map/ppermute | solution.py:1013
  6.3 5.0 %collective-permute-start.2 = (f32[16,128]{1,0:T(8,128)S(1)}, f32[16,128]{1,0:T(8,128)S(1)}, u32[]{:S(2)}, u32[]{:S(2)}) collective-permute-start(f32[16,128]{1,0:T(8,128)S(1)} %get-tuple-element.57.mx), channel_id=1, source_target_pairs={{0,4},{1,5},{2,6},{3,7},{4,0},{5,1},{6,2},{7,3},{8,12},{9,13},{10,... | collective-permute-start | bytes 24584 | tf_op jit(solution)/shard_map/ppermute | solution.py:1047
  11.7 8.4 %collective-permute-start.3 = (f32[6,16,128]{2,1,0:T(8,128)S(1)}, f32[6,16,128]{2,1,0:T(8,128)S(1)}, u32[]{:S(2)}, u32[]{:S(2)}) collective-permute-start(f32[6,16,128]{2,1,0:T(8,128)S(1)} %get-tuple-element.61), channel_id=1, source_target_pairs={{0,8},{8,16},{16,24},{24,0},{1,9},{9,17},{17,25},{25,1},{2,10},{10... | collective-permute-start | bytes 147464 | tf_op jit(solution)/shard_map/ppermute | solution.py:1005
  13.3 6.8 %collective-permute-start.4 = (f32[6,16,128]{2,1,0:T(8,128)S(1)}, f32[6,16,128]{2,1,0:T(8,128)S(1)}, u32[]{:S(2)}, u32[]{:S(2)}) collective-permute-start(f32[6,16,128]{2,1,0:T(8,128)S(1)} %get-tuple-element.62), channel_id=1, source_target_pairs={{0,24},{8,0},{16,8},{24,16},{1,25},{9,1},{17,9},{25,17},{2,26},{10... | collective-permute-start | bytes 147464 | tf_op jit(solution)/shard_map/ppermute | solution.py:1006
  15.5 4.5 %collective-permute-start.5 = (f32[16,128]{1,0:T(8,128)S(1)}, f32[16,128]{1,0:T(8,128)S(1)}, u32[]{:S(2)}, u32[]{:S(2)}) collective-permute-start(f32[16,128]{1,0:T(8,128)S(1)} %get-tuple-element.70.rest_0_), channel_id=1, source_target_pairs={{0,16},{8,24},{16,0},{24,8},{1,17},{9,25},{17,1},{25,9},{2,18},{10... | collective-permute-start | bytes 24584 | tf_op jit(solution)/shard_map/ppermute | solution.py:1067
  23.9 5.2 %collective-permute-start.6 = (f32[5,16,128]{2,1,0:T(8,128)S(1)}, f32[5,16,128]{2,1,0:T(8,128)S(1)}, u32[]{:S(2)}, u32[]{:S(2)}) collective-permute-start(f32[5,16,128]{2,1,0:T(8,128)S(1)} %get-tuple-element.82), channel_id=1, source_target_pairs={{0,1},{1,0},{2,3},{3,2},{4,5},{5,4},{6,7},{7,6},{8,9},{9,8},{10,11... | collective-permute-start | bytes 122888 | tf_op jit(solution)/shard_map/ppermute | solution.py:1012
  24.0 5.2 %collective-permute-start.7 = (f32[5,16,128]{2,1,0:T(8,128)S(1)}, f32[5,16,128]{2,1,0:T(8,128)S(1)}, u32[]{:S(2)}, u32[]{:S(2)}) collective-permute-start(f32[5,16,128]{2,1,0:T(8,128)S(1)} %get-tuple-element.83), channel_id=1, source_target_pairs={{0,7},{1,2},{2,1},{3,4},{4,3},{5,6},{6,5},{7,0},{8,15},{9,10},{10,... | collective-permute-start | bytes 122888 | tf_op jit(solution)/shard_map/ppermute | solution.py:1013
  31.7 5.9 %collective-permute-start.8 = (f32[4,16,128]{2,1,0:T(8,128)S(1)}, f32[4,16,128]{2,1,0:T(8,128)S(1)}, u32[]{:S(2)}, u32[]{:S(2)}) collective-permute-start(f32[4,16,128]{2,1,0:T(8,128)S(1)} %get-tuple-element.98), channel_id=1, source_target_pairs={{0,1},{1,0},{2,3},{3,2},{4,5},{5,4},{6,7},{7,6},{8,9},{9,8},{10,11... | collective-permute-start | bytes 98312 | tf_op jit(solution)/shard_map/ppermute | solution.py:1012
  31.8 5.8 %collective-permute-start.9 = (f32[4,16,128]{2,1,0:T(8,128)S(1)}, f32[4,16,128]{2,1,0:T(8,128)S(1)}, u32[]{:S(2)}, u32[]{:S(2)}) collective-permute-start(f32[4,16,128]{2,1,0:T(8,128)S(1)} %get-tuple-element.99), channel_id=1, source_target_pairs={{0,7},{1,2},{2,1},{3,4},{4,3},{5,6},{6,5},{7,0},{8,15},{9,10},{10,... | collective-permute-start | bytes 98312 | tf_op jit(solution)/shard_map/ppermute | solution.py:1013

commit v6 on v5

--- a/solution.py
+++ b/solution.py
@@ -887,7 +887,7 @@
 
 def kick_rim_kernel(
     geo, aux, kn, press, ge, mvh, kst, press_t, ra, rb, s, st, near, dt,
-    moved, mine, other, strip, out, out_t, acc,
+    target, mine, other, strip, out, out_t, acc, moved, sems,
 ):
     rows, slots, lanes = geo.shape[2:]
     nge = ge.shape[2]
@@ -965,10 +965,12 @@
         for e in crossing:
             total = total - roll(out_t[e, k], STRIP_SHIFT[e])
         ends.append(jnp.where(key == 5.0, total, roll(total, 4)))
-    for row in range(rows):
-        live = aux[1, row] > 0.0
-        factor = jnp.where(live, step / aux[2, row], 0.0)
-        for k in range(3):
+    factors = [
+        jnp.where(aux[1, row] > 0.0, step / aux[2, row], 0.0) for row in range(rows)
+    ]
+    copies = [pltpu.make_async_copy(moved.at[k], target.at[k], sems.at[k]) for k in range(3)]
+    for k in range(3):
+        for row, factor in enumerate(factors):
             parts = [near[variant, k, row] for variant in range(3)]
             if row == 0:
                 parts = [part + out[variant, k, 0] for variant, part in enumerate(parts)]
@@ -977,6 +979,9 @@
             edge = jnp.where(border, roll(ends[k], -(STRIDE * (row + HALO) + 5)), 0.0)
             total = (parts[0] + edge) + (roll(parts[1], 1) + roll(parts[2], -1))
             moved[k, pl.ds(row, slots, stride=rows), :] = aux[3 + k, row] + factor * total
+        copies[k].start()
+    for copy in copies:
+        copy.wait()
 
 
 VMEM_SPEC = pl.BlockSpec(memory_space=pltpu.VMEM)
@@ -1115,8 +1120,9 @@
         (geo, aux, kn, press, ge, mvh, kst, press_t, ra, rb, s, st, near, dt),
         [(3, slots * rows, lanes)],
         [(NKICK,) + two, (3, NKICK) + two, (npart + 1, 2) + tile, (4, 3) + two, (npart, 3) + tile]
-        + [(3,) + sums],
+        + [(3,) + sums, (3, slots * rows, lanes), pltpu.SemaphoreType.DMA((3,))],
         name="kick_rim",
+        far_out=(0,),
     )[0]
     return heated.reshape(temp.shape), moved.reshape(vel.shape)
 

time: 40.2 us -> 40.2 us (level)
  no operation moved by 1% of the time
where the time goes in v6:
time: 40.2 us; the launch traced here: 40 us
  Pallas kernels  26.6 us (66%)
  starting transfers between devices  12.6 us (31%)
  between operations  0.77 us (2%)
    pallas_call x8, Pallas kernels, call(): pl.pallas_call(kernel, in_specs=[VMEM_SPEC] * len(args), out_specs=[HBM_S...  25.1 us
    ppermute x3, starting transfers between devices, paired(): lax.ppermute(sb, axis, [(i, (((i + 1) % n ^ 1) - 1) % n) for i in range(n)])  6.73 us
    ppermute x1, starting transfers between devices, swap(): from_upper = lax.ppermute(to_lower, axis, ring(axis, -1))  2.25 us
    ppermute x1, starting transfers between devices, swap(): from_lower = lax.ppermute(to_upper, axis, ring(axis, 1))  1.63 us
    pallas_call x1, Pallas kernels, body(): pl.pallas_call(prep_kernel, in_specs=[HBM_SPEC] * len(inputs), out_specs=...  1.54 us
  transfers between devices with their start and end apart: 10, of which 0 were waited for; matrix products, arithmetic and copies ran while one was open for 0% of the time, Pallas kernels for 40%

profile of v6, /device:TPU:0, one launch (start us, length us, event | category | flops | bytes accessed | tf_op | source)
XLA Modules:
  0.0 40.0 jit_solution(16319598160135643223)
XLA Ops:
  0.6 1.5 %prep.1 = (f32[3,7,8,16,128]{4,3,2,1,0:T(8,128)S(1)}, f32[6,8,16,128]{3,2,1,0:T(8,128)S(1)}, f32[22,16,128]{2,1,0:T(8,128)S(1)}, f32[22,16,128]{2,1,0:T(8,128)S(1)}, f32[16,128]{1,0:T(8,128)S(1)}) custom-call(s32[8,128]{1,0:T(8,128)} %refs_0_.1, f32[3,128,128]{2,1,0:T(8,128)} %bitcast.9, f32[2,128,128]{2,1,0:T(8,128)} %bitcast.12, f32[128,128]{1,0:T(8,128)} %bitcast.13, ...), custom_call_target="tpu_custom_call" | custom-call | tf_op jit(solution)/shard_map/prep/pallas_call | solution.py:1032
  2.2 0.6 %collective-permute-start = (f32[22,16,128]{2,1,0:T(8,128)S(1)}, f32[22,16,128]{2,1,0:T(8,128)S(1)}, u32[]{:S(2)}, u32[]{:S(2)}) collective-permute-start(f32[22,16,128]{2,1,0:T(8,128)S(1)} %get-tuple-element.54), channel_id=1, source_target_pairs={{0,1},{1,0},{2,3},{3,2},{4,5},{5,4},{6,7},{7,6},{8,9},{9,8},{10,11... | collective-permute-start | bytes 540680 | tf_op jit(solution)/shard_map/ppermute | solution.py:1017
  2.7 3.5 %collective-permute-start.1 = (f32[22,16,128]{2,1,0:T(8,128)S(1)}, f32[22,16,128]{2,1,0:T(8,128)S(1)}, u32[]{:S(2)}, u32[]{:S(2)}) collective-permute-start(f32[22,16,128]{2,1,0:T(8,128)S(1)} %get-tuple-element.55), channel_id=1, source_target_pairs={{0,7},{1,2},{2,1},{3,4},{4,3},{5,6},{6,5},{7,0},{8,15},{9,10},{10,... | collective-permute-start | bytes 540680 | tf_op jit(solution)/shard_map/ppermute | solution.py:1018
  6.3 0.5 %collective-permute-start.2 = (f32[16,128]{1,0:T(8,128)S(1)}, f32[16,128]{1,0:T(8,128)S(1)}, u32[]{:S(2)}, u32[]{:S(2)}) collective-permute-start(f32[16,128]{1,0:T(8,128)S(1)} %get-tuple-element.57.mx), channel_id=1, source_target_pairs={{0,4},{1,5},{2,6},{3,7},{4,0},{5,1},{6,2},{7,3},{8,12},{9,13},{10,... | collective-permute-start | bytes 24584 | tf_op jit(solution)/shard_map/ppermute | solution.py:1052
  6.8 4.5 %near.1 = (f32[11,16,10,8,128]{4,3,2,1,0:T(8,128)S(1)}, f32[11,16,10,8,128]{4,3,2,1,0:T(8,128)S(1)}, f32[10,16,128]{2,1,0:T(8,128)S(1)}) custom-call(f32[3,7,8,16,128]{4,3,2,1,0:T(8,128)S(1)} %get-tuple-element.52.geo, f32[6,8,16,128]{3,2,1,0:T(8,128)S(1)} %get-tuple-element.53.aux), custom_call_target="tpu_custom_call" | custom-call | tf_op jit(solution)/shard_map/near/pallas_call | solution.py:992
  11.3 0.0 collective-permute-done.2.rest_0_
  11.3 0.0 collective-permute-done.ra
  11.3 0.0 collective-permute-done.1.rb
  11.3 0.4 pack.1
  11.7 1.6 %collective-permute-start.3 = (f32[6,16,128]{2,1,0:T(8,128)S(1)}, f32[6,16,128]{2,1,0:T(8,128)S(1)}, u32[]{:S(2)}, u32[]{:S(2)}) collective-permute-start(f32[6,16,128]{2,1,0:T(8,128)S(1)} %get-tuple-element.61), channel_id=1, source_target_pairs={{0,8},{8,16},{16,24},{24,0},{1,9},{9,17},{17,25},{25,1},{2,10},{10... | collective-permute-start | bytes 147464 | tf_op jit(solution)/shard_map/ppermute | solution.py:1010
  13.3 2.2 %collective-permute-start.4 = (f32[6,16,128]{2,1,0:T(8,128)S(1)}, f32[6,16,128]{2,1,0:T(8,128)S(1)}, u32[]{:S(2)}, u32[]{:S(2)}) collective-permute-start(f32[6,16,128]{2,1,0:T(8,128)S(1)} %get-tuple-element.62), channel_id=1, source_target_pairs={{0,24},{8,0},{16,8},{24,16},{1,25},{9,1},{17,9},{25,17},{2,26},{10... | collective-permute-start | bytes 147464 | tf_op jit(solution)/shard_map/ppermute | solution.py:1011
  15.5 0.8 %collective-permute-start.5 = (f32[16,128]{1,0:T(8,128)S(1)}, f32[16,128]{1,0:T(8,128)S(1)}, u32[]{:S(2)}, u32[]{:S(2)}) collective-permute-start(f32[16,128]{1,0:T(8,128)S(1)} %get-tuple-element.70.rest_0_), channel_id=1, source_target_pairs={{0,16},{8,24},{16,0},{24,8},{1,17},{9,25},{17,1},{25,9},{2,18},{10... | collective-permute-start | bytes 24584 | tf_op jit(solution)/shard_map/ppermute | solution.py:1072
  16.3 3.7 %rim.1 = (f32[11,16,10,8,128]{4,3,2,1,0:T(8,128)S(1)}, f32[11,16,10,8,128]{4,3,2,1,0:T(8,128)S(1)}, f32[3,12,16,128]{3,2,1,0:T(8,128)S(1)}, f32[3,12,16,128]{3,2,1,0:T(8,128)S(1)}) custom-call(f32[3,7,6,16,128]{4,3,2,1,0:T(8,128)S(1)} %get-tuple-element.64.ge, ...), custom_call_target="tpu_custom_call", output_to_operand_aliasing={{0}: (1, {}), {1}: (2, {})} | custom-call | tf_op jit(solution)/shard_map/rim/pallas_call | solution.py:992
  20.0 0.0 collective-permute-done.5.rest_1_
  20.1 0.0 collective-permute-done.3.rl
  20.1 0.0 collective-permute-done.4.rr
  20.1 3.8 %first_half.1 = (f32[2,16,10,8,128]{4,3,2,1,0:T(8,128)S(1)}, f32[2,16,10,8,128]{4,3,2,1,0:T(8,128)S(1)}, f32[8,16,128]{2,1,0:T(8,128)S(1)}, f32[2,16,128]{2,1,0:...) custom-call(f32[6,8,16,128]{3,2,1,0:T(8,128)S(1)} %get-tuple-element, ...), custom_call_target="tpu_custom_call" | custom-call | tf_op jit(solution)/shard_map/first_half/pallas_call | solution.py:992
  23.9 0.1 collective-permute-start.6
  24.0 1.3 %collective-permute-start.7 = (f32[5,16,128]{2,1,0:T(8,128)S(1)}, f32[5,16,128]{2,1,0:T(8,128)S(1)}, u32[]{:S(2)}, u32[]{:S(2)}) collective-permute-start(f32[5,16,128]{2,1,0:T(8,128)S(1)} %get-tuple-element.83), channel_id=1, source_target_pairs={{0,7},{1,2},{2,1},{3,4},{4,3},{5,6},{6,5},{7,0},{8,15},{9,10},{10,... | collective-permute-start | bytes 122888 | tf_op jit(solution)/shard_map/ppermute | solution.py:1018
  25.4 3.8 %density.1 = (f32[3,5,8,16,128]{4,3,2,1,0:T(8,128)S(1)}, f32[6,9,16,128]{3,2,1,0:T(8,128)S(1)}, f32[8,16,128]{2,1,0:T(8,128)S(1)}, f32[2,16,128]{2,1,0:T(8,128)S...) custom-call(f32[6,8,16,128]{3,2,1,0:T(8,128)S(1)} %get-tuple-element.53., ...), custom_call_target="tpu_custom_call" | custom-call | tf_op jit(solution)/shard_map/density/pallas_call | solution.py:992
  29.2 0.0 collective-permute-done.6.ra
  29.2 0.0 collective-permute-done.7.rb
  29.2 2.5 %second_half.1 = (f32[128,128]{1,0:T(8,128)S(1)}, f32[3,8,16,128]{3,2,1,0:T(8,128)S(1)}, f32[16,128]{1,0:T(8,128)S(1)}, f32[4,16,128]{2,1,0:T(8,128)S(1)}, f32[4...) custom-call(f32[6,8,16,128]{3,2,1,0:T(8,128)S(1)} %get-tuple-element.53.aux, f32[8,16,128]{2,1,0:T(8,128)S(1)} %get-tuple-element.77.v1, ...), custom_call_target="tpu_custom_call" | custom-call | tf_op jit(solution)/shard_map/second_half/pallas_call | solution.py:992
  31.7 0.1 collective-permute-start.8
  31.8 1.8 %collective-permute-start.9 = (f32[4,16,128]{2,1,0:T(8,128)S(1)}, f32[4,16,128]{2,1,0:T(8,128)S(1)}, u32[]{:S(2)}, u32[]{:S(2)}) collective-permute-start(f32[4,16,128]{2,1,0:T(8,128)S(1)} %get-tuple-element.99), channel_id=1, source_target_pairs={{0,7},{1,2},{2,1},{3,4},{4,3},{5,6},{6,5},{7,0},{8,15},{9,10},{10,... | collective-permute-start | bytes 98312 | tf_op jit(solution)/shard_map/ppermute | solution.py:1018
  33.6 3.9 %kick_near.1 = (f32[3,3,8,16,128]{4,3,2,1,0:T(8,128)S(1)}, f32[128,128]{1,0:T(8,128)}) custom-call(f32[3,7,8,16,128]{4,3,2,1,0:T(8,128)S(1)} %get-tuple-element.52.geo, f32[3,5,8,16,128]{4,3,2,1,0:T(8,128)S(1)} %get-tuple-element.76.kn, f32[3,8,16,128]{3,2,1,0:T(8,128)S(1)} %get-tuple-element.92.press, f32[8,16,10,8,128]{4,3,2,1,0:T(8,128)S(1)} %get-tuple-element.93.qm, ...), custom_call_target="tpu_custom_call" | custom-call | tf_op jit(solution)/shard_map/kick_near/pallas_call | solution.py:992
  37.6 0.0 collective-permute-done.8.ra
  37.6 0.0 collective-permute-done.9.rb
  37.6 2.4 %kick_rim.1 = f32[3,128,128]{2,1,0:T(8,128)} custom-call(f32[3,7,8,16,128]{4,3,2,1,0:T(8,128)S(1)} %get-tuple-element.52.geo, f32[6,8,16,128]{3,2,1,0:T(8,128)S(1)} %get-tuple-element.53.aux, f32[3,5,8,16,128]{4,3,2,1,0:T(8,128)S(1)} %get-tuple-element.76.kn, f32[3,8,16,128]{3,2,1,0:T(8,128)S(1)} %get-tuple-element.92.press, ...), custom_call_target="tpu_custom_call" | custom-call | tf_op jit(solution)/shard_map/kick_rim/pallas_call | solution.py:992
Async XLA Ops:
  2.2 9.1 %collective-permute-start = (f32[22,16,128]{2,1,0:T(8,128)S(1)}, f32[22,16,128]{2,1,0:T(8,128)S(1)}, u32[]{:S(2)}, u32[]{:S(2)}) collective-permute-start(f32[22,16,128]{2,1,0:T(8,128)S(1)} %get-tuple-element.54), channel_id=1, source_target_pairs={{0,1},{1,0},{2,3},{3,2},{4,5},{5,4},{6,7},{7,6},{8,9},{9,8},{10,11... | collective-permute-start | bytes 540680 | tf_op jit(solution)/shard_map/ppermute | solution.py:1017
  2.7 8.5 %collective-permute-start.1 = (f32[22,16,128]{2,1,0:T(8,128)S(1)}, f32[22,16,128]{2,1,0:T(8,128)S(1)}, u32[]{:S(2)}, u32[]{:S(2)}) collective-permute-start(f32[22,16,128]{2,1,0:T(8,128)S(1)} %get-tuple-element.55), channel_id=1, source_target_pairs={{0,7},{1,2},{2,1},{3,4},{4,3},{5,6},{6,5},{7,0},{8,15},{9,10},{10,... | collective-permute-start | bytes 540680 | tf_op jit(solution)/shard_map/ppermute | solution.py:1018
  6.3 5.0 %collective-permute-start.2 = (f32[16,128]{1,0:T(8,128)S(1)}, f32[16,128]{1,0:T(8,128)S(1)}, u32[]{:S(2)}, u32[]{:S(2)}) collective-permute-start(f32[16,128]{1,0:T(8,128)S(1)} %get-tuple-element.57.mx), channel_id=1, source_target_pairs={{0,4},{1,5},{2,6},{3,7},{4,0},{5,1},{6,2},{7,3},{8,12},{9,13},{10,... | collective-permute-start | bytes 24584 | tf_op jit(solution)/shard_map/ppermute | solution.py:1052
  11.7 8.4 %collective-permute-start.3 = (f32[6,16,128]{2,1,0:T(8,128)S(1)}, f32[6,16,128]{2,1,0:T(8,128)S(1)}, u32[]{:S(2)}, u32[]{:S(2)}) collective-permute-start(f32[6,16,128]{2,1,0:T(8,128)S(1)} %get-tuple-element.61), channel_id=1, source_target_pairs={{0,8},{8,16},{16,24},{24,0},{1,9},{9,17},{17,25},{25,1},{2,10},{10... | collective-permute-start | bytes 147464 | tf_op jit(solution)/shard_map/ppermute | solution.py:1010
  13.3 6.8 %collective-permute-start.4 = (f32[6,16,128]{2,1,0:T(8,128)S(1)}, f32[6,16,128]{2,1,0:T(8,128)S(1)}, u32[]{:S(2)}, u32[]{:S(2)}) collective-permute-start(f32[6,16,128]{2,1,0:T(8,128)S(1)} %get-tuple-element.62), channel_id=1, source_target_pairs={{0,24},{8,0},{16,8},{24,16},{1,25},{9,1},{17,9},{25,17},{2,26},{10... | collective-permute-start | bytes 147464 | tf_op jit(solution)/shard_map/ppermute | solution.py:1011
  15.5 4.5 %collective-permute-start.5 = (f32[16,128]{1,0:T(8,128)S(1)}, f32[16,128]{1,0:T(8,128)S(1)}, u32[]{:S(2)}, u32[]{:S(2)}) collective-permute-start(f32[16,128]{1,0:T(8,128)S(1)} %get-tuple-element.70.rest_0_), channel_id=1, source_target_pairs={{0,16},{8,24},{16,0},{24,8},{1,17},{9,25},{17,1},{25,9},{2,18},{10... | collective-permute-start | bytes 24584 | tf_op jit(solution)/shard_map/ppermute | solution.py:1072
  23.9 5.2 %collective-permute-start.6 = (f32[5,16,128]{2,1,0:T(8,128)S(1)}, f32[5,16,128]{2,1,0:T(8,128)S(1)}, u32[]{:S(2)}, u32[]{:S(2)}) collective-permute-start(f32[5,16,128]{2,1,0:T(8,128)S(1)} %get-tuple-element.82), channel_id=1, source_target_pairs={{0,1},{1,0},{2,3},{3,2},{4,5},{5,4},{6,7},{7,6},{8,9},{9,8},{10,11... | collective-permute-start | bytes 122888 | tf_op jit(solution)/shard_map/ppermute | solution.py:1017
  24.0 5.2 %collective-permute-start.7 = (f32[5,16,128]{2,1,0:T(8,128)S(1)}, f32[5,16,128]{2,1,0:T(8,128)S(1)}, u32[]{:S(2)}, u32[]{:S(2)}) collective-permute-start(f32[5,16,128]{2,1,0:T(8,128)S(1)} %get-tuple-element.83), channel_id=1, source_target_pairs={{0,7},{1,2},{2,1},{3,4},{4,3},{5,6},{6,5},{7,0},{8,15},{9,10},{10,... | collective-permute-start | bytes 122888 | tf_op jit(solution)/shard_map/ppermute | solution.py:1018
  31.7 5.9 %collective-permute-start.8 = (f32[4,16,128]{2,1,0:T(8,128)S(1)}, f32[4,16,128]{2,1,0:T(8,128)S(1)}, u32[]{:S(2)}, u32[]{:S(2)}) collective-permute-start(f32[4,16,128]{2,1,0:T(8,128)S(1)} %get-tuple-element.98), channel_id=1, source_target_pairs={{0,1},{1,0},{2,3},{3,2},{4,5},{5,4},{6,7},{7,6},{8,9},{9,8},{10,11... | collective-permute-start | bytes 98312 | tf_op jit(solution)/shard_map/ppermute | solution.py:1017
  31.8 5.8 %collective-permute-start.9 = (f32[4,16,128]{2,1,0:T(8,128)S(1)}, f32[4,16,128]{2,1,0:T(8,128)S(1)}, u32[]{:S(2)}, u32[]{:S(2)}) collective-permute-start(f32[4,16,128]{2,1,0:T(8,128)S(1)} %get-tuple-element.99), channel_id=1, source_target_pairs={{0,7},{1,2},{2,1},{3,4},{4,3},{5,6},{6,5},{7,0},{8,15},{9,10},{10,... | collective-permute-start | bytes 98312 | tf_op jit(solution)/shard_map/ppermute | solution.py:1018
